TPU v7x, 32 devices: a whole 2x2x4 slice. The times are simulated.
32 devices in a mesh: group: 2 (over x), ep: 4 (over y, core), kv: 4 (over z).
Axes of the slice: x: 2, y: 2, z: 4, core: 2. Of those that a mesh axis runs over, the one named last changes fastest.
Arguments:
- queries: bfloat16 [1024, 4096], P(('group', 'ep', 'kv')), parts along dimension 0, may hold values from -8 to 8
- new_keys: bfloat16 [1024, 512], P(('group', 'ep', 'kv')), parts along dimension 0, may hold values from -6 to 6
- new_values: bfloat16 [1024, 512], P(('group', 'ep', 'kv')), parts along dimension 0, may hold values from -6 to 6
- key_cache: bfloat16 [8, 16384, 512], P(('group', 'ep'), 'kv'), parts along dimension 0, may hold values from -8 to 8
- value_cache: bfloat16 [8, 16384, 512], P(('group', 'ep'), 'kv'), parts along dimension 0, may hold values from -6 to 6
- lengths: int32 [8], P(('group', 'ep')), parts along dimension 0, may hold values from 2 to 16384, as said below
- residual_in: bfloat16 [1024, 2048], P(('group', 'ep', 'kv')), parts along dimension 0, may hold values from -20 to 20
- out_weight: bfloat16 [4096, 2048], P('kv'), may hold values from -0.25 to 0.25
- norm_gain: float32 [2048], replicated, may hold values from 0.5 to 1.5
- gate_up_weight: bfloat16 [16, 2048, 1536], P(('ep', 'kv')), may hold values from -0.125 to 0.125
- down_weight: bfloat16 [16, 768, 2048], P(('ep', 'kv')), may hold values from -0.21875 to 0.21875
- expert_ids: int32 [1024, 8], P(('group', 'ep', 'kv')), parts along dimension 0, may hold values from 0 to 15, all different within a row; in each aligned block of 32 rows (0 to 31, 32 to 63, ...) at most 32 rows name the same one
- route_weights: float32 [1024, 8], P(('group', 'ep', 'kv')), parts along dimension 0, may hold values from 0.05 to 1
Outputs:
- layer_out: bfloat16 [1024, 2048], P(('group', 'ep', 'kv')), parts along dimension 0
There are 2 independent parts, one for each index of `group`. A program takes and returns all parts, laid end to end along the dimension named above; an argument that names none is the same for every part. Nothing has to cross between parts.
Inputs may be any that keep to these rules, and one draw needn't show every extreme that they name: `lengths`: some request of each group has all 16384 positions filled. `expert_ids`: each row names 8 different experts; within the rows of one device (aligned blocks of 32 rows) no expert is named more than 32 times, a bound that some block reaches.
All inputs are finite; a program needn't handle non-finite values.
Results may differ from a plain program's by a relative error of at most 0.019.
Values may be sent and summed in bfloat16 or wider, within the bound.
No kernel may reach another device: no remote copies, remote signals or barrier semaphores. Data moves between devices by JAX's collectives and lax.ppermute only.
A program may use at most 192 MiB of HBM per device.

v0:
```python
import functools
import math

import jax
import jax.numpy as jnp
from jax import lax
from jax.experimental import pallas as pl
from jax.experimental.pallas import tpu as pltpu
from jax.sharding import PartitionSpec as P

D = 2048
QH = 32
KVH = 4
HD = 128
FF = 768
TOPK = 8
BLOCK = 128

absent = -1e30
masked_score = -3e38
norm_epsilon = 1e-06
score_scale = math.log2(math.e) * HD**-0.5
key_step = 512
row_step = 256
f32 = jnp.float32
bf16 = jnp.bfloat16

HBM = pl.BlockSpec(memory_space=pltpu.HBM)
VM = pl.BlockSpec(memory_space=pltpu.VMEM)
SM = pl.BlockSpec(memory_space=pltpu.SMEM)


def in_hbm(array):
    return pltpu.with_memory_space_constraint(array, pltpu.HBM)


def shifted(array, axis, by):
    size = lax.axis_size(axis)
    if by % size == 0:
        return array
    return lax.ppermute(array, axis, [(i, (i + by) % size) for i in range(size)])


def swapped(array, axis, bit):
    return lax.ppermute(array, axis, [(i, i ^ bit) for i in range(lax.axis_size(axis))])


def scored(left, right):
    return lax.dot_general(left, right, (((1,), (1,)), ((), ())), preferred_element_type=f32)


def three_parts(value):
    first = value.astype(bf16).astype(f32)
    rest = value - first
    second = rest.astype(bf16).astype(f32)
    return first, second, rest - second


def attend(bounds, blocks, places, query_chunks, keys, values, fresh_keys, fresh_values, heads, own_first):
    count = len(query_chunks)
    rows = query_chunks[0].shape[0]
    block_count = QH // heads
    per_key_head = QH // KVH // heads
    cached = keys.shape[0]
    fresh = fresh_keys.shape[0]
    padded = cached + 128
    width = heads * HD
    size = count * heads * rows

    def body(*refs):
        bounds_ref, blocks_ref, places_ref = refs[:3]
        query_refs = refs[3 : 3 + count]
        key_hbm, value_hbm, fresh_key_ref, fresh_value_ref = refs[3 + count : 7 + count]
        outs = refs[7 + count : 7 + count + block_count]
        keys_in, values_in, ones, even, odd, largest, result, fresh_in, own_in, sems, fresh_sems = refs[7 + count + block_count :]
        if own_first:
            own_copy = pltpu.make_async_copy(query_refs[0], own_in, fresh_sems.at[2])
            own_copy.start()
            query_refs = (own_in, *query_refs[1:])
        fresh_copies = [
            pltpu.make_async_copy(ref, fresh_in.at[n], fresh_sems.at[n])
            for n, ref in enumerate((fresh_key_ref, fresh_value_ref))
        ]
        for copy in fresh_copies:
            copy.start()
        score_refs = (even, odd)
        filled = bounds_ref[0]
        fresh_start = bounds_ref[1]

        def lane_of(i):
            return pl.multiple_of((blocks_ref[i] // per_key_head) * HD, HD)

        def key_copy(i):
            return pltpu.make_async_copy(
                key_hbm.at[:, pl.ds(lane_of(i), HD)], keys_in.at[i, pl.ds(0, cached)], sems.at[0, i]
            )

        def value_copy(i):
            return pltpu.make_async_copy(
                value_hbm.at[:, pl.ds(lane_of(i), HD)], values_in.at[i, pl.ds(0, cached)], sems.at[1, i]
            )

        key_copy(0).start()
        place = lax.broadcasted_iota(jnp.int32, (padded, HD), 0)
        counted = (place < filled) | ((place >= cached) & (place < cached + fresh))
        ones[...] = jnp.where(counted, 1.0, 0.0).astype(bf16)
        blank = jnp.zeros((128 - fresh, HD), bf16)
        for copy in fresh_copies:
            copy.wait()
        for i in range(block_count):
            lanes = pl.ds(lane_of(i), HD)
            keys_in[i, cached : cached + fresh] = fresh_in[0, :, lanes]
            keys_in[i, cached + fresh :] = blank
            values_in[i, cached : cached + fresh] = fresh_in[1, :, lanes]
            values_in[i, cached + fresh :] = blank
        if own_first:
            own_copy.wait()

        def replace_unfilled(ref, i, filler):
            @pl.when(filled < cached)
            def _():
                def one(block, carry):
                    at = pl.ds(pl.multiple_of(block * row_step, row_step), row_step)
                    inside = lax.broadcasted_iota(jnp.int32, (row_step, HD), 0) + block * row_step < filled
                    ref[i, at] = jnp.where(inside, ref[i, at], filler)
                    return carry

                lax.fori_loop(filled // row_step, cached // row_step, one, 0)

        def arrive_keys(i):
            key_copy(i).wait()
            replace_unfilled(keys_in, i, jnp.broadcast_to(keys_in[i, :1], (row_step, HD)))

        def arrive_values(i):
            value_copy(i).wait()
            replace_unfilled(values_in, i, jnp.zeros((row_step, HD), bf16))

        def fill_scores(i, slot):
            out = score_refs[slot]
            lanes = pl.ds(pl.multiple_of(blocks_ref[i] * width, HD), width)
            chunks = [ref[:, lanes].astype(f32) * score_scale for ref in query_refs]
            stacked = jnp.concatenate([c[:, h * HD : (h + 1) * HD] for c in chunks for h in range(heads)], 0)
            high = stacked.astype(bf16)
            both = jnp.concatenate([high, (stacked - high.astype(f32)).astype(bf16)], 1)
            running = None
            for start in range(0, cached, key_step):
                part = keys_in[i, start : start + key_step]
                scores = scored(both, jnp.concatenate([part, part], 1))
                out[:, start : start + key_step] = scores
                for at in range(0, key_step, HD):
                    piece = scores[:, at : at + HD]
                    running = piece if running is None else jnp.maximum(running, piece)
            part = keys_in[i, cached:]
            scores = scored(both, jnp.concatenate([part, part], 1))
            row = lax.broadcasted_iota(jnp.int32, (rows, HD), 0)
            column = lax.broadcasted_iota(jnp.int32, (rows, HD), 1)
            masked = []
            for c in range(count):
                seen = (column < fresh) & (column + fresh_start <= row + places_ref[c] * rows)
                own = scores[c * heads * rows : (c + 1) * heads * rows]
                masked.append(jnp.where(jnp.tile(seen, (heads, 1)), own, masked_score))
            scores = jnp.concatenate(masked, 0)
            out[:, cached:] = scores
            running = jnp.maximum(running, scores)
            top = jnp.maximum(jnp.max(running, 1, keepdims=True), absent)
            largest[slot] = jnp.broadcast_to(top, (size, HD))

        def weigh(i, slot):
            top = largest[slot]
            probs = jnp.exp2(score_refs[slot][...] - top[:, :1]).astype(bf16)
            both = jnp.concatenate([values_in[i], ones[...]], 1)
            total = jnp.dot(probs, both, preferred_element_type=f32)
            lane = lax.broadcasted_iota(jnp.int32, (rows, HD), 1)
            for c in range(count):
                stats = jnp.zeros((rows, HD), f32)
                for h in range(heads):
                    at = (c * heads + h) * rows
                    piece = total[at : at + rows]
                    norm = piece[:, HD:]
                    some = norm > 0
                    safe = jnp.where(some, norm, 1.0)
                    result[c, :, h * HD : (h + 1) * HD] = (piece[:, :HD] / safe).astype(bf16)
                    level = jnp.where(some, top[at : at + rows] + jnp.log2(safe), absent)
                    for k, part in enumerate(three_parts(level)):
                        stats = jnp.where(lane == h + k * heads, part, stats)
                result[c, :, width:] = stats.astype(bf16)
            for n in range(slot, block_count, 2):

                @pl.when(i == n)
                def _():
                    outs[n][...] = result[...]

        arrive_keys(0)
        for i in range(1, block_count):
            key_copy(i).start()
            value_copy(i - 1).start()
        value_copy(block_count - 1).start()
        fill_scores(0, 0)

        def pair(t, carry):
            arrive_keys(2 * t + 1)
            arrive_values(2 * t)
            fill_scores(2 * t + 1, 1)
            weigh(2 * t, 0)

            @pl.when(t < block_count // 2 - 1)
            def _():
                arrive_keys(2 * t + 2)
                arrive_values(2 * t + 1)
                fill_scores(2 * t + 2, 0)
                weigh(2 * t + 1, 1)

            return carry

        lax.fori_loop(0, block_count // 2, pair, 0)
        arrive_values(block_count - 1)
        weigh(block_count - 1, 1)

    return pl.pallas_call(
        body,
        in_specs=[SM] * 3 + [HBM if own_first and n == 0 else VM for n in range(count)] + [HBM] * 4,
        out_specs=[VM] * block_count,
        out_shape=[jax.ShapeDtypeStruct((count, rows, width + HD), bf16)] * block_count,
        scratch_shapes=[
            pltpu.VMEM((block_count, padded, HD), bf16),
            pltpu.VMEM((block_count, padded, HD), bf16),
            pltpu.VMEM((padded, HD), bf16),
            pltpu.VMEM((size, padded), f32),
            pltpu.VMEM((size, padded), f32),
            pltpu.VMEM((2, size, HD), f32),
            pltpu.VMEM((count, rows, width + HD), bf16),
            pltpu.VMEM((2, fresh, KVH * HD), bf16),
            pltpu.VMEM((rows, QH * HD), bf16),
            pltpu.SemaphoreType.DMA((2, block_count)),
            pltpu.SemaphoreType.DMA((3,)),
        ],
        compiler_params=pltpu.CompilerParams(vmem_limit_bytes=12 * size * padded + (16 << 20)),
        cost_estimate=pl.CostEstimate(
            flops=block_count * size * padded * HD * 2 * 16,
            transcendentals=block_count * size * padded,
            bytes_accessed=4 * cached * KVH * HD,
        ),
    )(
        bounds,
        blocks,
        places,
        *[in_hbm(c) if own_first and n == 0 else c for n, c in enumerate(query_chunks)],
        *[in_hbm(a) for a in (keys, values, fresh_keys, fresh_values)],
    )


def project(pieces, weight, heads):
    arrays = []
    where = []
    for chunk in pieces:
        for array, index in chunk:
            found = [n for n, a in enumerate(arrays) if a is array]
            if not found:
                arrays.append(array)
                found = [len(arrays) - 1]
            where.append((found[0], index))
    chunks = len(pieces)
    sources = len(pieces[0])
    rows = arrays[0].shape[1]
    width = heads * HD
    step = 512

    def body(*refs):
        held = refs[: len(arrays)]
        weight_ref = refs[len(arrays)]
        outs = refs[len(arrays) + 1 : len(arrays) + 1 + chunks]
        attention = refs[-1]

        @pl.when(pl.program_id(0) == 0)
        def _():
            for t in range(chunks):
                spots = where[t * sources : (t + 1) * sources]
                stats = [held[a][c, :, width:].astype(f32) for a, c in spots]
                for h in range(heads):
                    levels = [
                        s[:, h : h + 1] + s[:, h + heads : h + heads + 1] + s[:, h + 2 * heads : h + 2 * heads + 1]
                        for s in stats
                    ]
                    top = functools.reduce(jnp.maximum, levels)
                    shares = [jnp.exp2(level - top) for level in levels]
                    total = functools.reduce(jnp.add, shares)
                    mixed = None
                    for (a, c), share in zip(spots, shares):
                        term = held[a][c, :, h * HD : (h + 1) * HD].astype(f32) * share
                        mixed = term if mixed is None else mixed + term
                    attention[t * rows : (t + 1) * rows, h * HD : (h + 1) * HD] = (mixed / total).astype(bf16)

        result = jnp.dot(attention[...], weight_ref[...], preferred_element_type=f32).astype(bf16)
        for t in range(chunks):
            outs[t][...] = result[t * rows : (t + 1) * rows]

    return pl.pallas_call(
        body,
        grid=(D // step,),
        in_specs=[VM] * len(arrays) + [pl.BlockSpec((width, step), lambda n: (0, n))],
        out_specs=[pl.BlockSpec((rows, step), lambda n: (0, n))] * chunks,
        out_shape=[jax.ShapeDtypeStruct((rows, D), bf16)] * chunks,
        scratch_shapes=[pltpu.VMEM((chunks * rows, width), bf16)],
        name="project",
    )(*arrays, in_hbm(weight))


def normalize(residual, shares, gain, gates, experts):
    rows = residual.shape[0]

    def body(residual_ref, *refs):
        share_refs = refs[: len(shares)]
        gain_ref, gates_ref, hidden_ref, message_ref = refs[len(shares) :]
        hidden = share_refs[0][...].astype(f32)
        for ref in share_refs[1:]:
            hidden = hidden + ref[...].astype(f32)
        hidden = residual_ref[...].astype(f32) + hidden
        hidden_ref[...] = hidden
        power = jnp.mean(hidden * hidden, axis=-1, keepdims=True)
        message_ref[:, :D] = (hidden * lax.rsqrt(power + norm_epsilon) * gain_ref[...]).astype(bf16)
        if experts:
            first, second, third = three_parts(gates_ref[...])
            lane = lax.broadcasted_iota(jnp.int32, first.shape, 1)
            parts = jnp.where(lane < experts, first, jnp.where(lane < 2 * experts, second, third))
            message_ref[:, D:] = parts.astype(bf16)

    return pl.pallas_call(
        body,
        in_specs=[VM] * (len(shares) + 3),
        out_specs=[VM] * 2,
        out_shape=[
            jax.ShapeDtypeStruct((rows, D), f32),
            jax.ShapeDtypeStruct((rows, D + (HD if experts else 0)), bf16),
        ],
        name="normalize",
    )(residual, *shares, gain, gates)


def run_expert(expert, messages, gate_up, down, experts):
    rows = messages[0].shape[0]
    count = len(messages)
    half = count // 2 * rows
    step = 256
    steps = FF // step

    def body(expert_ref, *refs):
        message_refs = refs[:count]
        gate_ref, up_ref, down_ref, kept_ref, sent_ref, features, total = refs[count:]
        stage = pl.program_id(0)

        @pl.when(stage == 0)
        def _():
            for c in range(count):
                features[c * rows : (c + 1) * rows] = message_refs[c][:, :D]

        gate = jnp.dot(features[...], gate_ref[...], preferred_element_type=f32)
        up = jnp.dot(features[...], up_ref[...], preferred_element_type=f32)
        inner = (gate / (1.0 + jnp.exp(-gate)) * up).astype(bf16)

        part = jnp.dot(inner, down_ref[...], preferred_element_type=f32)

        @pl.when(stage == 0)
        def _():
            total[...] = part

        @pl.when(stage > 0)
        def _():
            total[...] += part

        @pl.when(stage == steps - 1)
        def _():
            mine = expert_ref[0]
            lane = lax.broadcasted_iota(jnp.int32, (rows, HD), 1)
            chosen = (lane == mine) | (lane == mine + experts) | (lane == mine + 2 * experts)
            for c in range(count):
                parts = message_refs[c][:, D:].astype(f32)
                weight = jnp.sum(jnp.where(chosen, parts, 0.0), 1, keepdims=True)
                out = total[c * rows : (c + 1) * rows].astype(bf16).astype(f32) * weight
                if c < count // 2:
                    kept_ref[c * rows : (c + 1) * rows] = out
                else:
                    at = c * rows - half
                    sent_ref[at : at + rows] = out.astype(bf16)

    return pl.pallas_call(
        body,
        grid=(steps,),
        in_specs=[SM]
        + [VM] * count
        + [
            pl.BlockSpec((D, step), lambda n: (0, n)),
            pl.BlockSpec((D, step), lambda n: (0, n + steps)),
            pl.BlockSpec((step, D), lambda n: (n, 0)),
        ],
        out_specs=[VM] * 2,
        out_shape=[jax.ShapeDtypeStruct((half, D), f32), jax.ShapeDtypeStruct((half, D), bf16)],
        scratch_shapes=[pltpu.VMEM((count * rows, D), bf16), pltpu.VMEM((count * rows, D), f32)],
        compiler_params=pltpu.CompilerParams(vmem_limit_bytes=36 << 20),
        name="run_expert",
    )(expert, *messages, in_hbm(gate_up), in_hbm(gate_up), in_hbm(down))


def mix_all_rows(message, gate_up, down, experts):
    kv_count = lax.axis_size("kv")
    rows = message.shape[0]
    mine = (lax.axis_index("ep") * kv_count + lax.axis_index("kv")).reshape(1).astype(jnp.int32)
    order = sorted(range(kv_count), key=lambda c: -min(c, kv_count - c))
    here = {k: shifted(message, "kv", k) for k in order}
    across = {k: swapped(here[k], "ep", 2) for k in reversed(order)}
    own = [here[k] for k in order] + [across[k] for k in order]
    paired = {m: swapped(own[m], "ep", 1) for m in reversed(range(len(own)))}
    kept, sent = run_expert(mine, own + [paired[m] for m in range(len(own))], gate_up, down, experts)
    pair = kept + swapped(sent, "ep", 1).astype(f32)
    total = None
    for n, k in enumerate(order):
        at = n * rows
        far = at + kv_count * rows
        part = pair[at : at + rows] + swapped(pair[far : far + rows].astype(bf16), "ep", 2).astype(f32)
        if k:
            part = shifted(part.astype(bf16), "kv", -k).astype(f32)
        total = part if total is None else total + part
    return total


def mix_sent_rows(normed, gate_up, down, expert_ids, route_weights, capacity, experts):
    rows = normed.shape[0]
    pair_expert = expert_ids.reshape(-1)
    one_hot = (pair_expert[:, None] == jnp.arange(experts, dtype=jnp.int32)[None, :]).astype(jnp.int32)
    slot_index = jnp.sum((jnp.cumsum(one_hot, axis=0) - 1) * one_hot, axis=1)
    outbound = (
        jnp.zeros((experts, capacity, D), bf16).at[pair_expert, slot_index].set(jnp.repeat(normed, TOPK, axis=0))
    )
    received = lax.all_to_all(outbound, ("ep", "kv"), split_axis=0, concat_axis=0, tiled=True)
    sources, slots, width = received.shape
    mixed = jnp.dot(received.reshape(sources * slots, width), gate_up, preferred_element_type=f32)
    inner = (jax.nn.silu(mixed[:, :FF]) * mixed[:, FF:]).astype(bf16)
    outputs = jnp.dot(inner, down, preferred_element_type=f32).astype(bf16)
    returned = lax.all_to_all(
        outputs.reshape(sources, slots, width), ("ep", "kv"), split_axis=0, concat_axis=0, tiled=True
    )
    picked = returned[pair_expert, slot_index].reshape(rows, TOPK, D)
    return jnp.einsum("rk,rkd->rd", route_weights, picked.astype(f32))


def shards(
    queries,
    new_keys,
    new_values,
    key_cache,
    value_cache,
    lengths,
    residual_in,
    out_weight,
    norm_gain,
    gate_up_weight,
    down_weight,
    expert_ids,
    route_weights,
):
    kv_count = lax.axis_size("kv")
    kv_place = lax.axis_index("kv")
    ep_count = lax.axis_size("ep")
    experts = ep_count * kv_count
    rows = queries.shape[0]
    cached = key_cache.shape[1]
    heads = QH // kv_count
    assert key_cache.shape[0] == 1 and rows * kv_count == BLOCK

    near_first = sorted(range(kv_count), key=lambda c: min(c, kv_count - c))
    chunks = {c: shifted(queries, "kv", c) for c in near_first}
    bounds = jnp.stack([jnp.clip(lengths[0] - kv_place * cached, 0, cached), kv_place * rows]).astype(jnp.int32)
    blocks = (kv_place + 1 + jnp.arange(kv_count, dtype=jnp.int32)) % kv_count
    if kv_count == 4:
        calls = GROUPS
    else:
        calls = [near_first[at : at + 2] for at in range(0, kv_count, 2)]
    shares = {}

    def send(k, outs, call):
        landed = shifted(outs[k - 1], "kv", k)
        for index, c in enumerate(call):
            shares[k, c] = (landed, index)

    outs = None
    for call in calls:
        places = jnp.stack([(kv_place - c) % kv_count for c in call]).astype(jnp.int32)
        if outs is not None:
            places, *outs = lax.optimization_barrier((places, *outs))
            for k in range(kv_count):
                send(k, outs, before)
        outs = attend(
            bounds,
            blocks,
            places,
            [chunks[c] for c in call],
            key_cache[0],
            value_cache[0],
            new_keys,
            new_values,
            heads,
            0 in call,
        )
        before = call
    for k in range(kv_count):
        send(k, outs, before)
    pieces = [[shares[k, (t - k) % kv_count] for k in range(kv_count)] for t in range(kv_count)]
    projected = project(pieces, out_weight, heads)
    landed = [shifted(projected[t], "kv", -t) for t in range(kv_count)]

    capacity = min(rows, max(2, 2 * rows * TOPK // experts))
    everywhere = capacity == rows and ep_count == 4 and kv_count == 4 and 3 * experts <= HD
    named = expert_ids[:, :, None] == jnp.arange(experts, dtype=jnp.int32)[None, None, :]
    gates = jnp.sum(jnp.where(named, route_weights[:, :, None], 0.0), axis=1)
    if everywhere:
        gates = jnp.pad(jnp.tile(gates, (1, 3)), ((0, 0), (0, HD - 3 * experts)))
    hidden_state, message = normalize(
        residual_in, landed, norm_gain[None], gates, experts if everywhere else 0
    )
    if everywhere:
        mixture = mix_all_rows(message, gate_up_weight[0], down_weight[0], experts)
    else:
        mixture = mix_sent_rows(
            message, gate_up_weight[0], down_weight[0], expert_ids, route_weights, capacity, experts
        )
    return (hidden_state + mixture).astype(bf16)


GROUPS = [[0], [1, 3], [2]]


def solution(mesh):
    placed = (
        P(("group", "ep", "kv"), None),
        P(("group", "ep", "kv"), None),
        P(("group", "ep", "kv"), None),
        P(("group", "ep"), "kv", None),
        P(("group", "ep"), "kv", None),
        P(("group", "ep")),
        P(("group", "ep", "kv"), None),
        P("kv", None),
        P(),
        P(("ep", "kv"), None, None),
        P(("ep", "kv"), None, None),
        P(("group", "ep", "kv"), None),
        P(("group", "ep", "kv"), None),
    )
    return jax.shard_map(
        shards,
        mesh=mesh,
        in_specs=placed,
        out_specs=P(("group", "ep", "kv"), None),
        check_vma=False,
    )
```

profile of v0, /device:TPU:0, one launch (start us, length us, event | category | flops | bytes accessed | tf_op | source)
XLA Modules:
  0.0 161.1 jit_solution(8784757809846686559)
XLA Ops:
  0.0 3.0 %collective-permute-start = (bf16[32,4096]{1,0:T(8,128)(2,1)}, bf16[32,4096]{1,0:T(8,128)(2,1)S(1)}, u32[]{:S(2)}, u32[]{:S(2)}) collective-permute-start(bf16[32,4096]{1,0:T(8,128)(2,1)} %refs_3_.1), channel_id=1, source_target_pairs={{0,1},{1,2},{2,3},{3,0},{4,5},{5,6},{6,7},{7,4},{8,9},{9,10},{10,1... | collective-permute-start | bytes 786440 | tf_op jit(solution)/shard_map/ppermute | solution.py:41
  3.0 2.6 %collective-permute-start.3 = (bf16[32,4096]{1,0:T(8,128)(2,1)}, bf16[32,4096]{1,0:T(8,128)(2,1)S(1)}, u32[]{:S(2)}, u32[]{:S(2)}) collective-permute-start(bf16[32,4096]{1,0:T(8,128)(2,1)} %refs_3_.1), channel_id=1, source_target_pairs={{0,2},{1,3},{2,0},{3,1},{4,6},{5,7},{6,4},{7,5},{8,10},{9,11},{10,... | collective-permute-start | bytes 786440 | tf_op jit(solution)/shard_map/ppermute | solution.py:41
  5.6 1.3 collective-permute-start.1
  7.7 8.8 %shard_map.127 = (bf16[1,32,1152]{2,1,0:T(8,128)(2,1)S(1)}, bf16[1,32,1152]{2,1,0:T(8,128)(2,1)S(1)}, bf16[1,32,1152]{2,1,0:T(8,128)(2,1)S(1)}, bf16[1,32,1152]{2,1,0:T(8,128)(2,1)S(1)}) custom-call(s32[2]{0:T(128)S(1)} %pad_add_fusion.1.refs_0_, s32[4]{0:T(128)S(1)} %and_select_fusion.refs_1_, s32[1]{0:T(128)} %bitcast.5.refs_2_, bf16[32,4096]{1,0:T(8,128)(2,1)} %refs_3_.1, ...), custom_call_target="tpu_custom_call" | custom-call | flops 17716740096 | bytes 8388608 | tf_op jit(solution)/shard_map/pallas_call | solution.py:219
  16.5 0.6 copy-done.2
  17.2 0.7 collective-permute-start.6
  18.2 2.8 %collective-permute-start.11 = (bf16[1,32,1152]{2,1,0:T(8,128)(2,1)S(1)}, bf16[1,32,1152]{2,1,0:T(8,128)(2,1)S(1)}, u32[]{:S(2)}, u32[]{:S(2)}) collective-permute-start(bf16[1,32,1152]{2,1,0:T(8,128)(2,1)S(1)} %get-tuple-element.56), channel_id=1, source_target_pairs={{0,3},{1,0},{2,1},{3,2},{4,7},{5,4},{6,5},{7,6},{8,11},{9,8},{10,9... | collective-permute-start | bytes 221192 | tf_op jit(solution)/shard_map/ppermute | solution.py:41
  21.3 12.9 %shard_map.128 = (bf16[2,32,1152]{2,1,0:T(8,128)(2,1)S(1)}, bf16[2,32,1152]{2,1,0:T(8,128)(2,1)S(1)}, bf16[2,32,1152]{2,1,0:T(8,128)(2,1)S(1)}, bf16[2,32,1152]{2,1,0:T(8,128)(2,1)S(1)}) custom-call(s32[2]{0:T(128)S(1)} %pad_add_fusion.1.refs_0_, s32[4]{0:T(128)S(1)} %and_select_fusion.refs_1_, s32[2]{0:T(128)S(1)} %pad_add_fusion.refs_2_, ...), custom_call_target="tpu_custom_call" | custom-call | flops 35433480192 | bytes 8388608 | tf_op jit(solution)/shard_map/pallas_call | solution.py:219
  34.2 8.7 %shard_map.129 = (bf16[1,32,1152]{2,1,0:T(8,128)(2,1)S(1)}, bf16[1,32,1152]{2,1,0:T(8,128)(2,1)S(1)}, bf16[1,32,1152]{2,1,0:T(8,128)(2,1)S(1)}, bf16[1,32,1152]{2,1,0:T(8,128)(2,1)S(1)}) custom-call(s32[2]{0:T(128)S(1)} %pad_add_fusion.1.refs_0_, s32[4]{0:T(128)S(1)} %and_select_fusion.refs_1_, s32[1]{0:T(128)} %bitcast.8.refs_2_, ...), custom_call_target="tpu_custom_call" | custom-call | flops 17716740096 | bytes 8388608 | tf_op jit(solution)/shard_map/pallas_call | solution.py:219
  42.9 0.6 copy-done.3
  43.5 10.1 %collective-permute-start.4 = (bf16[1,32,1152]{2,1,0:T(8,128)(2,1)S(1)}, bf16[1,32,1152]{2,1,0:T(8,128)(2,1)S(1)}, u32[]{:S(2)}, u32[]{:S(2)}) collective-permute-start(bf16[1,32,1152]{2,1,0:T(8,128)(2,1)S(1)} %get-tuple-element.47), channel_id=1, source_target_pairs={{0,2},{1,3},{2,0},{3,1},{4,6},{5,7},{6,4},{7,5},{8,10},{9,11},{10,... | collective-permute-start | bytes 221192 | tf_op jit(solution)/shard_map/ppermute | solution.py:41
  53.6 0.9 collective-permute-start.2
  54.6 2.9 %collective-permute-start.5 = (bf16[2,32,1152]{2,1,0:T(8,128)(2,1)S(1)}, bf16[2,32,1152]{2,1,0:T(8,128)(2,1)S(1)}, u32[]{:S(2)}, u32[]{:S(2)}) collective-permute-start(bf16[2,32,1152]{2,1,0:T(8,128)(2,1)S(1)} %get-tuple-element.48), channel_id=1, source_target_pairs={{0,3},{1,0},{2,1},{3,2},{4,7},{5,4},{6,5},{7,6},{8,11},{9,8},{10,9... | collective-permute-start | bytes 442376 | tf_op jit(solution)/shard_map/ppermute | solution.py:41
  57.6 1.4 collective-permute-start.8
  59.0 1.4 collective-permute-start.10
  60.4 5.8 %collective-permute-done.8.refs_7_ = bf16[1,32,1152]{2,1,0:T(8,128)(2,1)S(1)} collective-permute-done((bf16[1,32,1152]{2,1,0:T(8,128)(2,1)S(1)}, bf16[1,32,1152]{2,1,0:T(8,128)(2,1)S(1)}, u32[]{:S(2)}, u32[]{:S(2)}) %collective-permute-start.8) | collective-permute-done | bytes 73760 | tf_op jit(solution)/shard_map/ppermute | solution.py:41
  66.2 3.7 %collective-permute-done.10.refs_10_ = bf16[1,32,1152]{2,1,0:T(8,128)(2,1)S(1)} collective-permute-done((bf16[1,32,1152]{2,1,0:T(8,128)(2,1)S(1)}, bf16[1,32,1152]{2,1,0:T(8,128)(2,1)S(1)}, u32[]{:S(2)}, u32[]{:S(2)}) %collective-permute-start.10) | collective-permute-done | bytes 73760 | tf_op jit(solution)/shard_map/ppermute | solution.py:41
  69.9 4.2 %collective-permute-done.7.refs_6_ = bf16[2,32,1152]{2,1,0:T(8,128)(2,1)S(1)} collective-permute-done((bf16[2,32,1152]{2,1,0:T(8,128)(2,1)S(1)}, bf16[2,32,1152]{2,1,0:T(8,128)(2,1)S(1)}, u32[]{:S(2)}, u32[]{:S(2)}) %collective-permute-start.7) | collective-permute-done | bytes 147488 | tf_op jit(solution)/shard_map/ppermute | solution.py:41
  74.8 6.3 %project.1 = (bf16[32,2048]{1,0:T(8,128)(2,1)}, bf16[32,2048]{1,0:T(8,128)(2,1)}, bf16[32,2048]{1,0:T(8,128)(2,1)}, bf16[32,2048]{1,0:T(8,128)(2,1)}) custom-call(bf16[1,32,1152]{2,1,0:T(8,128)(2,1)} %copy-done.2, bf16[2,32,1152]{2,1,0:T(8,128)(2,1)} %copy-done.5, bf16[1,32,1152]{2,1,0:T(8,128)(2,1)} %copy-done.14, bf16[2,32,1152]{2,1,0:T(8,128)(2,1)} %copy-done.6, ...), custom_call_target="tpu_custom_call" | custom-call | tf_op jit(solution)/shard_map/project/pallas_call | solution.py:297
  81.1 0.6 collective-permute-start.12
  81.8 3.2 %collective-permute-start.13 = (bf16[32,2048]{1,0:T(8,128)(2,1)}, bf16[32,2048]{1,0:T(8,128)(2,1)S(1)}, u32[]{:S(2)}, u32[]{:S(2)}) collective-permute-start(bf16[32,2048]{1,0:T(8,128)(2,1)} %get-tuple-element.59), channel_id=1, source_target_pairs={{0,2},{1,3},{2,0},{3,1},{4,6},{5,7},{6,4},{7,5},{8,10},{9,11},{10,... | collective-permute-start | bytes 393224 | tf_op jit(solution)/shard_map/ppermute | solution.py:41
  85.1 0.6 pad.4.refs_5_
  85.7 2.2 %collective-permute-done.12.refs_1_ = bf16[32,2048]{1,0:T(8,128)(2,1)S(1)} collective-permute-done((bf16[32,2048]{1,0:T(8,128)(2,1)}, bf16[32,2048]{1,0:T(8,128)(2,1)S(1)}, u32[]{:S(2)}, u32[]{:S(2)}) %collective-permute-start.12) | collective-permute-done | bytes 131104 | tf_op jit(solution)/shard_map/ppermute | solution.py:41
  88.0 9.7 %collective-permute-done.13.refs_2_ = bf16[32,2048]{1,0:T(8,128)(2,1)S(1)} collective-permute-done((bf16[32,2048]{1,0:T(8,128)(2,1)}, bf16[32,2048]{1,0:T(8,128)(2,1)S(1)}, u32[]{:S(2)}, u32[]{:S(2)}) %collective-permute-start.13) | collective-permute-done | bytes 131104 | tf_op jit(solution)/shard_map/ppermute | solution.py:41
  97.7 0.6 copy-done.9
  98.4 2.0 %normalize.1 = (f32[32,2048]{1,0:T(8,128)}, bf16[32,2176]{1,0:T(8,128)(2,1)}) custom-call(bf16[32,2048]{1,0:T(8,128)(2,1)} %residual_ref.1, bf16[32,2048]{1,0:T(8,128)(2,1)} %get-tuple-element.57.refs_0_, bf16[32,2048]{1,0:T(8,128)(2,1)} %copy-done.8, bf16[32,2048]{1,0:T(8,128)(2,1)} %copy-done.9, bf16[32,2048]{1,0:T(8,128)(2,1)} %copy-done.10, ...), custom_call_target="tpu_custom_call" | custom-call | tf_op jit(solution)/shard_map/normalize/pallas_call | solution.py:327
  100.4 1.7 %collective-permute-start.21 = (bf16[32,2176]{1,0:T(8,128)(2,1)}, bf16[32,2176]{1,0:T(8,128)(2,1)S(1)}, u32[]{:S(2)}, u32[]{:S(2)}) collective-permute-start(bf16[32,2176]{1,0:T(8,128)(2,1)} %get-tuple-element.62.refs_3_), channel_id=1, source_target_pairs={{0,8},{4,12},{8,0},{12,4},{1,9},{5,13},{9,1},{13,5},{2,10},{6,14},... | collective-permute-start | bytes 417800 | tf_op jit(solution)/shard_map/ppermute | solution.py:45
  102.2 2.0 %collective-permute-start.16 = (bf16[32,2176]{1,0:T(8,128)(2,1)}, bf16[32,2176]{1,0:T(8,128)(2,1)S(1)}, u32[]{:S(2)}, u32[]{:S(2)}) collective-permute-start(bf16[32,2176]{1,0:T(8,128)(2,1)} %get-tuple-element.62.refs_3_), channel_id=1, source_target_pairs={{0,1},{1,2},{2,3},{3,0},{4,5},{5,6},{6,7},{7,4},{8,9},{9,10},{10,1... | collective-permute-start | bytes 417800 | tf_op jit(solution)/shard_map/ppermute | solution.py:41
  104.2 0.9 collective-permute-start.15
  105.0 1.2 collective-permute-done.21.refs_7_
  106.2 1.9 %collective-permute-done.17.refs_2_ = bf16[32,2176]{1,0:T(8,128)(2,1)S(1)} collective-permute-done((bf16[32,2176]{1,0:T(8,128)(2,1)}, bf16[32,2176]{1,0:T(8,128)(2,1)S(1)}, u32[]{:S(2)}, u32[]{:S(2)}) %collective-permute-start.17) | collective-permute-done | bytes 139296 | tf_op jit(solution)/shard_map/ppermute | solution.py:41
  108.5 3.4 %collective-permute-done.16.refs_1_ = bf16[32,2176]{1,0:T(8,128)(2,1)S(1)} collective-permute-done((bf16[32,2176]{1,0:T(8,128)(2,1)}, bf16[32,2176]{1,0:T(8,128)(2,1)S(1)}, u32[]{:S(2)}, u32[]{:S(2)}) %collective-permute-start.16) | collective-permute-done | bytes 139296 | tf_op jit(solution)/shard_map/ppermute | solution.py:41
  112.1 4.6 %collective-permute-done.15.refs_0_ = bf16[32,2176]{1,0:T(8,128)(2,1)S(1)} collective-permute-done((bf16[32,2176]{1,0:T(8,128)(2,1)}, bf16[32,2176]{1,0:T(8,128)(2,1)S(1)}, u32[]{:S(2)}, u32[]{:S(2)}) %collective-permute-start.15) | collective-permute-done | bytes 139296 | tf_op jit(solution)/shard_map/ppermute | solution.py:41
  118.0 4.0 %collective-permute-done.18.refs_4_ = bf16[32,2176]{1,0:T(8,128)(2,1)S(1)} collective-permute-done((bf16[32,2176]{1,0:T(8,128)(2,1)S(1)}, bf16[32,2176]{1,0:T(8,128)(2,1)S(1)}, u32[]{:S(2)}, u32[]{:S(2)}) %collective-permute-start.18) | collective-permute-done | bytes 139296 | tf_op jit(solution)/shard_map/ppermute | solution.py:45
  122.0 1.3 collective-permute-done.26.refs_12_
  123.3 0.9 copy-done.1
  124.3 9.1 %run_expert.1 = (f32[256,2048]{1,0:T(8,128)S(1)}, bf16[256,2048]{1,0:T(8,128)(2,1)S(1)}) custom-call(s32[1]{0:T(128)} %bitcast.11.expert_ref, bf16[32,2176]{1,0:T(8,128)(2,1)S(1)} %collective-permute-done.15.refs_0_, bf16[32,2176]{1,0:T(8,128)(2,1)S(1)} %collective-permute-done.16.refs_1_, bf16[32,2176]{1,0:T(8,128)(2,1)S(1)} %collective-permute-done.17.refs_2_, ...), custom_call_target="tpu_custom_call" | custom-call | tf_op jit(solution)/shard_map/run_expert/pallas_call | solution.py:385
  133.5 2.5 %collective-permute-done.30 = bf16[256,2048]{1,0:T(8,128)(2,1)S(1)} collective-permute-done((bf16[256,2048]{1,0:T(8,128)(2,1)S(1)}, bf16[256,2048]{1,0:T(8,128)(2,1)S(1)}, u32[]{:S(2)}, u32[]{:S(2)}) %collective-permute-start.30) | collective-permute-done | bytes 1048608 | tf_op jit(solution)/shard_map/ppermute | solution.py:45
  136.9 1.7 %collective-permute-start.35 = (bf16[32,2048]{1,0:T(8,128)(2,1)S(1)}, bf16[32,2048]{1,0:T(8,128)(2,1)S(1)}, u32[]{:S(2)}, u32[]{:S(2)}) collective-permute-start(bf16[32,2048]{1,0:T(8,128)(2,1)S(1)} %get-tuple-element.72), channel_id=1, source_target_pairs={{0,8},{4,12},{8,0},{12,4},{1,9},{5,13},{9,1},{13,5},{2,10},{6,14},... | collective-permute-start | bytes 393224 | tf_op jit(solution)/shard_map/ppermute | solution.py:45
  138.9 1.7 %collective-permute-start.37 = (bf16[32,2048]{1,0:T(8,128)(2,1)S(1)}, bf16[32,2048]{1,0:T(8,128)(2,1)S(1)}, u32[]{:S(2)}, u32[]{:S(2)}) collective-permute-start(bf16[32,2048]{1,0:T(8,128)(2,1)S(1)} %get-tuple-element.71), channel_id=1, source_target_pairs={{0,8},{4,12},{8,0},{12,4},{1,9},{5,13},{9,1},{13,5},{2,10},{6,14},... | collective-permute-start | bytes 393224 | tf_op jit(solution)/shard_map/ppermute | solution.py:45
  140.6 2.3 %collective-permute-done.31 = bf16[32,2048]{1,0:T(8,128)(2,1)S(1)} collective-permute-done((bf16[32,2048]{1,0:T(8,128)(2,1)S(1)}, bf16[32,2048]{1,0:T(8,128)(2,1)S(1)}, u32[]{:S(2)}, u32[]{:S(2)}) %collective-permute-start.31) | collective-permute-done | bytes 131104 | tf_op jit(solution)/shard_map/ppermute | solution.py:45
  142.9 2.8 %collective-permute-done.35 = bf16[32,2048]{1,0:T(8,128)(2,1)S(1)} collective-permute-done((bf16[32,2048]{1,0:T(8,128)(2,1)S(1)}, bf16[32,2048]{1,0:T(8,128)(2,1)S(1)}, u32[]{:S(2)}, u32[]{:S(2)}) %collective-permute-start.35) | collective-permute-done | bytes 131104 | tf_op jit(solution)/shard_map/ppermute | solution.py:45
  145.7 2.8 %collective-permute-done.33 = bf16[32,2048]{1,0:T(8,128)(2,1)S(1)} collective-permute-done((bf16[32,2048]{1,0:T(8,128)(2,1)S(1)}, bf16[32,2048]{1,0:T(8,128)(2,1)S(1)}, u32[]{:S(2)}, u32[]{:S(2)}) %collective-permute-start.33) | collective-permute-done | bytes 131104 | tf_op jit(solution)/shard_map/ppermute | solution.py:45
  148.7 3.0 %collective-permute-start.36 = (bf16[32,2048]{1,0:T(8,128)(2,1)S(1)}, bf16[32,2048]{1,0:T(8,128)(2,1)S(1)}, u32[]{:S(2)}, u32[]{:S(2)}) collective-permute-start(bf16[32,2048]{1,0:T(8,128)(2,1)S(1)} %get-tuple-element.68), channel_id=1, source_target_pairs={{0,1},{1,2},{2,3},{3,0},{4,5},{5,6},{6,7},{7,4},{8,9},{9,10},{10,1... | collective-permute-start | bytes 393224 | tf_op jit(solution)/shard_map/ppermute | solution.py:41
  151.7 0.9 collective-permute-start.34
  152.6 6.5 %collective-permute-done.32 = bf16[32,2048]{1,0:T(8,128)(2,1)S(1)} collective-permute-done((bf16[32,2048]{1,0:T(8,128)(2,1)S(1)}, bf16[32,2048]{1,0:T(8,128)(2,1)S(1)}, u32[]{:S(2)}, u32[]{:S(2)}) %collective-permute-start.32) | collective-permute-done | bytes 131104 | tf_op jit(solution)/shard_map/ppermute | solution.py:41
  159.1 1.3 collective-permute-done.34
  160.4 0.8 fusion.2
  (83 shorter events, 5.3 us)
Async XLA Ops:
  0.0 18.2 %collective-permute-start = (bf16[32,4096]{1,0:T(8,128)(2,1)}, bf16[32,4096]{1,0:T(8,128)(2,1)S(1)}, u32[]{:S(2)}, u32[]{:S(2)}) collective-permute-start(bf16[32,4096]{1,0:T(8,128)(2,1)} %refs_3_.1), channel_id=1, source_target_pairs={{0,1},{1,2},{2,3},{3,0},{4,5},{5,6},{6,7},{7,4},{8,9},{9,10},{10,1... | collective-permute-start | bytes 786440 | tf_op jit(solution)/shard_map/ppermute | solution.py:41
  3.0 31.2 %collective-permute-start.3 = (bf16[32,4096]{1,0:T(8,128)(2,1)}, bf16[32,4096]{1,0:T(8,128)(2,1)S(1)}, u32[]{:S(2)}, u32[]{:S(2)}) collective-permute-start(bf16[32,4096]{1,0:T(8,128)(2,1)} %refs_3_.1), channel_id=1, source_target_pairs={{0,2},{1,3},{2,0},{3,1},{4,6},{5,7},{6,4},{7,5},{8,10},{9,11},{10,... | collective-permute-start | bytes 786440 | tf_op jit(solution)/shard_map/ppermute | solution.py:41
  5.6 15.7 %collective-permute-start.1 = (bf16[32,4096]{1,0:T(8,128)(2,1)}, bf16[32,4096]{1,0:T(8,128)(2,1)S(1)}, u32[]{:S(2)}, u32[]{:S(2)}) collective-permute-start(bf16[32,4096]{1,0:T(8,128)(2,1)} %refs_3_.1), channel_id=1, source_target_pairs={{0,3},{1,0},{2,1},{3,2},{4,7},{5,4},{6,5},{7,6},{8,11},{9,8},{10,9... | collective-permute-start | bytes 786440 | tf_op jit(solution)/shard_map/ppermute | solution.py:41
  17.2 37.4 %collective-permute-start.6 = (bf16[1,32,1152]{2,1,0:T(8,128)(2,1)S(1)}, bf16[1,32,1152]{2,1,0:T(8,128)(2,1)S(1)}, u32[]{:S(2)}, u32[]{:S(2)}) collective-permute-start(bf16[1,32,1152]{2,1,0:T(8,128)(2,1)S(1)} %get-tuple-element.50), channel_id=1, source_target_pairs={{0,1},{1,2},{2,3},{3,0},{4,5},{5,6},{6,7},{7,4},{8,9},{9,10},{10,1... | collective-permute-start | bytes 221192 | tf_op jit(solution)/shard_map/ppermute | solution.py:41
  17.9 39.6 %collective-permute-start.9 = (bf16[1,32,1152]{2,1,0:T(8,128)(2,1)S(1)}, bf16[1,32,1152]{2,1,0:T(8,128)(2,1)S(1)}, u32[]{:S(2)}, u32[]{:S(2)}) collective-permute-start(bf16[1,32,1152]{2,1,0:T(8,128)(2,1)S(1)} %get-tuple-element.54), channel_id=1, source_target_pairs={{0,2},{1,3},{2,0},{3,1},{4,6},{5,7},{6,4},{7,5},{8,10},{9,11},{10,... | collective-permute-start | bytes 221192 | tf_op jit(solution)/shard_map/ppermute | solution.py:41
  18.2 39.4 %collective-permute-start.11 = (bf16[1,32,1152]{2,1,0:T(8,128)(2,1)S(1)}, bf16[1,32,1152]{2,1,0:T(8,128)(2,1)S(1)}, u32[]{:S(2)}, u32[]{:S(2)}) collective-permute-start(bf16[1,32,1152]{2,1,0:T(8,128)(2,1)S(1)} %get-tuple-element.56), channel_id=1, source_target_pairs={{0,3},{1,0},{2,1},{3,2},{4,7},{5,4},{6,5},{7,6},{8,11},{9,8},{10,9... | collective-permute-start | bytes 221192 | tf_op jit(solution)/shard_map/ppermute | solution.py:41
  34.2 8.7 %copy-start = (bf16[2,32,1152]{2,1,0:T(8,128)(2,1)}, bf16[2,32,1152]{2,1,0:T(8,128)(2,1)S(1)}, u32[]{:S(2)}) copy-start(bf16[2,32,1152]{2,1,0:T(8,128)(2,1)S(1)} %get-tuple-element.49.refs_4_) | copy-start | bytes 442372
  43.5 15.5 %collective-permute-start.4 = (bf16[1,32,1152]{2,1,0:T(8,128)(2,1)S(1)}, bf16[1,32,1152]{2,1,0:T(8,128)(2,1)S(1)}, u32[]{:S(2)}, u32[]{:S(2)}) collective-permute-start(bf16[1,32,1152]{2,1,0:T(8,128)(2,1)S(1)} %get-tuple-element.47), channel_id=1, source_target_pairs={{0,2},{1,3},{2,0},{3,1},{4,6},{5,7},{6,4},{7,5},{8,10},{9,11},{10,... | collective-permute-start | bytes 221192 | tf_op jit(solution)/shard_map/ppermute | solution.py:41
  53.6 16.3 %collective-permute-start.2 = (bf16[2,32,1152]{2,1,0:T(8,128)(2,1)S(1)}, bf16[2,32,1152]{2,1,0:T(8,128)(2,1)S(1)}, u32[]{:S(2)}, u32[]{:S(2)}) collective-permute-start(bf16[2,32,1152]{2,1,0:T(8,128)(2,1)S(1)} %get-tuple-element.45), channel_id=1, source_target_pairs={{0,1},{1,2},{2,3},{3,0},{4,5},{5,6},{6,7},{7,4},{8,9},{9,10},{10,1... | collective-permute-start | bytes 442376 | tf_op jit(solution)/shard_map/ppermute | solution.py:41
  54.6 19.6 %copy-start.11 = (bf16[1,32,1152]{2,1,0:T(8,128)(2,1)}, bf16[1,32,1152]{2,1,0:T(8,128)(2,1)S(1)}, u32[]{:S(2)}) copy-start(bf16[1,32,1152]{2,1,0:T(8,128)(2,1)S(1)} %collective-permute-done.6.refs_5_) | copy-start | bytes 221188
  54.6 15.4 %collective-permute-start.5 = (bf16[2,32,1152]{2,1,0:T(8,128)(2,1)S(1)}, bf16[2,32,1152]{2,1,0:T(8,128)(2,1)S(1)}, u32[]{:S(2)}, u32[]{:S(2)}) collective-permute-start(bf16[2,32,1152]{2,1,0:T(8,128)(2,1)S(1)} %get-tuple-element.48), channel_id=1, source_target_pairs={{0,3},{1,0},{2,1},{3,2},{4,7},{5,4},{6,5},{7,6},{8,11},{9,8},{10,9... | collective-permute-start | bytes 442376 | tf_op jit(solution)/shard_map/ppermute | solution.py:41
  57.5 16.7 %copy-start.12 = (bf16[1,32,1152]{2,1,0:T(8,128)(2,1)}, bf16[1,32,1152]{2,1,0:T(8,128)(2,1)S(1)}, u32[]{:S(2)}) copy-start(bf16[1,32,1152]{2,1,0:T(8,128)(2,1)S(1)} %collective-permute-done.9.refs_9_) | copy-start | bytes 221188
  57.5 16.7 %collective-permute-start.7 = (bf16[2,32,1152]{2,1,0:T(8,128)(2,1)S(1)}, bf16[2,32,1152]{2,1,0:T(8,128)(2,1)S(1)}, u32[]{:S(2)}, u32[]{:S(2)}) collective-permute-start(bf16[2,32,1152]{2,1,0:T(8,128)(2,1)S(1)} %get-tuple-element.51), channel_id=1, source_target_pairs={{0,2},{1,3},{2,0},{3,1},{4,6},{5,7},{6,4},{7,5},{8,10},{9,11},{10,... | collective-permute-start | bytes 442376 | tf_op jit(solution)/shard_map/ppermute | solution.py:41
  57.6 16.6 %copy-start.13 = (bf16[1,32,1152]{2,1,0:T(8,128)(2,1)}, bf16[1,32,1152]{2,1,0:T(8,128)(2,1)S(1)}, u32[]{:S(2)}) copy-start(bf16[1,32,1152]{2,1,0:T(8,128)(2,1)S(1)} %collective-permute-done.11.refs_11_) | copy-start | bytes 221188
  57.6 8.6 %collective-permute-start.8 = (bf16[1,32,1152]{2,1,0:T(8,128)(2,1)S(1)}, bf16[1,32,1152]{2,1,0:T(8,128)(2,1)S(1)}, u32[]{:S(2)}, u32[]{:S(2)}) collective-permute-start(bf16[1,32,1152]{2,1,0:T(8,128)(2,1)S(1)} %get-tuple-element.52), channel_id=1, source_target_pairs={{0,3},{1,0},{2,1},{3,2},{4,7},{5,4},{6,5},{7,6},{8,11},{9,8},{10,9... | collective-permute-start | bytes 221192 | tf_op jit(solution)/shard_map/ppermute | solution.py:41
  59.0 15.2 %copy-start.14 = (bf16[1,32,1152]{2,1,0:T(8,128)(2,1)}, bf16[1,32,1152]{2,1,0:T(8,128)(2,1)S(1)}, u32[]{:S(2)}) copy-start(bf16[1,32,1152]{2,1,0:T(8,128)(2,1)S(1)} %collective-permute-done.4.refs_2_) | copy-start | bytes 221188
  59.0 10.9 %collective-permute-start.10 = (bf16[1,32,1152]{2,1,0:T(8,128)(2,1)S(1)}, bf16[1,32,1152]{2,1,0:T(8,128)(2,1)S(1)}, u32[]{:S(2)}, u32[]{:S(2)}) collective-permute-start(bf16[1,32,1152]{2,1,0:T(8,128)(2,1)S(1)} %get-tuple-element.55), channel_id=1, source_target_pairs={{0,1},{1,2},{2,3},{3,0},{4,5},{5,6},{6,7},{7,4},{8,9},{9,10},{10,1... | collective-permute-start | bytes 221192 | tf_op jit(solution)/shard_map/ppermute | solution.py:41
  66.2 8.0 %copy-start.15 = (bf16[1,32,1152]{2,1,0:T(8,128)(2,1)}, bf16[1,32,1152]{2,1,0:T(8,128)(2,1)S(1)}, u32[]{:S(2)}) copy-start(bf16[1,32,1152]{2,1,0:T(8,128)(2,1)S(1)} %collective-permute-done.8.refs_7_) | copy-start | bytes 221188
  74.8 10.2 %copy-start.17 = (f32[32,8]{0,1:T(8,128)S(1)}, f32[32,8]{0,1:T(8,128)}, u32[]{:S(2)}) copy-start(f32[32,8]{0,1:T(8,128)} %param.25) | copy-start | bytes 3076
  74.8 10.2 %copy-start.18 = (s32[32,8]{0,1:T(8,128)S(1)}, s32[32,8]{0,1:T(8,128)}, u32[]{:S(2)}) copy-start(s32[32,8]{0,1:T(8,128)} %param.24) | copy-start | bytes 3076
  81.1 6.8 %collective-permute-start.12 = (bf16[32,2048]{1,0:T(8,128)(2,1)}, bf16[32,2048]{1,0:T(8,128)(2,1)S(1)}, u32[]{:S(2)}, u32[]{:S(2)}) collective-permute-start(bf16[32,2048]{1,0:T(8,128)(2,1)} %get-tuple-element.58), channel_id=1, source_target_pairs={{0,3},{1,0},{2,1},{3,2},{4,7},{5,4},{6,5},{7,6},{8,11},{9,8},{10,9... | collective-permute-start | bytes 393224 | tf_op jit(solution)/shard_map/ppermute | solution.py:41
  81.8 15.9 %collective-permute-start.13 = (bf16[32,2048]{1,0:T(8,128)(2,1)}, bf16[32,2048]{1,0:T(8,128)(2,1)S(1)}, u32[]{:S(2)}, u32[]{:S(2)}) collective-permute-start(bf16[32,2048]{1,0:T(8,128)(2,1)} %get-tuple-element.59), channel_id=1, source_target_pairs={{0,2},{1,3},{2,0},{3,1},{4,6},{5,7},{6,4},{7,5},{8,10},{9,11},{10,... | collective-permute-start | bytes 393224 | tf_op jit(solution)/shard_map/ppermute | solution.py:41
  85.0 12.7 %collective-permute-start.14 = (bf16[32,2048]{1,0:T(8,128)(2,1)}, bf16[32,2048]{1,0:T(8,128)(2,1)S(1)}, u32[]{:S(2)}, u32[]{:S(2)}) collective-permute-start(bf16[32,2048]{1,0:T(8,128)(2,1)} %get-tuple-element.60), channel_id=1, source_target_pairs={{0,1},{1,2},{2,3},{3,0},{4,5},{5,6},{6,7},{7,4},{8,9},{9,10},{10,1... | collective-permute-start | bytes 393224 | tf_op jit(solution)/shard_map/ppermute | solution.py:41
  88.0 9.8 %copy-start.8 = (bf16[32,2048]{1,0:T(8,128)(2,1)}, bf16[32,2048]{1,0:T(8,128)(2,1)S(1)}, u32[]{:S(2)}) copy-start(bf16[32,2048]{1,0:T(8,128)(2,1)S(1)} %collective-permute-done.12.refs_1_) | copy-start | bytes 393220
  100.4 5.8 %collective-permute-start.21 = (bf16[32,2176]{1,0:T(8,128)(2,1)}, bf16[32,2176]{1,0:T(8,128)(2,1)S(1)}, u32[]{:S(2)}, u32[]{:S(2)}) collective-permute-start(bf16[32,2176]{1,0:T(8,128)(2,1)} %get-tuple-element.62.refs_3_), channel_id=1, source_target_pairs={{0,8},{4,12},{8,0},{12,4},{1,9},{5,13},{9,1},{13,5},{2,10},{6,14},... | collective-permute-start | bytes 417800 | tf_op jit(solution)/shard_map/ppermute | solution.py:45
  102.2 5.9 %collective-permute-start.17 = (bf16[32,2176]{1,0:T(8,128)(2,1)}, bf16[32,2176]{1,0:T(8,128)(2,1)S(1)}, u32[]{:S(2)}, u32[]{:S(2)}) collective-permute-start(bf16[32,2176]{1,0:T(8,128)(2,1)} %get-tuple-element.62.refs_3_), channel_id=1, source_target_pairs={{0,3},{1,0},{2,1},{3,2},{4,7},{5,4},{6,5},{7,6},{8,11},{9,8},{10,9... | collective-permute-start | bytes 417800 | tf_op jit(solution)/shard_map/ppermute | solution.py:41
  102.2 5.9 %collective-permute-start.25 = (bf16[32,2176]{1,0:T(8,128)(2,1)}, bf16[32,2176]{1,0:T(8,128)(2,1)S(1)}, u32[]{:S(2)}, u32[]{:S(2)}) collective-permute-start(bf16[32,2176]{1,0:T(8,128)(2,1)} %get-tuple-element.62.refs_3_), channel_id=1, source_target_pairs={{0,4},{4,0},{8,12},{12,8},{1,5},{5,1},{9,13},{13,9},{2,6},{6,2},{1... | collective-permute-start | bytes 417800 | tf_op jit(solution)/shard_map/ppermute | solution.py:45
  102.2 9.7 %collective-permute-start.16 = (bf16[32,2176]{1,0:T(8,128)(2,1)}, bf16[32,2176]{1,0:T(8,128)(2,1)S(1)}, u32[]{:S(2)}, u32[]{:S(2)}) collective-permute-start(bf16[32,2176]{1,0:T(8,128)(2,1)} %get-tuple-element.62.refs_3_), channel_id=1, source_target_pairs={{0,1},{1,2},{2,3},{3,0},{4,5},{5,6},{6,7},{7,4},{8,9},{9,10},{10,1... | collective-permute-start | bytes 417800 | tf_op jit(solution)/shard_map/ppermute | solution.py:41
  104.2 12.5 %collective-permute-start.15 = (bf16[32,2176]{1,0:T(8,128)(2,1)}, bf16[32,2176]{1,0:T(8,128)(2,1)S(1)}, u32[]{:S(2)}, u32[]{:S(2)}) collective-permute-start(bf16[32,2176]{1,0:T(8,128)(2,1)} %get-tuple-element.62.refs_3_), channel_id=1, source_target_pairs={{0,2},{1,3},{2,0},{3,1},{4,6},{5,7},{6,4},{7,5},{8,10},{9,11},{10,... | collective-permute-start | bytes 417800 | tf_op jit(solution)/shard_map/ppermute | solution.py:41
  106.2 10.8 %collective-permute-start.29 = (bf16[32,2176]{1,0:T(8,128)(2,1)S(1)}, bf16[32,2176]{1,0:T(8,128)(2,1)S(1)}, u32[]{:S(2)}, u32[]{:S(2)}) collective-permute-start(bf16[32,2176]{1,0:T(8,128)(2,1)S(1)} %collective-permute-done.21.refs_7_), channel_id=1, source_target_pairs={{0,4},{4,0},{8,12},{12,8},{1,5},{5,1},{9,13},{13,9},{2,6},{6,2},{1... | collective-permute-start | bytes 417800 | tf_op jit(solution)/shard_map/ppermute | solution.py:45
  108.1 8.9 %collective-permute-start.24 = (bf16[32,2176]{1,0:T(8,128)(2,1)S(1)}, bf16[32,2176]{1,0:T(8,128)(2,1)S(1)}, u32[]{:S(2)}, u32[]{:S(2)}) collective-permute-start(bf16[32,2176]{1,0:T(8,128)(2,1)S(1)} %collective-permute-done.17.refs_2_), channel_id=1, source_target_pairs={{0,4},{4,0},{8,12},{12,8},{1,5},{5,1},{9,13},{13,9},{2,6},{6,2},{1... | collective-permute-start | bytes 417800 | tf_op jit(solution)/shard_map/ppermute | solution.py:45
  108.1 9.4 %collective-permute-start.20 = (bf16[32,2176]{1,0:T(8,128)(2,1)S(1)}, bf16[32,2176]{1,0:T(8,128)(2,1)S(1)}, u32[]{:S(2)}, u32[]{:S(2)}) collective-permute-start(bf16[32,2176]{1,0:T(8,128)(2,1)S(1)} %collective-permute-done.17.refs_2_), channel_id=1, source_target_pairs={{0,8},{4,12},{8,0},{12,4},{1,9},{5,13},{9,1},{13,5},{2,10},{6,14},... | collective-permute-start | bytes 417800 | tf_op jit(solution)/shard_map/ppermute | solution.py:45
  111.9 5.7 %collective-permute-start.19 = (bf16[32,2176]{1,0:T(8,128)(2,1)S(1)}, bf16[32,2176]{1,0:T(8,128)(2,1)S(1)}, u32[]{:S(2)}, u32[]{:S(2)}) collective-permute-start(bf16[32,2176]{1,0:T(8,128)(2,1)S(1)} %collective-permute-done.16.refs_1_), channel_id=1, source_target_pairs={{0,8},{4,12},{8,0},{12,4},{1,9},{5,13},{9,1},{13,5},{2,10},{6,14},... | collective-permute-start | bytes 417800 | tf_op jit(solution)/shard_map/ppermute | solution.py:45
  116.7 5.3 %collective-permute-start.18 = (bf16[32,2176]{1,0:T(8,128)(2,1)S(1)}, bf16[32,2176]{1,0:T(8,128)(2,1)S(1)}, u32[]{:S(2)}, u32[]{:S(2)}) collective-permute-start(bf16[32,2176]{1,0:T(8,128)(2,1)S(1)} %collective-permute-done.15.refs_0_), channel_id=1, source_target_pairs={{0,8},{4,12},{8,0},{12,4},{1,9},{5,13},{9,1},{13,5},{2,10},{6,14},... | collective-permute-start | bytes 417800 | tf_op jit(solution)/shard_map/ppermute | solution.py:45
  117.0 5.0 %collective-permute-start.23 = (bf16[32,2176]{1,0:T(8,128)(2,1)S(1)}, bf16[32,2176]{1,0:T(8,128)(2,1)S(1)}, u32[]{:S(2)}, u32[]{:S(2)}) collective-permute-start(bf16[32,2176]{1,0:T(8,128)(2,1)S(1)} %collective-permute-done.16.refs_1_), channel_id=1, source_target_pairs={{0,4},{4,0},{8,12},{12,8},{1,5},{5,1},{9,13},{13,9},{2,6},{6,2},{1... | collective-permute-start | bytes 417800 | tf_op jit(solution)/shard_map/ppermute | solution.py:45
  117.0 5.0 %collective-permute-start.22 = (bf16[32,2176]{1,0:T(8,128)(2,1)S(1)}, bf16[32,2176]{1,0:T(8,128)(2,1)S(1)}, u32[]{:S(2)}, u32[]{:S(2)}) collective-permute-start(bf16[32,2176]{1,0:T(8,128)(2,1)S(1)} %collective-permute-done.15.refs_0_), channel_id=1, source_target_pairs={{0,4},{4,0},{8,12},{12,8},{1,5},{5,1},{9,13},{13,9},{2,6},{6,2},{1... | collective-permute-start | bytes 417800 | tf_op jit(solution)/shard_map/ppermute | solution.py:45
  117.5 4.5 %collective-permute-start.28 = (bf16[32,2176]{1,0:T(8,128)(2,1)S(1)}, bf16[32,2176]{1,0:T(8,128)(2,1)S(1)}, u32[]{:S(2)}, u32[]{:S(2)}) collective-permute-start(bf16[32,2176]{1,0:T(8,128)(2,1)S(1)} %collective-permute-done.20.refs_6_), channel_id=1, source_target_pairs={{0,4},{4,0},{8,12},{12,8},{1,5},{5,1},{9,13},{13,9},{2,6},{6,2},{1... | collective-permute-start | bytes 417800 | tf_op jit(solution)/shard_map/ppermute | solution.py:45
  117.6 4.4 %collective-permute-start.27 = (bf16[32,2176]{1,0:T(8,128)(2,1)S(1)}, bf16[32,2176]{1,0:T(8,128)(2,1)S(1)}, u32[]{:S(2)}, u32[]{:S(2)}) collective-permute-start(bf16[32,2176]{1,0:T(8,128)(2,1)S(1)} %collective-permute-done.19.refs_5_), channel_id=1, source_target_pairs={{0,4},{4,0},{8,12},{12,8},{1,5},{5,1},{9,13},{13,9},{2,6},{6,2},{1... | collective-permute-start | bytes 417800 | tf_op jit(solution)/shard_map/ppermute | solution.py:45
  122.0 1.4 collective-permute-start.26
  133.3 2.7 %collective-permute-start.30 = (bf16[256,2048]{1,0:T(8,128)(2,1)S(1)}, bf16[256,2048]{1,0:T(8,128)(2,1)S(1)}, u32[]{:S(2)}, u32[]{:S(2)}) collective-permute-start(bf16[256,2048]{1,0:T(8,128)(2,1)S(1)} %get-tuple-element.64), channel_id=1, source_target_pairs={{0,4},{4,0},{8,12},{12,8},{1,5},{5,1},{9,13},{13,9},{2,6},{6,2},{1... | collective-permute-start | bytes 3145736 | tf_op jit(solution)/shard_map/ppermute | solution.py:45
  136.5 23.9 %copy-start.4 = (f32[32,2048]{1,0:T(8,128)S(1)}, f32[32,2048]{1,0:T(8,128)}, u32[]{:S(2)}) copy-start(f32[32,2048]{1,0:T(8,128)} %get-tuple-element.61) | copy-start | bytes 786436
  136.5 6.4 %collective-permute-start.31 = (bf16[32,2048]{1,0:T(8,128)(2,1)S(1)}, bf16[32,2048]{1,0:T(8,128)(2,1)S(1)}, u32[]{:S(2)}, u32[]{:S(2)}) collective-permute-start(bf16[32,2048]{1,0:T(8,128)(2,1)S(1)} %get-tuple-element.70), channel_id=1, source_target_pairs={{0,8},{4,12},{8,0},{12,4},{1,9},{5,13},{9,1},{13,5},{2,10},{6,14},... | collective-permute-start | bytes 393224 | tf_op jit(solution)/shard_map/ppermute | solution.py:45
  136.9 8.8 %collective-permute-start.35 = (bf16[32,2048]{1,0:T(8,128)(2,1)S(1)}, bf16[32,2048]{1,0:T(8,128)(2,1)S(1)}, u32[]{:S(2)}, u32[]{:S(2)}) collective-permute-start(bf16[32,2048]{1,0:T(8,128)(2,1)S(1)} %get-tuple-element.72), channel_id=1, source_target_pairs={{0,8},{4,12},{8,0},{12,4},{1,9},{5,13},{9,1},{13,5},{2,10},{6,14},... | collective-permute-start | bytes 393224 | tf_op jit(solution)/shard_map/ppermute | solution.py:45
  138.6 9.9 %collective-permute-start.33 = (bf16[32,2048]{1,0:T(8,128)(2,1)S(1)}, bf16[32,2048]{1,0:T(8,128)(2,1)S(1)}, u32[]{:S(2)}, u32[]{:S(2)}) collective-permute-start(bf16[32,2048]{1,0:T(8,128)(2,1)S(1)} %get-tuple-element.73), channel_id=1, source_target_pairs={{0,8},{4,12},{8,0},{12,4},{1,9},{5,13},{9,1},{13,5},{2,10},{6,14},... | collective-permute-start | bytes 393224 | tf_op jit(solution)/shard_map/ppermute | solution.py:45
  138.9 13.7 %collective-permute-start.37 = (bf16[32,2048]{1,0:T(8,128)(2,1)S(1)}, bf16[32,2048]{1,0:T(8,128)(2,1)S(1)}, u32[]{:S(2)}, u32[]{:S(2)}) collective-permute-start(bf16[32,2048]{1,0:T(8,128)(2,1)S(1)} %get-tuple-element.71), channel_id=1, source_target_pairs={{0,8},{4,12},{8,0},{12,4},{1,9},{5,13},{9,1},{13,5},{2,10},{6,14},... | collective-permute-start | bytes 393224 | tf_op jit(solution)/shard_map/ppermute | solution.py:45
  148.6 10.4 %collective-permute-start.32 = (bf16[32,2048]{1,0:T(8,128)(2,1)S(1)}, bf16[32,2048]{1,0:T(8,128)(2,1)S(1)}, u32[]{:S(2)}, u32[]{:S(2)}) collective-permute-start(bf16[32,2048]{1,0:T(8,128)(2,1)S(1)} %get-tuple-element.67), channel_id=1, source_target_pairs={{0,2},{1,3},{2,0},{3,1},{4,6},{5,7},{6,4},{7,5},{8,10},{9,11},{10,... | collective-permute-start | bytes 393224 | tf_op jit(solution)/shard_map/ppermute | solution.py:41
  148.7 10.3 %collective-permute-start.36 = (bf16[32,2048]{1,0:T(8,128)(2,1)S(1)}, bf16[32,2048]{1,0:T(8,128)(2,1)S(1)}, u32[]{:S(2)}, u32[]{:S(2)}) collective-permute-start(bf16[32,2048]{1,0:T(8,128)(2,1)S(1)} %get-tuple-element.68), channel_id=1, source_target_pairs={{0,1},{1,2},{2,3},{3,0},{4,5},{5,6},{6,7},{7,4},{8,9},{9,10},{10,1... | collective-permute-start | bytes 393224 | tf_op jit(solution)/shard_map/ppermute | solution.py:41
  151.7 8.6 %collective-permute-start.34 = (bf16[32,2048]{1,0:T(8,128)(2,1)S(1)}, bf16[32,2048]{1,0:T(8,128)(2,1)S(1)}, u32[]{:S(2)}, u32[]{:S(2)}) collective-permute-start(bf16[32,2048]{1,0:T(8,128)(2,1)S(1)} %get-tuple-element.69), channel_id=1, source_target_pairs={{0,3},{1,0},{2,1},{3,2},{4,7},{5,4},{6,5},{7,6},{8,11},{9,8},{10,9... | collective-permute-start | bytes 393224 | tf_op jit(solution)/shard_map/ppermute | solution.py:41
  (9 other events, 17.1 us)
where the time goes:
time: 162 us; the launch traced here: 161 us
  waiting for transfers between devices  60.5 us (37%)
  Pallas kernels  47.7 us (29%)
  starting transfers between devices  46.3 us (29%)
  local copies, waits for them, and re-layouts  4.17 us (3%)
    ppermute x21, waiting for transfers between devices, shifted(): lax.ppermute(array, axis, [(i, (i + by) % size) for i in range(size)])  43.6 us
    ppermute x21, starting transfers between devices, shifted(): lax.ppermute(array, axis, [(i, (i + by) % size) for i in range(size)])  38.3 us
    pallas_call x3, Pallas kernels, attend(): pl.pallas_call(body, in_specs=[SM] * 3 + [HBM if own_first and n == 0 els...  30.3 us
    ppermute x17, waiting for transfers between devices, swapped(): lax.ppermute(array, axis, [(i, i ^ bit) for i in range(lax.axis_size(axis...  16.9 us
    pallas_call x1, Pallas kernels, run_expert(): pl.pallas_call(body, grid=(steps,), in_specs=[SM] + [VM] * count + [pl.Bl...  9.06 us
    ppermute x17, starting transfers between devices, swapped(): lax.ppermute(array, axis, [(i, i ^ bit) for i in range(lax.axis_size(axis...  8.01 us
    pallas_call x1, Pallas kernels, project(): pl.pallas_call(body, grid=(D // step,), in_specs=[VM] * len(arrays) + [pl...  6.31 us
    unnamed x38, local copies, waits for them, and re-layouts  3.45 us
  transfers between devices with their start and end apart: 38, of which 18 were waited for; matrix products, arithmetic and copies ran while one was open for 1% of the time, Pallas kernels for 19%

commit v1 on v0

--- a/solution.py
+++ b/solution.py
@@ -467,7 +467,13 @@
     assert key_cache.shape[0] == 1 and rows * kv_count == BLOCK
 
     near_first = sorted(range(kv_count), key=lambda c: min(c, kv_count - c))
-    chunks = {c: shifted(queries, "kv", c) for c in near_first}
+    chunks = {}
+    waiting = queries
+    for c in near_first:
+        distance = min(c, kv_count - c)
+        if distance == 2:
+            waiting = lax.optimization_barrier((queries, chunks[1], chunks[kv_count - 1]))[0]
+        chunks[c] = shifted(waiting, "kv", c)
     bounds = jnp.stack([jnp.clip(lengths[0] - kv_place * cached, 0, cached), kv_place * rows]).astype(jnp.int32)
     blocks = (kv_place + 1 + jnp.arange(kv_count, dtype=jnp.int32)) % kv_count
     if kv_count == 4:
@@ -476,18 +482,24 @@
         calls = [near_first[at : at + 2] for at in range(0, kv_count, 2)]
     shares = {}
 
-    def send(k, outs, call):
-        landed = shifted(outs[k - 1], "kv", k)
-        for index, c in enumerate(call):
-            shares[k, c] = (landed, index)
+    def send(outs, call):
+        landed = [shifted(outs[k - 1], "kv", k) for k in range(kv_count)]
+        for k in range(kv_count):
+            for index, c in enumerate(call):
+                shares[k, c] = (landed[k], index)
+        return landed
 
     outs = None
+    sent = []
     for call in calls:
         places = jnp.stack([(kv_place - c) % kv_count for c in call]).astype(jnp.int32)
         if outs is not None:
-            places, *outs = lax.optimization_barrier((places, *outs))
-            for k in range(kv_count):
-                send(k, outs, before)
+            places, outs, sent = lax.optimization_barrier((places, outs, sent))
+            for k, landed in enumerate(sent):
+                for index, c in enumerate(earlier):
+                    shares[k, c] = (landed, index)
+            sent = send(outs, before)
+            earlier = before
         outs = attend(
             bounds,
             blocks,
@@ -501,8 +513,7 @@
             0 in call,
         )
         before = call
-    for k in range(kv_count):
-        send(k, outs, before)
+    send(outs, before)
     pieces = [[shares[k, (t - k) % kv_count] for k in range(kv_count)] for t in range(kv_count)]
     projected = project(pieces, out_weight, heads)
     landed = [shifted(projected[t], "kv", -t) for t in range(kv_count)]

time: 162 us -> 143 us (0.88)
  waiting for transfers between devices: 60.5 us -> 46.7 us
  starting transfers between devices: 46.3 us -> 40.8 us
    ppermute x21, waiting for transfers between devices: 43.6 us -> 30.5 us  [shifted(): lax.ppermute(array, axis, [(i, (i + by) % size) for i in range(size)])]
    ppermute x21, starting transfers between devices: 38.3 us -> 31.7 us  [shifted(): lax.ppermute(array, axis, [(i, (i + by) % size) for i in range(size)])]
    unnamed x38 -> x40, local copies, waits for them, and re-layouts: 3.45 us -> 3.49 us
  transfers between devices with their start and end apart: 38 -> 38, of which waited for: 18 -> 17; matrix products, arithmetic and copies ran while one was open for 1% -> 1% of each run, Pallas kernels for 19% -> 21%
where the time goes in v1:
time: 143 us; the launch traced here: 142 us
  Pallas kernels  47.7 us (33%)
  waiting for transfers between devices  46.7 us (33%)
  starting transfers between devices  40.8 us (29%)
  local copies, waits for them, and re-layouts  4.22 us (3%)
  other arithmetic  1.43 us (1%)
    ppermute x21, starting transfers between devices, shifted(): lax.ppermute(array, axis, [(i, (i + by) % size) for i in range(size)])  31.7 us
    ppermute x21, waiting for transfers between devices, shifted(): lax.ppermute(array, axis, [(i, (i + by) % size) for i in range(size)])  30.5 us
    pallas_call x3, Pallas kernels, attend(): pl.pallas_call(body, in_specs=[SM] * 3 + [HBM if own_first and n == 0 els...  30.3 us
    ppermute x17, waiting for transfers between devices, swapped(): lax.ppermute(array, axis, [(i, i ^ bit) for i in range(lax.axis_size(axis...  16.1 us
    ppermute x17, starting transfers between devices, swapped(): lax.ppermute(array, axis, [(i, i ^ bit) for i in range(lax.axis_size(axis...  9.19 us
    pallas_call x1, Pallas kernels, run_expert(): pl.pallas_call(body, grid=(steps,), in_specs=[SM] + [VM] * count + [pl.Bl...  9.06 us
    pallas_call x1, Pallas kernels, project(): pl.pallas_call(body, grid=(D // step,), in_specs=[VM] * len(arrays) + [pl...  6.31 us
    unnamed x40, local copies, waits for them, and re-layouts  3.49 us
  transfers between devices with their start and end apart: 38, of which 17 were waited for; matrix products, arithmetic and copies ran while one was open for 1% of the time, Pallas kernels for 21%

profile of v1, /device:TPU:0, one launch (start us, length us, event | category | flops | bytes accessed | tf_op | source)
XLA Modules:
  0.0 141.9 jit_solution(13130511813894880588)
XLA Ops:
  0.0 3.0 %collective-permute-start = (bf16[32,4096]{1,0:T(8,128)(2,1)}, bf16[32,4096]{1,0:T(8,128)(2,1)S(1)}, u32[]{:S(2)}, u32[]{:S(2)}) collective-permute-start(bf16[32,4096]{1,0:T(8,128)(2,1)} %refs_3_.1), channel_id=1, source_target_pairs={{0,1},{1,2},{2,3},{3,0},{4,5},{5,6},{6,7},{7,4},{8,9},{9,10},{10,1... | collective-permute-start | bytes 786440 | tf_op jit(solution)/shard_map/ppermute | solution.py:41
  3.0 2.0 %collective-permute-start.1 = (bf16[32,4096]{1,0:T(8,128)(2,1)}, bf16[32,4096]{1,0:T(8,128)(2,1)S(1)}, u32[]{:S(2)}, u32[]{:S(2)}) collective-permute-start(bf16[32,4096]{1,0:T(8,128)(2,1)} %refs_3_.1), channel_id=1, source_target_pairs={{0,3},{1,0},{2,1},{3,2},{4,7},{5,4},{6,5},{7,6},{8,11},{9,8},{10,9... | collective-permute-start | bytes 786440 | tf_op jit(solution)/shard_map/ppermute | solution.py:41
  5.8 8.8 %shard_map.127 = (bf16[1,32,1152]{2,1,0:T(8,128)(2,1)S(1)}, bf16[1,32,1152]{2,1,0:T(8,128)(2,1)S(1)}, bf16[1,32,1152]{2,1,0:T(8,128)(2,1)S(1)}, bf16[1,32,1152]{2,1,0:T(8,128)(2,1)S(1)}) custom-call(s32[2]{0:T(128)S(1)} %pad_add_fusion.refs_0_, s32[4]{0:T(128)S(1)} %and_select_fusion.refs_1_, s32[1]{0:T(128)} %bitcast.6.refs_2_, bf16[32,4096]{1,0:T(8,128)(2,1)} %refs_3_.1, ...), custom_call_target="tpu_custom_call" | custom-call | flops 17716740096 | bytes 8388608 | tf_op jit(solution)/shard_map/pallas_call | solution.py:219
  15.3 2.6 %collective-permute-start.3 = (bf16[1,32,1152]{2,1,0:T(8,128)(2,1)S(1)}, bf16[1,32,1152]{2,1,0:T(8,128)(2,1)S(1)}, u32[]{:S(2)}, u32[]{:S(2)}) collective-permute-start(bf16[1,32,1152]{2,1,0:T(8,128)(2,1)S(1)} %get-tuple-element.51), channel_id=1, source_target_pairs={{0,2},{1,3},{2,0},{3,1},{4,6},{5,7},{6,4},{7,5},{8,10},{9,11},{10,... | collective-permute-start | bytes 221192 | tf_op jit(solution)/shard_map/ppermute | solution.py:41
  17.9 1.3 collective-permute-start.4
  19.2 2.0 %collective-permute-start.6 = (bf16[32,4096]{1,0:T(8,128)(2,1)S(1)}, bf16[32,4096]{1,0:T(8,128)(2,1)S(1)}, u32[]{:S(2)}, u32[]{:S(2)}) collective-permute-start(bf16[32,4096]{1,0:T(8,128)(2,1)S(1)} %copy-done.19), channel_id=1, source_target_pairs={{0,2},{1,3},{2,0},{3,1},{4,6},{5,7},{6,4},{7,5},{8,10},{9,11},{10,... | collective-permute-start | bytes 786440 | tf_op jit(solution)/shard_map/ppermute | solution.py:41
  21.2 12.9 %shard_map.128 = (bf16[2,32,1152]{2,1,0:T(8,128)(2,1)S(1)}, bf16[2,32,1152]{2,1,0:T(8,128)(2,1)S(1)}, bf16[2,32,1152]{2,1,0:T(8,128)(2,1)S(1)}, bf16[2,32,1152]{2,1,0:T(8,128)(2,1)S(1)}) custom-call(s32[2]{0:T(128)S(1)} %pad_add_fusion.refs_0_, s32[4]{0:T(128)S(1)} %and_select_fusion.refs_1_, s32[2]{0:T(128)S(1)} %pad_add_fusion.1.refs_2_, ...), custom_call_target="tpu_custom_call" | custom-call | flops 35433480192 | bytes 8388608 | tf_op jit(solution)/shard_map/pallas_call | solution.py:219
  34.2 3.8 %collective-permute-start.8 = (bf16[2,32,1152]{2,1,0:T(8,128)(2,1)S(1)}, bf16[2,32,1152]{2,1,0:T(8,128)(2,1)S(1)}, u32[]{:S(2)}, u32[]{:S(2)}) collective-permute-start(bf16[2,32,1152]{2,1,0:T(8,128)(2,1)S(1)} %get-tuple-element.58), channel_id=1, source_target_pairs={{0,3},{1,0},{2,1},{3,2},{4,7},{5,4},{6,5},{7,6},{8,11},{9,8},{10,9... | collective-permute-start | bytes 442376 | tf_op jit(solution)/shard_map/ppermute | solution.py:41
  38.0 8.7 %shard_map.129 = (bf16[1,32,1152]{2,1,0:T(8,128)(2,1)S(1)}, bf16[1,32,1152]{2,1,0:T(8,128)(2,1)S(1)}, bf16[1,32,1152]{2,1,0:T(8,128)(2,1)S(1)}, bf16[1,32,1152]{2,1,0:T(8,128)(2,1)S(1)}) custom-call(s32[2]{0:T(128)S(1)} %pad_add_fusion.refs_0_, s32[4]{0:T(128)S(1)} %and_select_fusion.refs_1_, s32[1]{0:T(128)} %bitcast.refs_2_, ...), custom_call_target="tpu_custom_call" | custom-call | flops 17716740096 | bytes 8388608 | tf_op jit(solution)/shard_map/pallas_call | solution.py:219
  47.4 2.9 %collective-permute-start.7 = (bf16[1,32,1152]{2,1,0:T(8,128)(2,1)S(1)}, bf16[1,32,1152]{2,1,0:T(8,128)(2,1)S(1)}, u32[]{:S(2)}, u32[]{:S(2)}) collective-permute-start(bf16[1,32,1152]{2,1,0:T(8,128)(2,1)S(1)} %get-tuple-element.57), channel_id=1, source_target_pairs={{0,2},{1,3},{2,0},{3,1},{4,6},{5,7},{6,4},{7,5},{8,10},{9,11},{10,... | collective-permute-start | bytes 221192 | tf_op jit(solution)/shard_map/ppermute | solution.py:41
  50.3 2.0 %collective-permute-start.11 = (bf16[1,32,1152]{2,1,0:T(8,128)(2,1)S(1)}, bf16[1,32,1152]{2,1,0:T(8,128)(2,1)S(1)}, u32[]{:S(2)}, u32[]{:S(2)}) collective-permute-start(bf16[1,32,1152]{2,1,0:T(8,128)(2,1)S(1)} %get-tuple-element.65), channel_id=1, source_target_pairs={{0,1},{1,2},{2,3},{3,0},{4,5},{5,6},{6,7},{7,4},{8,9},{9,10},{10,1... | collective-permute-start | bytes 221192 | tf_op jit(solution)/shard_map/ppermute | solution.py:41
  52.4 1.1 collective-permute-done.7.refs_2_
  53.4 2.2 %collective-permute-done.10.refs_7_ = bf16[1,32,1152]{2,1,0:T(8,128)(2,1)S(1)} collective-permute-done((bf16[1,32,1152]{2,1,0:T(8,128)(2,1)S(1)}, bf16[1,32,1152]{2,1,0:T(8,128)(2,1)S(1)}, u32[]{:S(2)}, u32[]{:S(2)}) %collective-permute-start.10) | collective-permute-done | bytes 73760 | tf_op jit(solution)/shard_map/ppermute | solution.py:41
  55.6 1.7 %collective-permute-done.11.refs_10_ = bf16[1,32,1152]{2,1,0:T(8,128)(2,1)S(1)} collective-permute-done((bf16[1,32,1152]{2,1,0:T(8,128)(2,1)S(1)}, bf16[1,32,1152]{2,1,0:T(8,128)(2,1)S(1)}, u32[]{:S(2)}, u32[]{:S(2)}) %collective-permute-start.11) | collective-permute-done | bytes 73760 | tf_op jit(solution)/shard_map/ppermute | solution.py:41
  57.9 6.3 %project.1 = (bf16[32,2048]{1,0:T(8,128)(2,1)}, bf16[32,2048]{1,0:T(8,128)(2,1)}, bf16[32,2048]{1,0:T(8,128)(2,1)}, bf16[32,2048]{1,0:T(8,128)(2,1)}) custom-call(bf16[1,32,1152]{2,1,0:T(8,128)(2,1)} %copy-done.2, bf16[2,32,1152]{2,1,0:T(8,128)(2,1)} %copy-done.5, bf16[1,32,1152]{2,1,0:T(8,128)(2,1)} %copy-done.14, bf16[2,32,1152]{2,1,0:T(8,128)(2,1)} %copy-done.6, ...), custom_call_target="tpu_custom_call" | custom-call | tf_op jit(solution)/shard_map/project/pallas_call | solution.py:297
  64.4 2.2 %collective-permute-start.13 = (bf16[32,2048]{1,0:T(8,128)(2,1)}, bf16[32,2048]{1,0:T(8,128)(2,1)S(1)}, u32[]{:S(2)}, u32[]{:S(2)}) collective-permute-start(bf16[32,2048]{1,0:T(8,128)(2,1)} %get-tuple-element.69), channel_id=1, source_target_pairs={{0,2},{1,3},{2,0},{3,1},{4,6},{5,7},{6,4},{7,5},{8,10},{9,11},{10,... | collective-permute-start | bytes 393224 | tf_op jit(solution)/shard_map/ppermute | solution.py:41
  66.6 1.9 %collective-permute-start.14 = (bf16[32,2048]{1,0:T(8,128)(2,1)}, bf16[32,2048]{1,0:T(8,128)(2,1)S(1)}, u32[]{:S(2)}, u32[]{:S(2)}) collective-permute-start(bf16[32,2048]{1,0:T(8,128)(2,1)} %get-tuple-element.70), channel_id=1, source_target_pairs={{0,1},{1,2},{2,3},{3,0},{4,5},{5,6},{6,7},{7,4},{8,9},{9,10},{10,1... | collective-permute-start | bytes 393224 | tf_op jit(solution)/shard_map/ppermute | solution.py:41
  69.2 1.0 collective-permute-done.12.refs_1_
  70.2 9.2 %collective-permute-done.13.refs_2_ = bf16[32,2048]{1,0:T(8,128)(2,1)S(1)} collective-permute-done((bf16[32,2048]{1,0:T(8,128)(2,1)}, bf16[32,2048]{1,0:T(8,128)(2,1)S(1)}, u32[]{:S(2)}, u32[]{:S(2)}) %collective-permute-start.13) | collective-permute-done | bytes 131104 | tf_op jit(solution)/shard_map/ppermute | solution.py:41
  80.1 2.0 %normalize.1 = (f32[32,2048]{1,0:T(8,128)}, bf16[32,2176]{1,0:T(8,128)(2,1)}) custom-call(bf16[32,2048]{1,0:T(8,128)(2,1)} %residual_ref.1, bf16[32,2048]{1,0:T(8,128)(2,1)} %get-tuple-element.67.refs_0_, bf16[32,2048]{1,0:T(8,128)(2,1)} %copy-done.8, bf16[32,2048]{1,0:T(8,128)(2,1)} %copy-done.9, bf16[32,2048]{1,0:T(8,128)(2,1)} %copy-done.10, ...), custom_call_target="tpu_custom_call" | custom-call | tf_op jit(solution)/shard_map/normalize/pallas_call | solution.py:327
  82.2 1.2 collective-permute-start.21
  83.3 1.4 collective-permute-start.17
  84.7 0.6 collective-permute-start.16
  85.4 1.6 %collective-permute-start.15 = (bf16[32,2176]{1,0:T(8,128)(2,1)}, bf16[32,2176]{1,0:T(8,128)(2,1)S(1)}, u32[]{:S(2)}, u32[]{:S(2)}) collective-permute-start(bf16[32,2176]{1,0:T(8,128)(2,1)} %get-tuple-element.72.refs_3_), channel_id=1, source_target_pairs={{0,2},{1,3},{2,0},{3,1},{4,6},{5,7},{6,4},{7,5},{8,10},{9,11},{10,... | collective-permute-start | bytes 417800 | tf_op jit(solution)/shard_map/ppermute | solution.py:41
  87.0 1.0 collective-permute-done.21.refs_7_
  88.0 0.9 collective-permute-done.17.refs_2_
  88.9 0.8 collective-permute-start.20
  89.8 3.5 %collective-permute-done.16.refs_1_ = bf16[32,2176]{1,0:T(8,128)(2,1)S(1)} collective-permute-done((bf16[32,2176]{1,0:T(8,128)(2,1)}, bf16[32,2176]{1,0:T(8,128)(2,1)S(1)}, u32[]{:S(2)}, u32[]{:S(2)}) %collective-permute-start.16) | collective-permute-done | bytes 139296 | tf_op jit(solution)/shard_map/ppermute | solution.py:41
  93.3 1.1 collective-permute-start.19
  94.4 3.8 %collective-permute-done.15.refs_0_ = bf16[32,2176]{1,0:T(8,128)(2,1)S(1)} collective-permute-done((bf16[32,2176]{1,0:T(8,128)(2,1)}, bf16[32,2176]{1,0:T(8,128)(2,1)S(1)}, u32[]{:S(2)}, u32[]{:S(2)}) %collective-permute-start.15) | collective-permute-done | bytes 139296 | tf_op jit(solution)/shard_map/ppermute | solution.py:41
  98.2 0.7 collective-permute-start.18
  100.0 3.4 %collective-permute-done.18.refs_4_ = bf16[32,2176]{1,0:T(8,128)(2,1)S(1)} collective-permute-done((bf16[32,2176]{1,0:T(8,128)(2,1)S(1)}, bf16[32,2176]{1,0:T(8,128)(2,1)S(1)}, u32[]{:S(2)}, u32[]{:S(2)}) %collective-permute-start.18) | collective-permute-done | bytes 139296 | tf_op jit(solution)/shard_map/ppermute | solution.py:45
  103.4 1.3 collective-permute-done.26.refs_12_
  104.7 0.9 copy-done.1
  105.6 9.1 %run_expert.1 = (f32[256,2048]{1,0:T(8,128)S(1)}, bf16[256,2048]{1,0:T(8,128)(2,1)S(1)}) custom-call(s32[1]{0:T(128)} %bitcast.11.expert_ref, bf16[32,2176]{1,0:T(8,128)(2,1)S(1)} %collective-permute-done.15.refs_0_, bf16[32,2176]{1,0:T(8,128)(2,1)S(1)} %collective-permute-done.16.refs_1_, bf16[32,2176]{1,0:T(8,128)(2,1)S(1)} %collective-permute-done.17.refs_2_, ...), custom_call_target="tpu_custom_call" | custom-call | tf_op jit(solution)/shard_map/run_expert/pallas_call | solution.py:385
  114.9 2.5 %collective-permute-done.30 = bf16[256,2048]{1,0:T(8,128)(2,1)S(1)} collective-permute-done((bf16[256,2048]{1,0:T(8,128)(2,1)S(1)}, bf16[256,2048]{1,0:T(8,128)(2,1)S(1)}, u32[]{:S(2)}, u32[]{:S(2)}) %collective-permute-start.30) | collective-permute-done | bytes 1048608 | tf_op jit(solution)/shard_map/ppermute | solution.py:45
  117.9 1.0 collective-permute-start.31
  118.9 1.1 collective-permute-start.35
  120.0 1.0 collective-permute-start.33
  120.9 1.1 collective-permute-start.37
  122.0 2.3 %collective-permute-done.31 = bf16[32,2048]{1,0:T(8,128)(2,1)S(1)} collective-permute-done((bf16[32,2048]{1,0:T(8,128)(2,1)S(1)}, bf16[32,2048]{1,0:T(8,128)(2,1)S(1)}, u32[]{:S(2)}, u32[]{:S(2)}) %collective-permute-start.31) | collective-permute-done | bytes 131104 | tf_op jit(solution)/shard_map/ppermute | solution.py:45
  124.3 2.8 %collective-permute-done.35 = bf16[32,2048]{1,0:T(8,128)(2,1)S(1)} collective-permute-done((bf16[32,2048]{1,0:T(8,128)(2,1)S(1)}, bf16[32,2048]{1,0:T(8,128)(2,1)S(1)}, u32[]{:S(2)}, u32[]{:S(2)}) %collective-permute-start.35) | collective-permute-done | bytes 131104 | tf_op jit(solution)/shard_map/ppermute | solution.py:45
  127.1 2.8 %collective-permute-done.33 = bf16[32,2048]{1,0:T(8,128)(2,1)S(1)} collective-permute-done((bf16[32,2048]{1,0:T(8,128)(2,1)S(1)}, bf16[32,2048]{1,0:T(8,128)(2,1)S(1)}, u32[]{:S(2)}, u32[]{:S(2)}) %collective-permute-start.33) | collective-permute-done | bytes 131104 | tf_op jit(solution)/shard_map/ppermute | solution.py:45
  130.1 2.4 %collective-permute-start.36 = (bf16[32,2048]{1,0:T(8,128)(2,1)S(1)}, bf16[32,2048]{1,0:T(8,128)(2,1)S(1)}, u32[]{:S(2)}, u32[]{:S(2)}) collective-permute-start(bf16[32,2048]{1,0:T(8,128)(2,1)S(1)} %get-tuple-element.78), channel_id=1, source_target_pairs={{0,1},{1,2},{2,3},{3,0},{4,5},{5,6},{6,7},{7,4},{8,9},{9,10},{10,1... | collective-permute-start | bytes 393224 | tf_op jit(solution)/shard_map/ppermute | solution.py:41
  132.4 1.5 %collective-permute-start.34 = (bf16[32,2048]{1,0:T(8,128)(2,1)S(1)}, bf16[32,2048]{1,0:T(8,128)(2,1)S(1)}, u32[]{:S(2)}, u32[]{:S(2)}) collective-permute-start(bf16[32,2048]{1,0:T(8,128)(2,1)S(1)} %get-tuple-element.79), channel_id=1, source_target_pairs={{0,3},{1,0},{2,1},{3,2},{4,7},{5,4},{6,5},{7,6},{8,11},{9,8},{10,9... | collective-permute-start | bytes 393224 | tf_op jit(solution)/shard_map/ppermute | solution.py:41
  134.0 6.2 %collective-permute-done.32 = bf16[32,2048]{1,0:T(8,128)(2,1)S(1)} collective-permute-done((bf16[32,2048]{1,0:T(8,128)(2,1)S(1)}, bf16[32,2048]{1,0:T(8,128)(2,1)S(1)}, u32[]{:S(2)}, u32[]{:S(2)}) %collective-permute-start.32) | collective-permute-done | bytes 131104 | tf_op jit(solution)/shard_map/ppermute | solution.py:41
  140.1 1.0 collective-permute-done.34
  141.1 0.8 fusion.2
  (85 shorter events, 5.6 us)
Async XLA Ops:
  0.0 19.2 %collective-permute-start = (bf16[32,4096]{1,0:T(8,128)(2,1)}, bf16[32,4096]{1,0:T(8,128)(2,1)S(1)}, u32[]{:S(2)}, u32[]{:S(2)}) collective-permute-start(bf16[32,4096]{1,0:T(8,128)(2,1)} %refs_3_.1), channel_id=1, source_target_pairs={{0,1},{1,2},{2,3},{3,0},{4,5},{5,6},{6,7},{7,4},{8,9},{9,10},{10,1... | collective-permute-start | bytes 786440 | tf_op jit(solution)/shard_map/ppermute | solution.py:41
  3.0 16.2 %collective-permute-start.1 = (bf16[32,4096]{1,0:T(8,128)(2,1)}, bf16[32,4096]{1,0:T(8,128)(2,1)S(1)}, u32[]{:S(2)}, u32[]{:S(2)}) collective-permute-start(bf16[32,4096]{1,0:T(8,128)(2,1)} %refs_3_.1), channel_id=1, source_target_pairs={{0,3},{1,0},{2,1},{3,2},{4,7},{5,4},{6,5},{7,6},{8,11},{9,8},{10,9... | collective-permute-start | bytes 786440 | tf_op jit(solution)/shard_map/ppermute | solution.py:41
  5.8 13.4 %copy-start.19 = (bf16[32,4096]{1,0:T(8,128)(2,1)S(1)}, bf16[32,4096]{1,0:T(8,128)(2,1)}, u32[]{:S(2)}) copy-start(bf16[32,4096]{1,0:T(8,128)(2,1)} %refs_3_.1) | copy-start | bytes 786436
  15.3 18.8 %collective-permute-start.2 = (bf16[1,32,1152]{2,1,0:T(8,128)(2,1)S(1)}, bf16[1,32,1152]{2,1,0:T(8,128)(2,1)S(1)}, u32[]{:S(2)}, u32[]{:S(2)}) collective-permute-start(bf16[1,32,1152]{2,1,0:T(8,128)(2,1)S(1)} %get-tuple-element.50), channel_id=1, source_target_pairs={{0,1},{1,2},{2,3},{3,0},{4,5},{5,6},{6,7},{7,4},{8,9},{9,10},{10,1... | collective-permute-start | bytes 221192 | tf_op jit(solution)/shard_map/ppermute | solution.py:41
  15.3 18.8 %collective-permute-start.3 = (bf16[1,32,1152]{2,1,0:T(8,128)(2,1)S(1)}, bf16[1,32,1152]{2,1,0:T(8,128)(2,1)S(1)}, u32[]{:S(2)}, u32[]{:S(2)}) collective-permute-start(bf16[1,32,1152]{2,1,0:T(8,128)(2,1)S(1)} %get-tuple-element.51), channel_id=1, source_target_pairs={{0,2},{1,3},{2,0},{3,1},{4,6},{5,7},{6,4},{7,5},{8,10},{9,11},{10,... | collective-permute-start | bytes 221192 | tf_op jit(solution)/shard_map/ppermute | solution.py:41
  17.9 16.3 %collective-permute-start.4 = (bf16[1,32,1152]{2,1,0:T(8,128)(2,1)S(1)}, bf16[1,32,1152]{2,1,0:T(8,128)(2,1)S(1)}, u32[]{:S(2)}, u32[]{:S(2)}) collective-permute-start(bf16[1,32,1152]{2,1,0:T(8,128)(2,1)S(1)} %get-tuple-element.52), channel_id=1, source_target_pairs={{0,3},{1,0},{2,1},{3,2},{4,7},{5,4},{6,5},{7,6},{8,11},{9,8},{10,9... | collective-permute-start | bytes 221192 | tf_op jit(solution)/shard_map/ppermute | solution.py:41
  19.2 18.8 %collective-permute-start.6 = (bf16[32,4096]{1,0:T(8,128)(2,1)S(1)}, bf16[32,4096]{1,0:T(8,128)(2,1)S(1)}, u32[]{:S(2)}, u32[]{:S(2)}) collective-permute-start(bf16[32,4096]{1,0:T(8,128)(2,1)S(1)} %copy-done.19), channel_id=1, source_target_pairs={{0,2},{1,3},{2,0},{3,1},{4,6},{5,7},{6,4},{7,5},{8,10},{9,11},{10,... | collective-permute-start | bytes 786440 | tf_op jit(solution)/shard_map/ppermute | solution.py:41
  34.1 12.6 %copy-start = (bf16[2,32,1152]{2,1,0:T(8,128)(2,1)}, bf16[2,32,1152]{2,1,0:T(8,128)(2,1)S(1)}, u32[]{:S(2)}) copy-start(bf16[2,32,1152]{2,1,0:T(8,128)(2,1)S(1)} %get-tuple-element.59.refs_4_) | copy-start | bytes 442372
  34.1 12.6 %copy-start.11 = (bf16[1,32,1152]{2,1,0:T(8,128)(2,1)}, bf16[1,32,1152]{2,1,0:T(8,128)(2,1)S(1)}, u32[]{:S(2)}) copy-start(bf16[1,32,1152]{2,1,0:T(8,128)(2,1)S(1)} %collective-permute-done.2.refs_5_) | copy-start | bytes 221188
  34.1 12.6 %copy-start.12 = (bf16[1,32,1152]{2,1,0:T(8,128)(2,1)}, bf16[1,32,1152]{2,1,0:T(8,128)(2,1)S(1)}, u32[]{:S(2)}) copy-start(bf16[1,32,1152]{2,1,0:T(8,128)(2,1)S(1)} %collective-permute-done.3.refs_9_) | copy-start | bytes 221188
  34.1 12.6 %copy-start.13 = (bf16[1,32,1152]{2,1,0:T(8,128)(2,1)}, bf16[1,32,1152]{2,1,0:T(8,128)(2,1)S(1)}, u32[]{:S(2)}) copy-start(bf16[1,32,1152]{2,1,0:T(8,128)(2,1)S(1)} %collective-permute-done.4.refs_11_) | copy-start | bytes 221188
  34.1 16.2 %collective-permute-start.5 = (bf16[2,32,1152]{2,1,0:T(8,128)(2,1)S(1)}, bf16[2,32,1152]{2,1,0:T(8,128)(2,1)S(1)}, u32[]{:S(2)}, u32[]{:S(2)}) collective-permute-start(bf16[2,32,1152]{2,1,0:T(8,128)(2,1)S(1)} %get-tuple-element.54), channel_id=1, source_target_pairs={{0,1},{1,2},{2,3},{3,0},{4,5},{5,6},{6,7},{7,4},{8,9},{9,10},{10,1... | collective-permute-start | bytes 442376 | tf_op jit(solution)/shard_map/ppermute | solution.py:41
  34.2 18.1 %collective-permute-start.8 = (bf16[2,32,1152]{2,1,0:T(8,128)(2,1)S(1)}, bf16[2,32,1152]{2,1,0:T(8,128)(2,1)S(1)}, u32[]{:S(2)}, u32[]{:S(2)}) collective-permute-start(bf16[2,32,1152]{2,1,0:T(8,128)(2,1)S(1)} %get-tuple-element.58), channel_id=1, source_target_pairs={{0,3},{1,0},{2,1},{3,2},{4,7},{5,4},{6,5},{7,6},{8,11},{9,8},{10,9... | collective-permute-start | bytes 442376 | tf_op jit(solution)/shard_map/ppermute | solution.py:41
  38.0 14.3 %collective-permute-start.9 = (bf16[2,32,1152]{2,1,0:T(8,128)(2,1)S(1)}, bf16[2,32,1152]{2,1,0:T(8,128)(2,1)S(1)}, u32[]{:S(2)}, u32[]{:S(2)}) collective-permute-start(bf16[2,32,1152]{2,1,0:T(8,128)(2,1)S(1)} %get-tuple-element.61), channel_id=1, source_target_pairs={{0,2},{1,3},{2,0},{3,1},{4,6},{5,7},{6,4},{7,5},{8,10},{9,11},{10,... | collective-permute-start | bytes 442376 | tf_op jit(solution)/shard_map/ppermute | solution.py:41
  47.4 6.0 %collective-permute-start.7 = (bf16[1,32,1152]{2,1,0:T(8,128)(2,1)S(1)}, bf16[1,32,1152]{2,1,0:T(8,128)(2,1)S(1)}, u32[]{:S(2)}, u32[]{:S(2)}) collective-permute-start(bf16[1,32,1152]{2,1,0:T(8,128)(2,1)S(1)} %get-tuple-element.57), channel_id=1, source_target_pairs={{0,2},{1,3},{2,0},{3,1},{4,6},{5,7},{6,4},{7,5},{8,10},{9,11},{10,... | collective-permute-start | bytes 221192 | tf_op jit(solution)/shard_map/ppermute | solution.py:41
  50.3 5.3 %collective-permute-start.10 = (bf16[1,32,1152]{2,1,0:T(8,128)(2,1)S(1)}, bf16[1,32,1152]{2,1,0:T(8,128)(2,1)S(1)}, u32[]{:S(2)}, u32[]{:S(2)}) collective-permute-start(bf16[1,32,1152]{2,1,0:T(8,128)(2,1)S(1)} %get-tuple-element.62), channel_id=1, source_target_pairs={{0,3},{1,0},{2,1},{3,2},{4,7},{5,4},{6,5},{7,6},{8,11},{9,8},{10,9... | collective-permute-start | bytes 221192 | tf_op jit(solution)/shard_map/ppermute | solution.py:41
  50.3 7.0 %copy-start.5 = (bf16[2,32,1152]{2,1,0:T(8,128)(2,1)}, bf16[2,32,1152]{2,1,0:T(8,128)(2,1)S(1)}, u32[]{:S(2)}) copy-start(bf16[2,32,1152]{2,1,0:T(8,128)(2,1)S(1)} %collective-permute-done.5.refs_1_) | copy-start | bytes 442372
  50.3 7.0 %collective-permute-start.11 = (bf16[1,32,1152]{2,1,0:T(8,128)(2,1)S(1)}, bf16[1,32,1152]{2,1,0:T(8,128)(2,1)S(1)}, u32[]{:S(2)}, u32[]{:S(2)}) collective-permute-start(bf16[1,32,1152]{2,1,0:T(8,128)(2,1)S(1)} %get-tuple-element.65), channel_id=1, source_target_pairs={{0,1},{1,2},{2,3},{3,0},{4,5},{5,6},{6,7},{7,4},{8,9},{9,10},{10,1... | collective-permute-start | bytes 221192 | tf_op jit(solution)/shard_map/ppermute | solution.py:41
  57.9 10.6 %copy-start.17 = (f32[32,8]{0,1:T(8,128)S(1)}, f32[32,8]{0,1:T(8,128)}, u32[]{:S(2)}) copy-start(f32[32,8]{0,1:T(8,128)} %param.25) | copy-start | bytes 3076
  57.9 10.6 %copy-start.18 = (s32[32,8]{0,1:T(8,128)S(1)}, s32[32,8]{0,1:T(8,128)}, u32[]{:S(2)}) copy-start(s32[32,8]{0,1:T(8,128)} %param.24) | copy-start | bytes 3076
  64.2 5.9 %collective-permute-start.12 = (bf16[32,2048]{1,0:T(8,128)(2,1)}, bf16[32,2048]{1,0:T(8,128)(2,1)S(1)}, u32[]{:S(2)}, u32[]{:S(2)}) collective-permute-start(bf16[32,2048]{1,0:T(8,128)(2,1)} %get-tuple-element.68), channel_id=1, source_target_pairs={{0,3},{1,0},{2,1},{3,2},{4,7},{5,4},{6,5},{7,6},{8,11},{9,8},{10,9... | collective-permute-start | bytes 393224 | tf_op jit(solution)/shard_map/ppermute | solution.py:41
  64.4 15.0 %collective-permute-start.13 = (bf16[32,2048]{1,0:T(8,128)(2,1)}, bf16[32,2048]{1,0:T(8,128)(2,1)S(1)}, u32[]{:S(2)}, u32[]{:S(2)}) collective-permute-start(bf16[32,2048]{1,0:T(8,128)(2,1)} %get-tuple-element.69), channel_id=1, source_target_pairs={{0,2},{1,3},{2,0},{3,1},{4,6},{5,7},{6,4},{7,5},{8,10},{9,11},{10,... | collective-permute-start | bytes 393224 | tf_op jit(solution)/shard_map/ppermute | solution.py:41
  66.6 12.8 %collective-permute-start.14 = (bf16[32,2048]{1,0:T(8,128)(2,1)}, bf16[32,2048]{1,0:T(8,128)(2,1)S(1)}, u32[]{:S(2)}, u32[]{:S(2)}) collective-permute-start(bf16[32,2048]{1,0:T(8,128)(2,1)} %get-tuple-element.70), channel_id=1, source_target_pairs={{0,1},{1,2},{2,3},{3,0},{4,5},{5,6},{6,7},{7,4},{8,9},{9,10},{10,1... | collective-permute-start | bytes 393224 | tf_op jit(solution)/shard_map/ppermute | solution.py:41
  70.2 9.2 %copy-start.8 = (bf16[32,2048]{1,0:T(8,128)(2,1)}, bf16[32,2048]{1,0:T(8,128)(2,1)S(1)}, u32[]{:S(2)}) copy-start(bf16[32,2048]{1,0:T(8,128)(2,1)S(1)} %collective-permute-done.12.refs_1_) | copy-start | bytes 393220
  82.2 5.8 %collective-permute-start.21 = (bf16[32,2176]{1,0:T(8,128)(2,1)}, bf16[32,2176]{1,0:T(8,128)(2,1)S(1)}, u32[]{:S(2)}, u32[]{:S(2)}) collective-permute-start(bf16[32,2176]{1,0:T(8,128)(2,1)} %get-tuple-element.72.refs_3_), channel_id=1, source_target_pairs={{0,8},{4,12},{8,0},{12,4},{1,9},{5,13},{9,1},{13,5},{2,10},{6,14},... | collective-permute-start | bytes 417800 | tf_op jit(solution)/shard_map/ppermute | solution.py:45
  83.3 5.6 %collective-permute-start.17 = (bf16[32,2176]{1,0:T(8,128)(2,1)}, bf16[32,2176]{1,0:T(8,128)(2,1)S(1)}, u32[]{:S(2)}, u32[]{:S(2)}) collective-permute-start(bf16[32,2176]{1,0:T(8,128)(2,1)} %get-tuple-element.72.refs_3_), channel_id=1, source_target_pairs={{0,3},{1,0},{2,1},{3,2},{4,7},{5,4},{6,5},{7,6},{8,11},{9,8},{10,9... | collective-permute-start | bytes 417800 | tf_op jit(solution)/shard_map/ppermute | solution.py:41
  84.7 4.2 %collective-permute-start.25 = (bf16[32,2176]{1,0:T(8,128)(2,1)}, bf16[32,2176]{1,0:T(8,128)(2,1)S(1)}, u32[]{:S(2)}, u32[]{:S(2)}) collective-permute-start(bf16[32,2176]{1,0:T(8,128)(2,1)} %get-tuple-element.72.refs_3_), channel_id=1, source_target_pairs={{0,4},{4,0},{8,12},{12,8},{1,5},{5,1},{9,13},{13,9},{2,6},{6,2},{1... | collective-permute-start | bytes 417800 | tf_op jit(solution)/shard_map/ppermute | solution.py:45
  84.7 8.6 %collective-permute-start.16 = (bf16[32,2176]{1,0:T(8,128)(2,1)}, bf16[32,2176]{1,0:T(8,128)(2,1)S(1)}, u32[]{:S(2)}, u32[]{:S(2)}) collective-permute-start(bf16[32,2176]{1,0:T(8,128)(2,1)} %get-tuple-element.72.refs_3_), channel_id=1, source_target_pairs={{0,1},{1,2},{2,3},{3,0},{4,5},{5,6},{6,7},{7,4},{8,9},{9,10},{10,1... | collective-permute-start | bytes 417800 | tf_op jit(solution)/shard_map/ppermute | solution.py:41
  85.4 12.9 %collective-permute-start.15 = (bf16[32,2176]{1,0:T(8,128)(2,1)}, bf16[32,2176]{1,0:T(8,128)(2,1)S(1)}, u32[]{:S(2)}, u32[]{:S(2)}) collective-permute-start(bf16[32,2176]{1,0:T(8,128)(2,1)} %get-tuple-element.72.refs_3_), channel_id=1, source_target_pairs={{0,2},{1,3},{2,0},{3,1},{4,6},{5,7},{6,4},{7,5},{8,10},{9,11},{10,... | collective-permute-start | bytes 417800 | tf_op jit(solution)/shard_map/ppermute | solution.py:41
  88.0 10.9 %collective-permute-start.29 = (bf16[32,2176]{1,0:T(8,128)(2,1)S(1)}, bf16[32,2176]{1,0:T(8,128)(2,1)S(1)}, u32[]{:S(2)}, u32[]{:S(2)}) collective-permute-start(bf16[32,2176]{1,0:T(8,128)(2,1)S(1)} %collective-permute-done.21.refs_7_), channel_id=1, source_target_pairs={{0,4},{4,0},{8,12},{12,8},{1,5},{5,1},{9,13},{13,9},{2,6},{6,2},{1... | collective-permute-start | bytes 417800 | tf_op jit(solution)/shard_map/ppermute | solution.py:45
  88.9 10.0 %collective-permute-start.24 = (bf16[32,2176]{1,0:T(8,128)(2,1)S(1)}, bf16[32,2176]{1,0:T(8,128)(2,1)S(1)}, u32[]{:S(2)}, u32[]{:S(2)}) collective-permute-start(bf16[32,2176]{1,0:T(8,128)(2,1)S(1)} %collective-permute-done.17.refs_2_), channel_id=1, source_target_pairs={{0,4},{4,0},{8,12},{12,8},{1,5},{5,1},{9,13},{13,9},{2,6},{6,2},{1... | collective-permute-start | bytes 417800 | tf_op jit(solution)/shard_map/ppermute | solution.py:45
  88.9 10.5 %collective-permute-start.20 = (bf16[32,2176]{1,0:T(8,128)(2,1)S(1)}, bf16[32,2176]{1,0:T(8,128)(2,1)S(1)}, u32[]{:S(2)}, u32[]{:S(2)}) collective-permute-start(bf16[32,2176]{1,0:T(8,128)(2,1)S(1)} %collective-permute-done.17.refs_2_), channel_id=1, source_target_pairs={{0,8},{4,12},{8,0},{12,4},{1,9},{5,13},{9,1},{13,5},{2,10},{6,14},... | collective-permute-start | bytes 417800 | tf_op jit(solution)/shard_map/ppermute | solution.py:45
  93.3 6.2 %collective-permute-start.19 = (bf16[32,2176]{1,0:T(8,128)(2,1)S(1)}, bf16[32,2176]{1,0:T(8,128)(2,1)S(1)}, u32[]{:S(2)}, u32[]{:S(2)}) collective-permute-start(bf16[32,2176]{1,0:T(8,128)(2,1)S(1)} %collective-permute-done.16.refs_1_), channel_id=1, source_target_pairs={{0,8},{4,12},{8,0},{12,4},{1,9},{5,13},{9,1},{13,5},{2,10},{6,14},... | collective-permute-start | bytes 417800 | tf_op jit(solution)/shard_map/ppermute | solution.py:45
  98.2 5.1 %collective-permute-start.18 = (bf16[32,2176]{1,0:T(8,128)(2,1)S(1)}, bf16[32,2176]{1,0:T(8,128)(2,1)S(1)}, u32[]{:S(2)}, u32[]{:S(2)}) collective-permute-start(bf16[32,2176]{1,0:T(8,128)(2,1)S(1)} %collective-permute-done.15.refs_0_), channel_id=1, source_target_pairs={{0,8},{4,12},{8,0},{12,4},{1,9},{5,13},{9,1},{13,5},{2,10},{6,14},... | collective-permute-start | bytes 417800 | tf_op jit(solution)/shard_map/ppermute | solution.py:45
  98.9 4.4 %collective-permute-start.23 = (bf16[32,2176]{1,0:T(8,128)(2,1)S(1)}, bf16[32,2176]{1,0:T(8,128)(2,1)S(1)}, u32[]{:S(2)}, u32[]{:S(2)}) collective-permute-start(bf16[32,2176]{1,0:T(8,128)(2,1)S(1)} %collective-permute-done.16.refs_1_), channel_id=1, source_target_pairs={{0,4},{4,0},{8,12},{12,8},{1,5},{5,1},{9,13},{13,9},{2,6},{6,2},{1... | collective-permute-start | bytes 417800 | tf_op jit(solution)/shard_map/ppermute | solution.py:45
  99.0 4.4 %collective-permute-start.22 = (bf16[32,2176]{1,0:T(8,128)(2,1)S(1)}, bf16[32,2176]{1,0:T(8,128)(2,1)S(1)}, u32[]{:S(2)}, u32[]{:S(2)}) collective-permute-start(bf16[32,2176]{1,0:T(8,128)(2,1)S(1)} %collective-permute-done.15.refs_0_), channel_id=1, source_target_pairs={{0,4},{4,0},{8,12},{12,8},{1,5},{5,1},{9,13},{13,9},{2,6},{6,2},{1... | collective-permute-start | bytes 417800 | tf_op jit(solution)/shard_map/ppermute | solution.py:45
  99.5 3.9 %collective-permute-start.28 = (bf16[32,2176]{1,0:T(8,128)(2,1)S(1)}, bf16[32,2176]{1,0:T(8,128)(2,1)S(1)}, u32[]{:S(2)}, u32[]{:S(2)}) collective-permute-start(bf16[32,2176]{1,0:T(8,128)(2,1)S(1)} %collective-permute-done.20.refs_6_), channel_id=1, source_target_pairs={{0,4},{4,0},{8,12},{12,8},{1,5},{5,1},{9,13},{13,9},{2,6},{6,2},{1... | collective-permute-start | bytes 417800 | tf_op jit(solution)/shard_map/ppermute | solution.py:45
  99.5 3.8 %collective-permute-start.27 = (bf16[32,2176]{1,0:T(8,128)(2,1)S(1)}, bf16[32,2176]{1,0:T(8,128)(2,1)S(1)}, u32[]{:S(2)}, u32[]{:S(2)}) collective-permute-start(bf16[32,2176]{1,0:T(8,128)(2,1)S(1)} %collective-permute-done.19.refs_5_), channel_id=1, source_target_pairs={{0,4},{4,0},{8,12},{12,8},{1,5},{5,1},{9,13},{13,9},{2,6},{6,2},{1... | collective-permute-start | bytes 417800 | tf_op jit(solution)/shard_map/ppermute | solution.py:45
  103.3 1.4 collective-permute-start.26
  114.7 2.7 %collective-permute-start.30 = (bf16[256,2048]{1,0:T(8,128)(2,1)S(1)}, bf16[256,2048]{1,0:T(8,128)(2,1)S(1)}, u32[]{:S(2)}, u32[]{:S(2)}) collective-permute-start(bf16[256,2048]{1,0:T(8,128)(2,1)S(1)} %get-tuple-element.74), channel_id=1, source_target_pairs={{0,4},{4,0},{8,12},{12,8},{1,5},{5,1},{9,13},{13,9},{2,6},{6,2},{1... | collective-permute-start | bytes 3145736 | tf_op jit(solution)/shard_map/ppermute | solution.py:45
  117.8 23.3 %copy-start.4 = (f32[32,2048]{1,0:T(8,128)S(1)}, f32[32,2048]{1,0:T(8,128)}, u32[]{:S(2)}) copy-start(f32[32,2048]{1,0:T(8,128)} %get-tuple-element.71) | copy-start | bytes 786436
  117.9 6.4 %collective-permute-start.31 = (bf16[32,2048]{1,0:T(8,128)(2,1)S(1)}, bf16[32,2048]{1,0:T(8,128)(2,1)S(1)}, u32[]{:S(2)}, u32[]{:S(2)}) collective-permute-start(bf16[32,2048]{1,0:T(8,128)(2,1)S(1)} %get-tuple-element.80), channel_id=1, source_target_pairs={{0,8},{4,12},{8,0},{12,4},{1,9},{5,13},{9,1},{13,5},{2,10},{6,14},... | collective-permute-start | bytes 393224 | tf_op jit(solution)/shard_map/ppermute | solution.py:45
  118.9 8.2 %collective-permute-start.35 = (bf16[32,2048]{1,0:T(8,128)(2,1)S(1)}, bf16[32,2048]{1,0:T(8,128)(2,1)S(1)}, u32[]{:S(2)}, u32[]{:S(2)}) collective-permute-start(bf16[32,2048]{1,0:T(8,128)(2,1)S(1)} %get-tuple-element.82), channel_id=1, source_target_pairs={{0,8},{4,12},{8,0},{12,4},{1,9},{5,13},{9,1},{13,5},{2,10},{6,14},... | collective-permute-start | bytes 393224 | tf_op jit(solution)/shard_map/ppermute | solution.py:45
  120.0 9.9 %collective-permute-start.33 = (bf16[32,2048]{1,0:T(8,128)(2,1)S(1)}, bf16[32,2048]{1,0:T(8,128)(2,1)S(1)}, u32[]{:S(2)}, u32[]{:S(2)}) collective-permute-start(bf16[32,2048]{1,0:T(8,128)(2,1)S(1)} %get-tuple-element.83), channel_id=1, source_target_pairs={{0,8},{4,12},{8,0},{12,4},{1,9},{5,13},{9,1},{13,5},{2,10},{6,14},... | collective-permute-start | bytes 393224 | tf_op jit(solution)/shard_map/ppermute | solution.py:45
  120.9 13.0 %collective-permute-start.37 = (bf16[32,2048]{1,0:T(8,128)(2,1)S(1)}, bf16[32,2048]{1,0:T(8,128)(2,1)S(1)}, u32[]{:S(2)}, u32[]{:S(2)}) collective-permute-start(bf16[32,2048]{1,0:T(8,128)(2,1)S(1)} %get-tuple-element.81), channel_id=1, source_target_pairs={{0,8},{4,12},{8,0},{12,4},{1,9},{5,13},{9,1},{13,5},{2,10},{6,14},... | collective-permute-start | bytes 393224 | tf_op jit(solution)/shard_map/ppermute | solution.py:45
  130.0 10.1 %collective-permute-start.32 = (bf16[32,2048]{1,0:T(8,128)(2,1)S(1)}, bf16[32,2048]{1,0:T(8,128)(2,1)S(1)}, u32[]{:S(2)}, u32[]{:S(2)}) collective-permute-start(bf16[32,2048]{1,0:T(8,128)(2,1)S(1)} %get-tuple-element.77), channel_id=1, source_target_pairs={{0,2},{1,3},{2,0},{3,1},{4,6},{5,7},{6,4},{7,5},{8,10},{9,11},{10,... | collective-permute-start | bytes 393224 | tf_op jit(solution)/shard_map/ppermute | solution.py:41
  130.1 10.0 %collective-permute-start.36 = (bf16[32,2048]{1,0:T(8,128)(2,1)S(1)}, bf16[32,2048]{1,0:T(8,128)(2,1)S(1)}, u32[]{:S(2)}, u32[]{:S(2)}) collective-permute-start(bf16[32,2048]{1,0:T(8,128)(2,1)S(1)} %get-tuple-element.78), channel_id=1, source_target_pairs={{0,1},{1,2},{2,3},{3,0},{4,5},{5,6},{6,7},{7,4},{8,9},{9,10},{10,1... | collective-permute-start | bytes 393224 | tf_op jit(solution)/shard_map/ppermute | solution.py:41
  132.4 8.6 %collective-permute-start.34 = (bf16[32,2048]{1,0:T(8,128)(2,1)S(1)}, bf16[32,2048]{1,0:T(8,128)(2,1)S(1)}, u32[]{:S(2)}, u32[]{:S(2)}) collective-permute-start(bf16[32,2048]{1,0:T(8,128)(2,1)S(1)} %get-tuple-element.79), channel_id=1, source_target_pairs={{0,3},{1,0},{2,1},{3,2},{4,7},{5,4},{6,5},{7,6},{8,11},{9,8},{10,9... | collective-permute-start | bytes 393224 | tf_op jit(solution)/shard_map/ppermute | solution.py:41
  (10 other events, 19.7 us)

commit v2 on v1

--- a/solution.py
+++ b/solution.py
@@ -21,7 +21,6 @@
 norm_epsilon = 1e-06
 score_scale = math.log2(math.e) * HD**-0.5
 key_step = 512
-row_step = 256
 f32 = jnp.float32
 bf16 = jnp.bfloat16
 
@@ -116,24 +115,11 @@
         if own_first:
             own_copy.wait()
 
-        def replace_unfilled(ref, i, filler):
-            @pl.when(filled < cached)
-            def _():
-                def one(block, carry):
-                    at = pl.ds(pl.multiple_of(block * row_step, row_step), row_step)
-                    inside = lax.broadcasted_iota(jnp.int32, (row_step, HD), 0) + block * row_step < filled
-                    ref[i, at] = jnp.where(inside, ref[i, at], filler)
-                    return carry
-
-                lax.fori_loop(filled // row_step, cached // row_step, one, 0)
-
         def arrive_keys(i):
             key_copy(i).wait()
-            replace_unfilled(keys_in, i, jnp.broadcast_to(keys_in[i, :1], (row_step, HD)))
 
         def arrive_values(i):
             value_copy(i).wait()
-            replace_unfilled(values_in, i, jnp.zeros((row_step, HD), bf16))
 
         def fill_scores(i, slot):
             out = score_refs[slot]
@@ -143,8 +129,10 @@
             high = stacked.astype(bf16)
             both = jnp.concatenate([high, (stacked - high.astype(f32)).astype(bf16)], 1)
             running = None
+            first = jnp.broadcast_to(keys_in[i, :1], (key_step, HD))
             for start in range(0, cached, key_step):
                 part = keys_in[i, start : start + key_step]
+                part = jnp.where(ones[start : start + key_step] > 0, part, first)
                 scores = scored(both, jnp.concatenate([part, part], 1))
                 out[:, start : start + key_step] = scores
                 for at in range(0, key_step, HD):
@@ -168,7 +156,7 @@
         def weigh(i, slot):
             top = largest[slot]
             probs = jnp.exp2(score_refs[slot][...] - top[:, :1]).astype(bf16)
-            both = jnp.concatenate([values_in[i], ones[...]], 1)
+            both = jnp.concatenate([values_in[i] * ones[...], ones[...]], 1)
             total = jnp.dot(probs, both, preferred_element_type=f32)
             lane = lax.broadcasted_iota(jnp.int32, (rows, HD), 1)
             for c in range(count):
@@ -275,20 +263,22 @@
         def _():
             for t in range(chunks):
                 spots = where[t * sources : (t + 1) * sources]
-                stats = [held[a][c, :, width:].astype(f32) for a, c in spots]
+                levels = []
+                for a, c in spots:
+                    stats = held[a][c, :, width:].astype(f32)
+                    levels.append(
+                        stats + pltpu.roll(stats, HD - heads, axis=1) + pltpu.roll(stats, HD - 2 * heads, axis=1)
+                    )
+                top = functools.reduce(jnp.maximum, levels)
+                weights = [jnp.exp2(level - top) for level in levels]
+                total = functools.reduce(jnp.add, weights)
+                weights = [weight / total for weight in weights]
                 for h in range(heads):
-                    levels = [
-                        s[:, h : h + 1] + s[:, h + heads : h + heads + 1] + s[:, h + 2 * heads : h + 2 * heads + 1]
-                        for s in stats
-                    ]
-                    top = functools.reduce(jnp.maximum, levels)
-                    shares = [jnp.exp2(level - top) for level in levels]
-                    total = functools.reduce(jnp.add, shares)
                     mixed = None
-                    for (a, c), share in zip(spots, shares):
-                        term = held[a][c, :, h * HD : (h + 1) * HD].astype(f32) * share
+                    for (a, c), weight in zip(spots, weights):
+                        term = held[a][c, :, h * HD : (h + 1) * HD].astype(f32) * weight[:, h : h + 1]
                         mixed = term if mixed is None else mixed + term
-                    attention[t * rows : (t + 1) * rows, h * HD : (h + 1) * HD] = (mixed / total).astype(bf16)
+                    attention[t * rows : (t + 1) * rows, h * HD : (h + 1) * HD] = mixed.astype(bf16)
 
         result = jnp.dot(attention[...], weight_ref[...], preferred_element_type=f32).astype(bf16)
         for t in range(chunks):

time: 143 us -> 137 us (0.958)
  waiting for transfers between devices: 46.7 us -> 44.3 us
  starting transfers between devices: 40.8 us -> 38.4 us
    ppermute x21, waiting for transfers between devices: 30.5 us -> 28.6 us  [shifted(): lax.ppermute(array, axis, [(i, (i + by) % size) for i in range(size)])]
    ppermute x21, starting transfers between devices: 31.7 us -> 30 us  [shifted(): lax.ppermute(array, axis, [(i, (i + by) % size) for i in range(size)])]
  transfers between devices with their start and end apart: 38 -> 38, of which waited for: 17 -> 17; matrix products, arithmetic and copies ran while one was open for 1% -> 1% of each run, Pallas kernels for 21% -> 22%
where the time goes in v2:
time: 137 us
  Pallas kernels  47.6 us (35%)
  waiting for transfers between devices  44.3 us (32%)
  starting transfers between devices  38.4 us (28%)
  local copies, waits for them, and re-layouts  4.22 us (3%)
  other arithmetic  1.43 us (1%)
    pallas_call x3, Pallas kernels, attend(): pl.pallas_call(body, in_specs=[SM] * 3 + [HBM if own_first and n == 0 els...  30.4 us
    ppermute x21, starting transfers between devices, shifted(): lax.ppermute(array, axis, [(i, (i + by) % size) for i in range(size)])  30 us
    ppermute x21, waiting for transfers between devices, shifted(): lax.ppermute(array, axis, [(i, (i + by) % size) for i in range(size)])  28.6 us
    ppermute x17, waiting for transfers between devices, swapped(): lax.ppermute(array, axis, [(i, i ^ bit) for i in range(lax.axis_size(axis...  15.7 us
    pallas_call x1, Pallas kernels, run_expert(): pl.pallas_call(body, grid=(steps,), in_specs=[SM] + [VM] * count + [pl.Bl...  9.06 us
    ppermute x17, starting transfers between devices, swapped(): lax.ppermute(array, axis, [(i, i ^ bit) for i in range(lax.axis_size(axis...  8.39 us
    pallas_call x1, Pallas kernels, project(): pl.pallas_call(body, grid=(D // step,), in_specs=[VM] * len(arrays) + [pl...  6.12 us
    unnamed x40, local copies, waits for them, and re-layouts  3.49 us
  transfers between devices with their start and end apart: 38, of which 17 were waited for; matrix products, arithmetic and copies ran while one was open for 1% of the time, Pallas kernels for 22%

profile of v2, /device:TPU:0, one launch (start us, length us, event | category | flops | bytes accessed | tf_op | source)
XLA Modules:
  0.0 136.9 jit_solution(13382230355318031404)
XLA Ops:
  0.0 3.0 %collective-permute-start = (bf16[32,4096]{1,0:T(8,128)(2,1)}, bf16[32,4096]{1,0:T(8,128)(2,1)S(1)}, u32[]{:S(2)}, u32[]{:S(2)}) collective-permute-start(bf16[32,4096]{1,0:T(8,128)(2,1)} %refs_3_.1), channel_id=1, source_target_pairs={{0,1},{1,2},{2,3},{3,0},{4,5},{5,6},{6,7},{7,4},{8,9},{9,10},{10,1... | collective-permute-start | bytes 786440 | tf_op jit(solution)/shard_map/ppermute | solution.py:40
  3.0 2.0 %collective-permute-start.1 = (bf16[32,4096]{1,0:T(8,128)(2,1)}, bf16[32,4096]{1,0:T(8,128)(2,1)S(1)}, u32[]{:S(2)}, u32[]{:S(2)}) collective-permute-start(bf16[32,4096]{1,0:T(8,128)(2,1)} %refs_3_.1), channel_id=1, source_target_pairs={{0,3},{1,0},{2,1},{3,2},{4,7},{5,4},{6,5},{7,6},{8,11},{9,8},{10,9... | collective-permute-start | bytes 786440 | tf_op jit(solution)/shard_map/ppermute | solution.py:40
  5.8 8.8 %shard_map.127 = (bf16[1,32,1152]{2,1,0:T(8,128)(2,1)S(1)}, bf16[1,32,1152]{2,1,0:T(8,128)(2,1)S(1)}, bf16[1,32,1152]{2,1,0:T(8,128)(2,1)S(1)}, bf16[1,32,1152]{2,1,0:T(8,128)(2,1)S(1)}) custom-call(s32[2]{0:T(128)S(1)} %pad_add_fusion.refs_0_, s32[4]{0:T(128)S(1)} %and_select_fusion.refs_1_, s32[1]{0:T(128)} %bitcast.6.refs_2_, bf16[32,4096]{1,0:T(8,128)(2,1)} %refs_3_.1, ...), custom_call_target="tpu_custom_call" | custom-call | flops 17716740096 | bytes 8388608 | tf_op jit(solution)/shard_map/pallas_call | solution.py:207
  14.6 0.6 copy-done.2
  15.3 2.6 %collective-permute-start.3 = (bf16[1,32,1152]{2,1,0:T(8,128)(2,1)S(1)}, bf16[1,32,1152]{2,1,0:T(8,128)(2,1)S(1)}, u32[]{:S(2)}, u32[]{:S(2)}) collective-permute-start(bf16[1,32,1152]{2,1,0:T(8,128)(2,1)S(1)} %get-tuple-element.51), channel_id=1, source_target_pairs={{0,2},{1,3},{2,0},{3,1},{4,6},{5,7},{6,4},{7,5},{8,10},{9,11},{10,... | collective-permute-start | bytes 221192 | tf_op jit(solution)/shard_map/ppermute | solution.py:40
  17.9 1.3 collective-permute-start.4
  19.3 2.0 %collective-permute-start.6 = (bf16[32,4096]{1,0:T(8,128)(2,1)S(1)}, bf16[32,4096]{1,0:T(8,128)(2,1)S(1)}, u32[]{:S(2)}, u32[]{:S(2)}) collective-permute-start(bf16[32,4096]{1,0:T(8,128)(2,1)S(1)} %copy-done.19), channel_id=1, source_target_pairs={{0,2},{1,3},{2,0},{3,1},{4,6},{5,7},{6,4},{7,5},{8,10},{9,11},{10,... | collective-permute-start | bytes 786440 | tf_op jit(solution)/shard_map/ppermute | solution.py:40
  21.2 12.9 %shard_map.128 = (bf16[2,32,1152]{2,1,0:T(8,128)(2,1)S(1)}, bf16[2,32,1152]{2,1,0:T(8,128)(2,1)S(1)}, bf16[2,32,1152]{2,1,0:T(8,128)(2,1)S(1)}, bf16[2,32,1152]{2,1,0:T(8,128)(2,1)S(1)}) custom-call(s32[2]{0:T(128)S(1)} %pad_add_fusion.refs_0_, s32[4]{0:T(128)S(1)} %and_select_fusion.refs_1_, s32[2]{0:T(128)S(1)} %pad_add_fusion.1.refs_2_, ...), custom_call_target="tpu_custom_call" | custom-call | flops 35433480192 | bytes 8388608 | tf_op jit(solution)/shard_map/pallas_call | solution.py:207
  34.3 3.8 %collective-permute-start.8 = (bf16[2,32,1152]{2,1,0:T(8,128)(2,1)S(1)}, bf16[2,32,1152]{2,1,0:T(8,128)(2,1)S(1)}, u32[]{:S(2)}, u32[]{:S(2)}) collective-permute-start(bf16[2,32,1152]{2,1,0:T(8,128)(2,1)S(1)} %get-tuple-element.58), channel_id=1, source_target_pairs={{0,3},{1,0},{2,1},{3,2},{4,7},{5,4},{6,5},{7,6},{8,11},{9,8},{10,9... | collective-permute-start | bytes 442376 | tf_op jit(solution)/shard_map/ppermute | solution.py:40
  38.1 8.7 %shard_map.129 = (bf16[1,32,1152]{2,1,0:T(8,128)(2,1)S(1)}, bf16[1,32,1152]{2,1,0:T(8,128)(2,1)S(1)}, bf16[1,32,1152]{2,1,0:T(8,128)(2,1)S(1)}, bf16[1,32,1152]{2,1,0:T(8,128)(2,1)S(1)}) custom-call(s32[2]{0:T(128)S(1)} %pad_add_fusion.refs_0_, s32[4]{0:T(128)S(1)} %and_select_fusion.refs_1_, s32[1]{0:T(128)} %bitcast.refs_2_, ...), custom_call_target="tpu_custom_call" | custom-call | flops 17716740096 | bytes 8388608 | tf_op jit(solution)/shard_map/pallas_call | solution.py:207
  46.9 0.6 copy-done.3
  47.5 2.9 %collective-permute-start.7 = (bf16[1,32,1152]{2,1,0:T(8,128)(2,1)S(1)}, bf16[1,32,1152]{2,1,0:T(8,128)(2,1)S(1)}, u32[]{:S(2)}, u32[]{:S(2)}) collective-permute-start(bf16[1,32,1152]{2,1,0:T(8,128)(2,1)S(1)} %get-tuple-element.57), channel_id=1, source_target_pairs={{0,2},{1,3},{2,0},{3,1},{4,6},{5,7},{6,4},{7,5},{8,10},{9,11},{10,... | collective-permute-start | bytes 221192 | tf_op jit(solution)/shard_map/ppermute | solution.py:40
  50.4 2.0 %collective-permute-start.11 = (bf16[1,32,1152]{2,1,0:T(8,128)(2,1)S(1)}, bf16[1,32,1152]{2,1,0:T(8,128)(2,1)S(1)}, u32[]{:S(2)}, u32[]{:S(2)}) collective-permute-start(bf16[1,32,1152]{2,1,0:T(8,128)(2,1)S(1)} %get-tuple-element.65), channel_id=1, source_target_pairs={{0,1},{1,2},{2,3},{3,0},{4,5},{5,6},{6,7},{7,4},{8,9},{9,10},{10,1... | collective-permute-start | bytes 221192 | tf_op jit(solution)/shard_map/ppermute | solution.py:40
  52.5 1.9 %collective-permute-done.7.refs_2_ = bf16[1,32,1152]{2,1,0:T(8,128)(2,1)S(1)} collective-permute-done((bf16[1,32,1152]{2,1,0:T(8,128)(2,1)S(1)}, bf16[1,32,1152]{2,1,0:T(8,128)(2,1)S(1)}, u32[]{:S(2)}, u32[]{:S(2)}) %collective-permute-start.7) | collective-permute-done | bytes 73760 | tf_op jit(solution)/shard_map/ppermute | solution.py:40
  54.4 0.8 collective-permute-done.10.refs_7_
  55.1 1.5 %collective-permute-done.11.refs_10_ = bf16[1,32,1152]{2,1,0:T(8,128)(2,1)S(1)} collective-permute-done((bf16[1,32,1152]{2,1,0:T(8,128)(2,1)S(1)}, bf16[1,32,1152]{2,1,0:T(8,128)(2,1)S(1)}, u32[]{:S(2)}, u32[]{:S(2)}) %collective-permute-start.11) | collective-permute-done | bytes 73760 | tf_op jit(solution)/shard_map/ppermute | solution.py:40
  56.7 0.6 copy-done.16
  57.3 6.1 %project.1 = (bf16[32,2048]{1,0:T(8,128)(2,1)}, bf16[32,2048]{1,0:T(8,128)(2,1)}, bf16[32,2048]{1,0:T(8,128)(2,1)}, bf16[32,2048]{1,0:T(8,128)(2,1)}) custom-call(bf16[1,32,1152]{2,1,0:T(8,128)(2,1)} %copy-done.2, bf16[2,32,1152]{2,1,0:T(8,128)(2,1)} %copy-done.5, bf16[1,32,1152]{2,1,0:T(8,128)(2,1)} %copy-done.14, bf16[2,32,1152]{2,1,0:T(8,128)(2,1)} %copy-done.6, ...), custom_call_target="tpu_custom_call" | custom-call | tf_op jit(solution)/shard_map/project/pallas_call | solution.py:287
  63.4 0.9 collective-permute-start.12
  64.3 0.8 collective-permute-start.13
  65.1 1.0 collective-permute-start.14
  66.2 0.6 pad.4.refs_5_
  66.8 3.0 %collective-permute-done.12.refs_1_ = bf16[32,2048]{1,0:T(8,128)(2,1)S(1)} collective-permute-done((bf16[32,2048]{1,0:T(8,128)(2,1)}, bf16[32,2048]{1,0:T(8,128)(2,1)S(1)}, u32[]{:S(2)}, u32[]{:S(2)}) %collective-permute-start.12) | collective-permute-done | bytes 131104 | tf_op jit(solution)/shard_map/ppermute | solution.py:40
  69.9 4.2 %collective-permute-done.13.refs_2_ = bf16[32,2048]{1,0:T(8,128)(2,1)S(1)} collective-permute-done((bf16[32,2048]{1,0:T(8,128)(2,1)}, bf16[32,2048]{1,0:T(8,128)(2,1)S(1)}, u32[]{:S(2)}, u32[]{:S(2)}) %collective-permute-start.13) | collective-permute-done | bytes 131104 | tf_op jit(solution)/shard_map/ppermute | solution.py:40
  74.1 0.6 copy-done.9
  74.8 2.0 %normalize.1 = (f32[32,2048]{1,0:T(8,128)}, bf16[32,2176]{1,0:T(8,128)(2,1)}) custom-call(bf16[32,2048]{1,0:T(8,128)(2,1)} %residual_ref.1, bf16[32,2048]{1,0:T(8,128)(2,1)} %get-tuple-element.67.refs_0_, bf16[32,2048]{1,0:T(8,128)(2,1)} %copy-done.8, bf16[32,2048]{1,0:T(8,128)(2,1)} %copy-done.9, bf16[32,2048]{1,0:T(8,128)(2,1)} %copy-done.10, ...), custom_call_target="tpu_custom_call" | custom-call | tf_op jit(solution)/shard_map/normalize/pallas_call | solution.py:317
  76.8 1.6 %collective-permute-start.21 = (bf16[32,2176]{1,0:T(8,128)(2,1)}, bf16[32,2176]{1,0:T(8,128)(2,1)S(1)}, u32[]{:S(2)}, u32[]{:S(2)}) collective-permute-start(bf16[32,2176]{1,0:T(8,128)(2,1)} %get-tuple-element.72.refs_3_), channel_id=1, source_target_pairs={{0,8},{4,12},{8,0},{12,4},{1,9},{5,13},{9,1},{13,5},{2,10},{6,14},... | collective-permute-start | bytes 417800 | tf_op jit(solution)/shard_map/ppermute | solution.py:44
  78.4 1.1 collective-permute-start.17
  79.5 0.9 collective-permute-start.16
  80.4 1.6 %collective-permute-start.15 = (bf16[32,2176]{1,0:T(8,128)(2,1)}, bf16[32,2176]{1,0:T(8,128)(2,1)S(1)}, u32[]{:S(2)}, u32[]{:S(2)}) collective-permute-start(bf16[32,2176]{1,0:T(8,128)(2,1)} %get-tuple-element.72.refs_3_), channel_id=1, source_target_pairs={{0,2},{1,3},{2,0},{3,1},{4,6},{5,7},{6,4},{7,5},{8,10},{9,11},{10,... | collective-permute-start | bytes 417800 | tf_op jit(solution)/shard_map/ppermute | solution.py:40
  82.1 1.6 %collective-permute-done.17.refs_2_ = bf16[32,2176]{1,0:T(8,128)(2,1)S(1)} collective-permute-done((bf16[32,2176]{1,0:T(8,128)(2,1)}, bf16[32,2176]{1,0:T(8,128)(2,1)S(1)}, u32[]{:S(2)}, u32[]{:S(2)}) %collective-permute-start.17) | collective-permute-done | bytes 139296 | tf_op jit(solution)/shard_map/ppermute | solution.py:40
  84.2 3.9 %collective-permute-done.16.refs_1_ = bf16[32,2176]{1,0:T(8,128)(2,1)S(1)} collective-permute-done((bf16[32,2176]{1,0:T(8,128)(2,1)}, bf16[32,2176]{1,0:T(8,128)(2,1)S(1)}, u32[]{:S(2)}, u32[]{:S(2)}) %collective-permute-start.16) | collective-permute-done | bytes 139296 | tf_op jit(solution)/shard_map/ppermute | solution.py:40
  88.6 4.7 %collective-permute-done.15.refs_0_ = bf16[32,2176]{1,0:T(8,128)(2,1)S(1)} collective-permute-done((bf16[32,2176]{1,0:T(8,128)(2,1)}, bf16[32,2176]{1,0:T(8,128)(2,1)S(1)}, u32[]{:S(2)}, u32[]{:S(2)}) %collective-permute-start.15) | collective-permute-done | bytes 139296 | tf_op jit(solution)/shard_map/ppermute | solution.py:40
  94.8 3.9 %collective-permute-done.18.refs_4_ = bf16[32,2176]{1,0:T(8,128)(2,1)S(1)} collective-permute-done((bf16[32,2176]{1,0:T(8,128)(2,1)S(1)}, bf16[32,2176]{1,0:T(8,128)(2,1)S(1)}, u32[]{:S(2)}, u32[]{:S(2)}) %collective-permute-start.18) | collective-permute-done | bytes 139296 | tf_op jit(solution)/shard_map/ppermute | solution.py:44
  98.7 1.3 collective-permute-done.26.refs_12_
  100.0 0.9 copy-done.1
  100.9 9.1 %run_expert.1 = (f32[256,2048]{1,0:T(8,128)S(1)}, bf16[256,2048]{1,0:T(8,128)(2,1)S(1)}) custom-call(s32[1]{0:T(128)} %bitcast.11.expert_ref, bf16[32,2176]{1,0:T(8,128)(2,1)S(1)} %collective-permute-done.15.refs_0_, bf16[32,2176]{1,0:T(8,128)(2,1)S(1)} %collective-permute-done.16.refs_1_, bf16[32,2176]{1,0:T(8,128)(2,1)S(1)} %collective-permute-done.17.refs_2_, ...), custom_call_target="tpu_custom_call" | custom-call | tf_op jit(solution)/shard_map/run_expert/pallas_call | solution.py:375
  110.2 2.5 %collective-permute-done.30 = bf16[256,2048]{1,0:T(8,128)(2,1)S(1)} collective-permute-done((bf16[256,2048]{1,0:T(8,128)(2,1)S(1)}, bf16[256,2048]{1,0:T(8,128)(2,1)S(1)}, u32[]{:S(2)}, u32[]{:S(2)}) %collective-permute-start.30) | collective-permute-done | bytes 1048608 | tf_op jit(solution)/shard_map/ppermute | solution.py:44
  113.6 1.7 %collective-permute-start.35 = (bf16[32,2048]{1,0:T(8,128)(2,1)S(1)}, bf16[32,2048]{1,0:T(8,128)(2,1)S(1)}, u32[]{:S(2)}, u32[]{:S(2)}) collective-permute-start(bf16[32,2048]{1,0:T(8,128)(2,1)S(1)} %get-tuple-element.82), channel_id=1, source_target_pairs={{0,8},{4,12},{8,0},{12,4},{1,9},{5,13},{9,1},{13,5},{2,10},{6,14},... | collective-permute-start | bytes 393224 | tf_op jit(solution)/shard_map/ppermute | solution.py:44
  115.6 1.7 %collective-permute-start.37 = (bf16[32,2048]{1,0:T(8,128)(2,1)S(1)}, bf16[32,2048]{1,0:T(8,128)(2,1)S(1)}, u32[]{:S(2)}, u32[]{:S(2)}) collective-permute-start(bf16[32,2048]{1,0:T(8,128)(2,1)S(1)} %get-tuple-element.81), channel_id=1, source_target_pairs={{0,8},{4,12},{8,0},{12,4},{1,9},{5,13},{9,1},{13,5},{2,10},{6,14},... | collective-permute-start | bytes 393224 | tf_op jit(solution)/shard_map/ppermute | solution.py:44
  117.3 2.3 %collective-permute-done.31 = bf16[32,2048]{1,0:T(8,128)(2,1)S(1)} collective-permute-done((bf16[32,2048]{1,0:T(8,128)(2,1)S(1)}, bf16[32,2048]{1,0:T(8,128)(2,1)S(1)}, u32[]{:S(2)}, u32[]{:S(2)}) %collective-permute-start.31) | collective-permute-done | bytes 131104 | tf_op jit(solution)/shard_map/ppermute | solution.py:44
  119.6 2.8 %collective-permute-done.35 = bf16[32,2048]{1,0:T(8,128)(2,1)S(1)} collective-permute-done((bf16[32,2048]{1,0:T(8,128)(2,1)S(1)}, bf16[32,2048]{1,0:T(8,128)(2,1)S(1)}, u32[]{:S(2)}, u32[]{:S(2)}) %collective-permute-start.35) | collective-permute-done | bytes 131104 | tf_op jit(solution)/shard_map/ppermute | solution.py:44
  122.4 2.8 %collective-permute-done.33 = bf16[32,2048]{1,0:T(8,128)(2,1)S(1)} collective-permute-done((bf16[32,2048]{1,0:T(8,128)(2,1)S(1)}, bf16[32,2048]{1,0:T(8,128)(2,1)S(1)}, u32[]{:S(2)}, u32[]{:S(2)}) %collective-permute-start.33) | collective-permute-done | bytes 131104 | tf_op jit(solution)/shard_map/ppermute | solution.py:44
  125.4 2.1 %collective-permute-start.36 = (bf16[32,2048]{1,0:T(8,128)(2,1)S(1)}, bf16[32,2048]{1,0:T(8,128)(2,1)S(1)}, u32[]{:S(2)}, u32[]{:S(2)}) collective-permute-start(bf16[32,2048]{1,0:T(8,128)(2,1)S(1)} %get-tuple-element.78), channel_id=1, source_target_pairs={{0,1},{1,2},{2,3},{3,0},{4,5},{5,6},{6,7},{7,4},{8,9},{9,10},{10,1... | collective-permute-start | bytes 393224 | tf_op jit(solution)/shard_map/ppermute | solution.py:40
  127.5 1.7 %collective-permute-start.34 = (bf16[32,2048]{1,0:T(8,128)(2,1)S(1)}, bf16[32,2048]{1,0:T(8,128)(2,1)S(1)}, u32[]{:S(2)}, u32[]{:S(2)}) collective-permute-start(bf16[32,2048]{1,0:T(8,128)(2,1)S(1)} %get-tuple-element.79), channel_id=1, source_target_pairs={{0,3},{1,0},{2,1},{3,2},{4,7},{5,4},{6,5},{7,6},{8,11},{9,8},{10,9... | collective-permute-start | bytes 393224 | tf_op jit(solution)/shard_map/ppermute | solution.py:40
  129.3 6.3 %collective-permute-done.32 = bf16[32,2048]{1,0:T(8,128)(2,1)S(1)} collective-permute-done((bf16[32,2048]{1,0:T(8,128)(2,1)S(1)}, bf16[32,2048]{1,0:T(8,128)(2,1)S(1)}, u32[]{:S(2)}, u32[]{:S(2)}) %collective-permute-start.32) | collective-permute-done | bytes 131104 | tf_op jit(solution)/shard_map/ppermute | solution.py:40
  135.6 0.6 collective-permute-done.34
  136.2 0.8 fusion.2
  (85 shorter events, 4.6 us)
Async XLA Ops:
  0.0 19.2 %collective-permute-start = (bf16[32,4096]{1,0:T(8,128)(2,1)}, bf16[32,4096]{1,0:T(8,128)(2,1)S(1)}, u32[]{:S(2)}, u32[]{:S(2)}) collective-permute-start(bf16[32,4096]{1,0:T(8,128)(2,1)} %refs_3_.1), channel_id=1, source_target_pairs={{0,1},{1,2},{2,3},{3,0},{4,5},{5,6},{6,7},{7,4},{8,9},{9,10},{10,1... | collective-permute-start | bytes 786440 | tf_op jit(solution)/shard_map/ppermute | solution.py:40
  3.0 16.2 %collective-permute-start.1 = (bf16[32,4096]{1,0:T(8,128)(2,1)}, bf16[32,4096]{1,0:T(8,128)(2,1)S(1)}, u32[]{:S(2)}, u32[]{:S(2)}) collective-permute-start(bf16[32,4096]{1,0:T(8,128)(2,1)} %refs_3_.1), channel_id=1, source_target_pairs={{0,3},{1,0},{2,1},{3,2},{4,7},{5,4},{6,5},{7,6},{8,11},{9,8},{10,9... | collective-permute-start | bytes 786440 | tf_op jit(solution)/shard_map/ppermute | solution.py:40
  5.8 13.4 %copy-start.19 = (bf16[32,4096]{1,0:T(8,128)(2,1)S(1)}, bf16[32,4096]{1,0:T(8,128)(2,1)}, u32[]{:S(2)}) copy-start(bf16[32,4096]{1,0:T(8,128)(2,1)} %refs_3_.1) | copy-start | bytes 786436
  15.3 18.8 %collective-permute-start.2 = (bf16[1,32,1152]{2,1,0:T(8,128)(2,1)S(1)}, bf16[1,32,1152]{2,1,0:T(8,128)(2,1)S(1)}, u32[]{:S(2)}, u32[]{:S(2)}) collective-permute-start(bf16[1,32,1152]{2,1,0:T(8,128)(2,1)S(1)} %get-tuple-element.50), channel_id=1, source_target_pairs={{0,1},{1,2},{2,3},{3,0},{4,5},{5,6},{6,7},{7,4},{8,9},{9,10},{10,1... | collective-permute-start | bytes 221192 | tf_op jit(solution)/shard_map/ppermute | solution.py:40
  15.3 18.8 %collective-permute-start.3 = (bf16[1,32,1152]{2,1,0:T(8,128)(2,1)S(1)}, bf16[1,32,1152]{2,1,0:T(8,128)(2,1)S(1)}, u32[]{:S(2)}, u32[]{:S(2)}) collective-permute-start(bf16[1,32,1152]{2,1,0:T(8,128)(2,1)S(1)} %get-tuple-element.51), channel_id=1, source_target_pairs={{0,2},{1,3},{2,0},{3,1},{4,6},{5,7},{6,4},{7,5},{8,10},{9,11},{10,... | collective-permute-start | bytes 221192 | tf_op jit(solution)/shard_map/ppermute | solution.py:40
  17.9 16.3 %collective-permute-start.4 = (bf16[1,32,1152]{2,1,0:T(8,128)(2,1)S(1)}, bf16[1,32,1152]{2,1,0:T(8,128)(2,1)S(1)}, u32[]{:S(2)}, u32[]{:S(2)}) collective-permute-start(bf16[1,32,1152]{2,1,0:T(8,128)(2,1)S(1)} %get-tuple-element.52), channel_id=1, source_target_pairs={{0,3},{1,0},{2,1},{3,2},{4,7},{5,4},{6,5},{7,6},{8,11},{9,8},{10,9... | collective-permute-start | bytes 221192 | tf_op jit(solution)/shard_map/ppermute | solution.py:40
  19.3 18.8 %collective-permute-start.6 = (bf16[32,4096]{1,0:T(8,128)(2,1)S(1)}, bf16[32,4096]{1,0:T(8,128)(2,1)S(1)}, u32[]{:S(2)}, u32[]{:S(2)}) collective-permute-start(bf16[32,4096]{1,0:T(8,128)(2,1)S(1)} %copy-done.19), channel_id=1, source_target_pairs={{0,2},{1,3},{2,0},{3,1},{4,6},{5,7},{6,4},{7,5},{8,10},{9,11},{10,... | collective-permute-start | bytes 786440 | tf_op jit(solution)/shard_map/ppermute | solution.py:40
  34.1 12.7 %copy-start = (bf16[2,32,1152]{2,1,0:T(8,128)(2,1)}, bf16[2,32,1152]{2,1,0:T(8,128)(2,1)S(1)}, u32[]{:S(2)}) copy-start(bf16[2,32,1152]{2,1,0:T(8,128)(2,1)S(1)} %get-tuple-element.59.refs_4_) | copy-start | bytes 442372
  34.2 12.7 %copy-start.11 = (bf16[1,32,1152]{2,1,0:T(8,128)(2,1)}, bf16[1,32,1152]{2,1,0:T(8,128)(2,1)S(1)}, u32[]{:S(2)}) copy-start(bf16[1,32,1152]{2,1,0:T(8,128)(2,1)S(1)} %collective-permute-done.2.refs_5_) | copy-start | bytes 221188
  34.2 12.7 %copy-start.12 = (bf16[1,32,1152]{2,1,0:T(8,128)(2,1)}, bf16[1,32,1152]{2,1,0:T(8,128)(2,1)S(1)}, u32[]{:S(2)}) copy-start(bf16[1,32,1152]{2,1,0:T(8,128)(2,1)S(1)} %collective-permute-done.3.refs_9_) | copy-start | bytes 221188
  34.2 12.7 %copy-start.13 = (bf16[1,32,1152]{2,1,0:T(8,128)(2,1)}, bf16[1,32,1152]{2,1,0:T(8,128)(2,1)S(1)}, u32[]{:S(2)}) copy-start(bf16[1,32,1152]{2,1,0:T(8,128)(2,1)S(1)} %collective-permute-done.4.refs_11_) | copy-start | bytes 221188
  34.2 16.2 %collective-permute-start.5 = (bf16[2,32,1152]{2,1,0:T(8,128)(2,1)S(1)}, bf16[2,32,1152]{2,1,0:T(8,128)(2,1)S(1)}, u32[]{:S(2)}, u32[]{:S(2)}) collective-permute-start(bf16[2,32,1152]{2,1,0:T(8,128)(2,1)S(1)} %get-tuple-element.54), channel_id=1, source_target_pairs={{0,1},{1,2},{2,3},{3,0},{4,5},{5,6},{6,7},{7,4},{8,9},{9,10},{10,1... | collective-permute-start | bytes 442376 | tf_op jit(solution)/shard_map/ppermute | solution.py:40
  34.3 18.2 %collective-permute-start.8 = (bf16[2,32,1152]{2,1,0:T(8,128)(2,1)S(1)}, bf16[2,32,1152]{2,1,0:T(8,128)(2,1)S(1)}, u32[]{:S(2)}, u32[]{:S(2)}) collective-permute-start(bf16[2,32,1152]{2,1,0:T(8,128)(2,1)S(1)} %get-tuple-element.58), channel_id=1, source_target_pairs={{0,3},{1,0},{2,1},{3,2},{4,7},{5,4},{6,5},{7,6},{8,11},{9,8},{10,9... | collective-permute-start | bytes 442376 | tf_op jit(solution)/shard_map/ppermute | solution.py:40
  38.1 14.4 %collective-permute-start.9 = (bf16[2,32,1152]{2,1,0:T(8,128)(2,1)S(1)}, bf16[2,32,1152]{2,1,0:T(8,128)(2,1)S(1)}, u32[]{:S(2)}, u32[]{:S(2)}) collective-permute-start(bf16[2,32,1152]{2,1,0:T(8,128)(2,1)S(1)} %get-tuple-element.61), channel_id=1, source_target_pairs={{0,2},{1,3},{2,0},{3,1},{4,6},{5,7},{6,4},{7,5},{8,10},{9,11},{10,... | collective-permute-start | bytes 442376 | tf_op jit(solution)/shard_map/ppermute | solution.py:40
  47.5 6.9 %collective-permute-start.7 = (bf16[1,32,1152]{2,1,0:T(8,128)(2,1)S(1)}, bf16[1,32,1152]{2,1,0:T(8,128)(2,1)S(1)}, u32[]{:S(2)}, u32[]{:S(2)}) collective-permute-start(bf16[1,32,1152]{2,1,0:T(8,128)(2,1)S(1)} %get-tuple-element.57), channel_id=1, source_target_pairs={{0,2},{1,3},{2,0},{3,1},{4,6},{5,7},{6,4},{7,5},{8,10},{9,11},{10,... | collective-permute-start | bytes 221192 | tf_op jit(solution)/shard_map/ppermute | solution.py:40
  50.4 4.7 %collective-permute-start.10 = (bf16[1,32,1152]{2,1,0:T(8,128)(2,1)S(1)}, bf16[1,32,1152]{2,1,0:T(8,128)(2,1)S(1)}, u32[]{:S(2)}, u32[]{:S(2)}) collective-permute-start(bf16[1,32,1152]{2,1,0:T(8,128)(2,1)S(1)} %get-tuple-element.62), channel_id=1, source_target_pairs={{0,3},{1,0},{2,1},{3,2},{4,7},{5,4},{6,5},{7,6},{8,11},{9,8},{10,9... | collective-permute-start | bytes 221192 | tf_op jit(solution)/shard_map/ppermute | solution.py:40
  50.4 6.2 %copy-start.5 = (bf16[2,32,1152]{2,1,0:T(8,128)(2,1)}, bf16[2,32,1152]{2,1,0:T(8,128)(2,1)S(1)}, u32[]{:S(2)}) copy-start(bf16[2,32,1152]{2,1,0:T(8,128)(2,1)S(1)} %collective-permute-done.5.refs_1_) | copy-start | bytes 442372
  50.4 6.2 %collective-permute-start.11 = (bf16[1,32,1152]{2,1,0:T(8,128)(2,1)S(1)}, bf16[1,32,1152]{2,1,0:T(8,128)(2,1)S(1)}, u32[]{:S(2)}, u32[]{:S(2)}) collective-permute-start(bf16[1,32,1152]{2,1,0:T(8,128)(2,1)S(1)} %get-tuple-element.65), channel_id=1, source_target_pairs={{0,1},{1,2},{2,3},{3,0},{4,5},{5,6},{6,7},{7,4},{8,9},{9,10},{10,1... | collective-permute-start | bytes 221192 | tf_op jit(solution)/shard_map/ppermute | solution.py:40
  57.3 8.8 %copy-start.17 = (f32[32,8]{0,1:T(8,128)S(1)}, f32[32,8]{0,1:T(8,128)}, u32[]{:S(2)}) copy-start(f32[32,8]{0,1:T(8,128)} %param.25) | copy-start | bytes 3076
  57.3 8.8 %copy-start.18 = (s32[32,8]{0,1:T(8,128)S(1)}, s32[32,8]{0,1:T(8,128)}, u32[]{:S(2)}) copy-start(s32[32,8]{0,1:T(8,128)} %param.24) | copy-start | bytes 3076
  63.4 6.5 %collective-permute-start.12 = (bf16[32,2048]{1,0:T(8,128)(2,1)}, bf16[32,2048]{1,0:T(8,128)(2,1)S(1)}, u32[]{:S(2)}, u32[]{:S(2)}) collective-permute-start(bf16[32,2048]{1,0:T(8,128)(2,1)} %get-tuple-element.68), channel_id=1, source_target_pairs={{0,3},{1,0},{2,1},{3,2},{4,7},{5,4},{6,5},{7,6},{8,11},{9,8},{10,9... | collective-permute-start | bytes 393224 | tf_op jit(solution)/shard_map/ppermute | solution.py:40
  64.3 9.7 %collective-permute-start.13 = (bf16[32,2048]{1,0:T(8,128)(2,1)}, bf16[32,2048]{1,0:T(8,128)(2,1)S(1)}, u32[]{:S(2)}, u32[]{:S(2)}) collective-permute-start(bf16[32,2048]{1,0:T(8,128)(2,1)} %get-tuple-element.69), channel_id=1, source_target_pairs={{0,2},{1,3},{2,0},{3,1},{4,6},{5,7},{6,4},{7,5},{8,10},{9,11},{10,... | collective-permute-start | bytes 393224 | tf_op jit(solution)/shard_map/ppermute | solution.py:40
  65.1 9.0 %collective-permute-start.14 = (bf16[32,2048]{1,0:T(8,128)(2,1)}, bf16[32,2048]{1,0:T(8,128)(2,1)S(1)}, u32[]{:S(2)}, u32[]{:S(2)}) collective-permute-start(bf16[32,2048]{1,0:T(8,128)(2,1)} %get-tuple-element.70), channel_id=1, source_target_pairs={{0,1},{1,2},{2,3},{3,0},{4,5},{5,6},{6,7},{7,4},{8,9},{9,10},{10,1... | collective-permute-start | bytes 393224 | tf_op jit(solution)/shard_map/ppermute | solution.py:40
  69.9 4.2 %copy-start.8 = (bf16[32,2048]{1,0:T(8,128)(2,1)}, bf16[32,2048]{1,0:T(8,128)(2,1)S(1)}, u32[]{:S(2)}) copy-start(bf16[32,2048]{1,0:T(8,128)(2,1)S(1)} %collective-permute-done.12.refs_1_) | copy-start | bytes 393220
  76.8 5.3 %collective-permute-start.21 = (bf16[32,2176]{1,0:T(8,128)(2,1)}, bf16[32,2176]{1,0:T(8,128)(2,1)S(1)}, u32[]{:S(2)}, u32[]{:S(2)}) collective-permute-start(bf16[32,2176]{1,0:T(8,128)(2,1)} %get-tuple-element.72.refs_3_), channel_id=1, source_target_pairs={{0,8},{4,12},{8,0},{12,4},{1,9},{5,13},{9,1},{13,5},{2,10},{6,14},... | collective-permute-start | bytes 417800 | tf_op jit(solution)/shard_map/ppermute | solution.py:44
  78.4 5.3 %collective-permute-start.17 = (bf16[32,2176]{1,0:T(8,128)(2,1)}, bf16[32,2176]{1,0:T(8,128)(2,1)S(1)}, u32[]{:S(2)}, u32[]{:S(2)}) collective-permute-start(bf16[32,2176]{1,0:T(8,128)(2,1)} %get-tuple-element.72.refs_3_), channel_id=1, source_target_pairs={{0,3},{1,0},{2,1},{3,2},{4,7},{5,4},{6,5},{7,6},{8,11},{9,8},{10,9... | collective-permute-start | bytes 417800 | tf_op jit(solution)/shard_map/ppermute | solution.py:40
  79.5 4.2 %collective-permute-start.25 = (bf16[32,2176]{1,0:T(8,128)(2,1)}, bf16[32,2176]{1,0:T(8,128)(2,1)S(1)}, u32[]{:S(2)}, u32[]{:S(2)}) collective-permute-start(bf16[32,2176]{1,0:T(8,128)(2,1)} %get-tuple-element.72.refs_3_), channel_id=1, source_target_pairs={{0,4},{4,0},{8,12},{12,8},{1,5},{5,1},{9,13},{13,9},{2,6},{6,2},{1... | collective-permute-start | bytes 417800 | tf_op jit(solution)/shard_map/ppermute | solution.py:44
  79.5 8.6 %collective-permute-start.16 = (bf16[32,2176]{1,0:T(8,128)(2,1)}, bf16[32,2176]{1,0:T(8,128)(2,1)S(1)}, u32[]{:S(2)}, u32[]{:S(2)}) collective-permute-start(bf16[32,2176]{1,0:T(8,128)(2,1)} %get-tuple-element.72.refs_3_), channel_id=1, source_target_pairs={{0,1},{1,2},{2,3},{3,0},{4,5},{5,6},{6,7},{7,4},{8,9},{9,10},{10,1... | collective-permute-start | bytes 417800 | tf_op jit(solution)/shard_map/ppermute | solution.py:40
  80.4 12.9 %collective-permute-start.15 = (bf16[32,2176]{1,0:T(8,128)(2,1)}, bf16[32,2176]{1,0:T(8,128)(2,1)S(1)}, u32[]{:S(2)}, u32[]{:S(2)}) collective-permute-start(bf16[32,2176]{1,0:T(8,128)(2,1)} %get-tuple-element.72.refs_3_), channel_id=1, source_target_pairs={{0,2},{1,3},{2,0},{3,1},{4,6},{5,7},{6,4},{7,5},{8,10},{9,11},{10,... | collective-permute-start | bytes 417800 | tf_op jit(solution)/shard_map/ppermute | solution.py:40
  82.1 11.7 %collective-permute-start.29 = (bf16[32,2176]{1,0:T(8,128)(2,1)S(1)}, bf16[32,2176]{1,0:T(8,128)(2,1)S(1)}, u32[]{:S(2)}, u32[]{:S(2)}) collective-permute-start(bf16[32,2176]{1,0:T(8,128)(2,1)S(1)} %collective-permute-done.21.refs_7_), channel_id=1, source_target_pairs={{0,4},{4,0},{8,12},{12,8},{1,5},{5,1},{9,13},{13,9},{2,6},{6,2},{1... | collective-permute-start | bytes 417800 | tf_op jit(solution)/shard_map/ppermute | solution.py:44
  83.7 10.1 %collective-permute-start.24 = (bf16[32,2176]{1,0:T(8,128)(2,1)S(1)}, bf16[32,2176]{1,0:T(8,128)(2,1)S(1)}, u32[]{:S(2)}, u32[]{:S(2)}) collective-permute-start(bf16[32,2176]{1,0:T(8,128)(2,1)S(1)} %collective-permute-done.17.refs_2_), channel_id=1, source_target_pairs={{0,4},{4,0},{8,12},{12,8},{1,5},{5,1},{9,13},{13,9},{2,6},{6,2},{1... | collective-permute-start | bytes 417800 | tf_op jit(solution)/shard_map/ppermute | solution.py:44
  83.7 10.6 %collective-permute-start.20 = (bf16[32,2176]{1,0:T(8,128)(2,1)S(1)}, bf16[32,2176]{1,0:T(8,128)(2,1)S(1)}, u32[]{:S(2)}, u32[]{:S(2)}) collective-permute-start(bf16[32,2176]{1,0:T(8,128)(2,1)S(1)} %collective-permute-done.17.refs_2_), channel_id=1, source_target_pairs={{0,8},{4,12},{8,0},{12,4},{1,9},{5,13},{9,1},{13,5},{2,10},{6,14},... | collective-permute-start | bytes 417800 | tf_op jit(solution)/shard_map/ppermute | solution.py:44
  88.1 6.3 %collective-permute-start.19 = (bf16[32,2176]{1,0:T(8,128)(2,1)S(1)}, bf16[32,2176]{1,0:T(8,128)(2,1)S(1)}, u32[]{:S(2)}, u32[]{:S(2)}) collective-permute-start(bf16[32,2176]{1,0:T(8,128)(2,1)S(1)} %collective-permute-done.16.refs_1_), channel_id=1, source_target_pairs={{0,8},{4,12},{8,0},{12,4},{1,9},{5,13},{9,1},{13,5},{2,10},{6,14},... | collective-permute-start | bytes 417800 | tf_op jit(solution)/shard_map/ppermute | solution.py:44
  93.3 5.3 %collective-permute-start.18 = (bf16[32,2176]{1,0:T(8,128)(2,1)S(1)}, bf16[32,2176]{1,0:T(8,128)(2,1)S(1)}, u32[]{:S(2)}, u32[]{:S(2)}) collective-permute-start(bf16[32,2176]{1,0:T(8,128)(2,1)S(1)} %collective-permute-done.15.refs_0_), channel_id=1, source_target_pairs={{0,8},{4,12},{8,0},{12,4},{1,9},{5,13},{9,1},{13,5},{2,10},{6,14},... | collective-permute-start | bytes 417800 | tf_op jit(solution)/shard_map/ppermute | solution.py:44
  93.8 4.9 %collective-permute-start.23 = (bf16[32,2176]{1,0:T(8,128)(2,1)S(1)}, bf16[32,2176]{1,0:T(8,128)(2,1)S(1)}, u32[]{:S(2)}, u32[]{:S(2)}) collective-permute-start(bf16[32,2176]{1,0:T(8,128)(2,1)S(1)} %collective-permute-done.16.refs_1_), channel_id=1, source_target_pairs={{0,4},{4,0},{8,12},{12,8},{1,5},{5,1},{9,13},{13,9},{2,6},{6,2},{1... | collective-permute-start | bytes 417800 | tf_op jit(solution)/shard_map/ppermute | solution.py:44
  93.8 4.9 %collective-permute-start.22 = (bf16[32,2176]{1,0:T(8,128)(2,1)S(1)}, bf16[32,2176]{1,0:T(8,128)(2,1)S(1)}, u32[]{:S(2)}, u32[]{:S(2)}) collective-permute-start(bf16[32,2176]{1,0:T(8,128)(2,1)S(1)} %collective-permute-done.15.refs_0_), channel_id=1, source_target_pairs={{0,4},{4,0},{8,12},{12,8},{1,5},{5,1},{9,13},{13,9},{2,6},{6,2},{1... | collective-permute-start | bytes 417800 | tf_op jit(solution)/shard_map/ppermute | solution.py:44
  94.3 4.4 %collective-permute-start.28 = (bf16[32,2176]{1,0:T(8,128)(2,1)S(1)}, bf16[32,2176]{1,0:T(8,128)(2,1)S(1)}, u32[]{:S(2)}, u32[]{:S(2)}) collective-permute-start(bf16[32,2176]{1,0:T(8,128)(2,1)S(1)} %collective-permute-done.20.refs_6_), channel_id=1, source_target_pairs={{0,4},{4,0},{8,12},{12,8},{1,5},{5,1},{9,13},{13,9},{2,6},{6,2},{1... | collective-permute-start | bytes 417800 | tf_op jit(solution)/shard_map/ppermute | solution.py:44
  94.4 4.3 %collective-permute-start.27 = (bf16[32,2176]{1,0:T(8,128)(2,1)S(1)}, bf16[32,2176]{1,0:T(8,128)(2,1)S(1)}, u32[]{:S(2)}, u32[]{:S(2)}) collective-permute-start(bf16[32,2176]{1,0:T(8,128)(2,1)S(1)} %collective-permute-done.19.refs_5_), channel_id=1, source_target_pairs={{0,4},{4,0},{8,12},{12,8},{1,5},{5,1},{9,13},{13,9},{2,6},{6,2},{1... | collective-permute-start | bytes 417800 | tf_op jit(solution)/shard_map/ppermute | solution.py:44
  98.7 1.4 collective-permute-start.26
  110.0 2.7 %collective-permute-start.30 = (bf16[256,2048]{1,0:T(8,128)(2,1)S(1)}, bf16[256,2048]{1,0:T(8,128)(2,1)S(1)}, u32[]{:S(2)}, u32[]{:S(2)}) collective-permute-start(bf16[256,2048]{1,0:T(8,128)(2,1)S(1)} %get-tuple-element.74), channel_id=1, source_target_pairs={{0,4},{4,0},{8,12},{12,8},{1,5},{5,1},{9,13},{13,9},{2,6},{6,2},{1... | collective-permute-start | bytes 3145736 | tf_op jit(solution)/shard_map/ppermute | solution.py:44
  113.1 23.0 %copy-start.4 = (f32[32,2048]{1,0:T(8,128)S(1)}, f32[32,2048]{1,0:T(8,128)}, u32[]{:S(2)}) copy-start(f32[32,2048]{1,0:T(8,128)} %get-tuple-element.71) | copy-start | bytes 786436
  113.2 6.4 %collective-permute-start.31 = (bf16[32,2048]{1,0:T(8,128)(2,1)S(1)}, bf16[32,2048]{1,0:T(8,128)(2,1)S(1)}, u32[]{:S(2)}, u32[]{:S(2)}) collective-permute-start(bf16[32,2048]{1,0:T(8,128)(2,1)S(1)} %get-tuple-element.80), channel_id=1, source_target_pairs={{0,8},{4,12},{8,0},{12,4},{1,9},{5,13},{9,1},{13,5},{2,10},{6,14},... | collective-permute-start | bytes 393224 | tf_op jit(solution)/shard_map/ppermute | solution.py:44
  113.6 8.8 %collective-permute-start.35 = (bf16[32,2048]{1,0:T(8,128)(2,1)S(1)}, bf16[32,2048]{1,0:T(8,128)(2,1)S(1)}, u32[]{:S(2)}, u32[]{:S(2)}) collective-permute-start(bf16[32,2048]{1,0:T(8,128)(2,1)S(1)} %get-tuple-element.82), channel_id=1, source_target_pairs={{0,8},{4,12},{8,0},{12,4},{1,9},{5,13},{9,1},{13,5},{2,10},{6,14},... | collective-permute-start | bytes 393224 | tf_op jit(solution)/shard_map/ppermute | solution.py:44
  115.3 9.9 %collective-permute-start.33 = (bf16[32,2048]{1,0:T(8,128)(2,1)S(1)}, bf16[32,2048]{1,0:T(8,128)(2,1)S(1)}, u32[]{:S(2)}, u32[]{:S(2)}) collective-permute-start(bf16[32,2048]{1,0:T(8,128)(2,1)S(1)} %get-tuple-element.83), channel_id=1, source_target_pairs={{0,8},{4,12},{8,0},{12,4},{1,9},{5,13},{9,1},{13,5},{2,10},{6,14},... | collective-permute-start | bytes 393224 | tf_op jit(solution)/shard_map/ppermute | solution.py:44
  115.6 13.6 %collective-permute-start.37 = (bf16[32,2048]{1,0:T(8,128)(2,1)S(1)}, bf16[32,2048]{1,0:T(8,128)(2,1)S(1)}, u32[]{:S(2)}, u32[]{:S(2)}) collective-permute-start(bf16[32,2048]{1,0:T(8,128)(2,1)S(1)} %get-tuple-element.81), channel_id=1, source_target_pairs={{0,8},{4,12},{8,0},{12,4},{1,9},{5,13},{9,1},{13,5},{2,10},{6,14},... | collective-permute-start | bytes 393224 | tf_op jit(solution)/shard_map/ppermute | solution.py:44
  125.3 10.2 %collective-permute-start.32 = (bf16[32,2048]{1,0:T(8,128)(2,1)S(1)}, bf16[32,2048]{1,0:T(8,128)(2,1)S(1)}, u32[]{:S(2)}, u32[]{:S(2)}) collective-permute-start(bf16[32,2048]{1,0:T(8,128)(2,1)S(1)} %get-tuple-element.77), channel_id=1, source_target_pairs={{0,2},{1,3},{2,0},{3,1},{4,6},{5,7},{6,4},{7,5},{8,10},{9,11},{10,... | collective-permute-start | bytes 393224 | tf_op jit(solution)/shard_map/ppermute | solution.py:40
  125.4 10.2 %collective-permute-start.36 = (bf16[32,2048]{1,0:T(8,128)(2,1)S(1)}, bf16[32,2048]{1,0:T(8,128)(2,1)S(1)}, u32[]{:S(2)}, u32[]{:S(2)}) collective-permute-start(bf16[32,2048]{1,0:T(8,128)(2,1)S(1)} %get-tuple-element.78), channel_id=1, source_target_pairs={{0,1},{1,2},{2,3},{3,0},{4,5},{5,6},{6,7},{7,4},{8,9},{9,10},{10,1... | collective-permute-start | bytes 393224 | tf_op jit(solution)/shard_map/ppermute | solution.py:40
  127.5 8.6 %collective-permute-start.34 = (bf16[32,2048]{1,0:T(8,128)(2,1)S(1)}, bf16[32,2048]{1,0:T(8,128)(2,1)S(1)}, u32[]{:S(2)}, u32[]{:S(2)}) collective-permute-start(bf16[32,2048]{1,0:T(8,128)(2,1)S(1)} %get-tuple-element.79), channel_id=1, source_target_pairs={{0,3},{1,0},{2,1},{3,2},{4,7},{5,4},{6,5},{7,6},{8,11},{9,8},{10,9... | collective-permute-start | bytes 393224 | tf_op jit(solution)/shard_map/ppermute | solution.py:40
  (10 other events, 16.3 us)

commit v3 on v2

--- a/solution.py
+++ b/solution.py
@@ -335,33 +335,28 @@
 
     def body(expert_ref, *refs):
         message_refs = refs[:count]
-        gate_ref, up_ref, down_ref, kept_ref, sent_ref, features, total = refs[count:]
+        gate_ref, up_ref, down_hbm, kept_ref, sent_ref, features, inner, down_in, down_sem = refs[count:]
         stage = pl.program_id(0)
+        down_copy = pltpu.make_async_copy(down_hbm, down_in, down_sem)
 
         @pl.when(stage == 0)
         def _():
+            down_copy.start()
             for c in range(count):
                 features[c * rows : (c + 1) * rows] = message_refs[c][:, :D]
 
         gate = jnp.dot(features[...], gate_ref[...], preferred_element_type=f32)
         up = jnp.dot(features[...], up_ref[...], preferred_element_type=f32)
-        inner = (gate / (1.0 + jnp.exp(-gate)) * up).astype(bf16)
-
-        part = jnp.dot(inner, down_ref[...], preferred_element_type=f32)
-
-        @pl.when(stage == 0)
-        def _():
-            total[...] = part
-
-        @pl.when(stage > 0)
-        def _():
-            total[...] += part
+        inner[stage] = (gate / (1.0 + jnp.exp(-gate)) * up).astype(bf16)
 
         @pl.when(stage == steps - 1)
         def _():
+            down_copy.wait()
             mine = expert_ref[0]
             lane = lax.broadcasted_iota(jnp.int32, (rows, HD), 1)
             chosen = (lane == mine) | (lane == mine + experts) | (lane == mine + 2 * experts)
+            joined = jnp.concatenate([inner[n] for n in range(steps)], 1)
+            total = jnp.dot(joined, down_in[...], preferred_element_type=f32)
             for c in range(count):
                 parts = message_refs[c][:, D:].astype(f32)
                 weight = jnp.sum(jnp.where(chosen, parts, 0.0), 1, keepdims=True)
@@ -380,11 +375,16 @@
         + [
             pl.BlockSpec((D, step), lambda n: (0, n)),
             pl.BlockSpec((D, step), lambda n: (0, n + steps)),
-            pl.BlockSpec((step, D), lambda n: (n, 0)),
+            HBM,
         ],
         out_specs=[VM] * 2,
         out_shape=[jax.ShapeDtypeStruct((half, D), f32), jax.ShapeDtypeStruct((half, D), bf16)],
-        scratch_shapes=[pltpu.VMEM((count * rows, D), bf16), pltpu.VMEM((count * rows, D), f32)],
+        scratch_shapes=[
+            pltpu.VMEM((count * rows, D), bf16),
+            pltpu.VMEM((steps, count * rows, step), bf16),
+            pltpu.VMEM((FF, D), bf16),
+            pltpu.SemaphoreType.DMA,
+        ],
         compiler_params=pltpu.CompilerParams(vmem_limit_bytes=36 << 20),
         name="run_expert",
     )(expert, *messages, in_hbm(gate_up), in_hbm(gate_up), in_hbm(down))

time: 137 us -> 136 us (level)
  no operation moved by 1% of the time
where the time goes in v3:
time: 136 us
  Pallas kernels  46.4 us (34%)
  waiting for transfers between devices  44.3 us (33%)
  starting transfers between devices  38.4 us (28%)
  local copies, waits for them, and re-layouts  4.22 us (3%)
  other arithmetic  1.43 us (1%)
    pallas_call x3, Pallas kernels, attend(): pl.pallas_call(body, in_specs=[SM] * 3 + [HBM if own_first and n == 0 els...  30.4 us
    ppermute x21, starting transfers between devices, shifted(): lax.ppermute(array, axis, [(i, (i + by) % size) for i in range(size)])  30 us
    ppermute x21, waiting for transfers between devices, shifted(): lax.ppermute(array, axis, [(i, (i + by) % size) for i in range(size)])  28.6 us
    ppermute x17, waiting for transfers between devices, swapped(): lax.ppermute(array, axis, [(i, i ^ bit) for i in range(lax.axis_size(axis...  15.7 us
    ppermute x17, starting transfers between devices, swapped(): lax.ppermute(array, axis, [(i, i ^ bit) for i in range(lax.axis_size(axis...  8.39 us
    pallas_call x1, Pallas kernels, run_expert(): pl.pallas_call(body, grid=(steps,), in_specs=[SM] + [VM] * count + [pl.Bl...  7.8 us
    pallas_call x1, Pallas kernels, project(): pl.pallas_call(body, grid=(D // step,), in_specs=[VM] * len(arrays) + [pl...  6.12 us
    unnamed x40, local copies, waits for them, and re-layouts  3.49 us
  transfers between devices with their start and end apart: 38, of which 17 were waited for; matrix products, arithmetic and copies ran while one was open for 1% of the time, Pallas kernels for 22%

profile of v3, /device:TPU:0, one launch (start us, length us, event | category | flops | bytes accessed | tf_op | source)
XLA Modules:
  0.0 135.7 jit_solution(3612249380359700416)
XLA Ops:
  0.0 3.0 %collective-permute-start = (bf16[32,4096]{1,0:T(8,128)(2,1)}, bf16[32,4096]{1,0:T(8,128)(2,1)S(1)}, u32[]{:S(2)}, u32[]{:S(2)}) collective-permute-start(bf16[32,4096]{1,0:T(8,128)(2,1)} %refs_3_.1), channel_id=1, source_target_pairs={{0,1},{1,2},{2,3},{3,0},{4,5},{5,6},{6,7},{7,4},{8,9},{9,10},{10,1... | collective-permute-start | bytes 786440 | tf_op jit(solution)/shard_map/ppermute | solution.py:40
  3.0 2.0 %collective-permute-start.1 = (bf16[32,4096]{1,0:T(8,128)(2,1)}, bf16[32,4096]{1,0:T(8,128)(2,1)S(1)}, u32[]{:S(2)}, u32[]{:S(2)}) collective-permute-start(bf16[32,4096]{1,0:T(8,128)(2,1)} %refs_3_.1), channel_id=1, source_target_pairs={{0,3},{1,0},{2,1},{3,2},{4,7},{5,4},{6,5},{7,6},{8,11},{9,8},{10,9... | collective-permute-start | bytes 786440 | tf_op jit(solution)/shard_map/ppermute | solution.py:40
  5.8 8.8 %shard_map.127 = (bf16[1,32,1152]{2,1,0:T(8,128)(2,1)S(1)}, bf16[1,32,1152]{2,1,0:T(8,128)(2,1)S(1)}, bf16[1,32,1152]{2,1,0:T(8,128)(2,1)S(1)}, bf16[1,32,1152]{2,1,0:T(8,128)(2,1)S(1)}) custom-call(s32[2]{0:T(128)S(1)} %pad_add_fusion.refs_0_, s32[4]{0:T(128)S(1)} %and_select_fusion.refs_1_, s32[1]{0:T(128)} %bitcast.6.refs_2_, bf16[32,4096]{1,0:T(8,128)(2,1)} %refs_3_.1, ...), custom_call_target="tpu_custom_call" | custom-call | flops 17716740096 | bytes 8388608 | tf_op jit(solution)/shard_map/pallas_call | solution.py:207
  14.6 0.6 copy-done.2
  15.3 2.6 %collective-permute-start.3 = (bf16[1,32,1152]{2,1,0:T(8,128)(2,1)S(1)}, bf16[1,32,1152]{2,1,0:T(8,128)(2,1)S(1)}, u32[]{:S(2)}, u32[]{:S(2)}) collective-permute-start(bf16[1,32,1152]{2,1,0:T(8,128)(2,1)S(1)} %get-tuple-element.51), channel_id=1, source_target_pairs={{0,2},{1,3},{2,0},{3,1},{4,6},{5,7},{6,4},{7,5},{8,10},{9,11},{10,... | collective-permute-start | bytes 221192 | tf_op jit(solution)/shard_map/ppermute | solution.py:40
  17.9 1.3 collective-permute-start.4
  19.3 2.0 %collective-permute-start.6 = (bf16[32,4096]{1,0:T(8,128)(2,1)S(1)}, bf16[32,4096]{1,0:T(8,128)(2,1)S(1)}, u32[]{:S(2)}, u32[]{:S(2)}) collective-permute-start(bf16[32,4096]{1,0:T(8,128)(2,1)S(1)} %copy-done.19), channel_id=1, source_target_pairs={{0,2},{1,3},{2,0},{3,1},{4,6},{5,7},{6,4},{7,5},{8,10},{9,11},{10,... | collective-permute-start | bytes 786440 | tf_op jit(solution)/shard_map/ppermute | solution.py:40
  21.2 12.9 %shard_map.128 = (bf16[2,32,1152]{2,1,0:T(8,128)(2,1)S(1)}, bf16[2,32,1152]{2,1,0:T(8,128)(2,1)S(1)}, bf16[2,32,1152]{2,1,0:T(8,128)(2,1)S(1)}, bf16[2,32,1152]{2,1,0:T(8,128)(2,1)S(1)}) custom-call(s32[2]{0:T(128)S(1)} %pad_add_fusion.refs_0_, s32[4]{0:T(128)S(1)} %and_select_fusion.refs_1_, s32[2]{0:T(128)S(1)} %pad_add_fusion.1.refs_2_, ...), custom_call_target="tpu_custom_call" | custom-call | flops 35433480192 | bytes 8388608 | tf_op jit(solution)/shard_map/pallas_call | solution.py:207
  34.3 3.8 %collective-permute-start.8 = (bf16[2,32,1152]{2,1,0:T(8,128)(2,1)S(1)}, bf16[2,32,1152]{2,1,0:T(8,128)(2,1)S(1)}, u32[]{:S(2)}, u32[]{:S(2)}) collective-permute-start(bf16[2,32,1152]{2,1,0:T(8,128)(2,1)S(1)} %get-tuple-element.58), channel_id=1, source_target_pairs={{0,3},{1,0},{2,1},{3,2},{4,7},{5,4},{6,5},{7,6},{8,11},{9,8},{10,9... | collective-permute-start | bytes 442376 | tf_op jit(solution)/shard_map/ppermute | solution.py:40
  38.1 8.7 %shard_map.129 = (bf16[1,32,1152]{2,1,0:T(8,128)(2,1)S(1)}, bf16[1,32,1152]{2,1,0:T(8,128)(2,1)S(1)}, bf16[1,32,1152]{2,1,0:T(8,128)(2,1)S(1)}, bf16[1,32,1152]{2,1,0:T(8,128)(2,1)S(1)}) custom-call(s32[2]{0:T(128)S(1)} %pad_add_fusion.refs_0_, s32[4]{0:T(128)S(1)} %and_select_fusion.refs_1_, s32[1]{0:T(128)} %bitcast.refs_2_, ...), custom_call_target="tpu_custom_call" | custom-call | flops 17716740096 | bytes 8388608 | tf_op jit(solution)/shard_map/pallas_call | solution.py:207
  46.9 0.6 copy-done.3
  47.5 2.9 %collective-permute-start.7 = (bf16[1,32,1152]{2,1,0:T(8,128)(2,1)S(1)}, bf16[1,32,1152]{2,1,0:T(8,128)(2,1)S(1)}, u32[]{:S(2)}, u32[]{:S(2)}) collective-permute-start(bf16[1,32,1152]{2,1,0:T(8,128)(2,1)S(1)} %get-tuple-element.57), channel_id=1, source_target_pairs={{0,2},{1,3},{2,0},{3,1},{4,6},{5,7},{6,4},{7,5},{8,10},{9,11},{10,... | collective-permute-start | bytes 221192 | tf_op jit(solution)/shard_map/ppermute | solution.py:40
  50.4 2.0 %collective-permute-start.11 = (bf16[1,32,1152]{2,1,0:T(8,128)(2,1)S(1)}, bf16[1,32,1152]{2,1,0:T(8,128)(2,1)S(1)}, u32[]{:S(2)}, u32[]{:S(2)}) collective-permute-start(bf16[1,32,1152]{2,1,0:T(8,128)(2,1)S(1)} %get-tuple-element.65), channel_id=1, source_target_pairs={{0,1},{1,2},{2,3},{3,0},{4,5},{5,6},{6,7},{7,4},{8,9},{9,10},{10,1... | collective-permute-start | bytes 221192 | tf_op jit(solution)/shard_map/ppermute | solution.py:40
  52.5 1.9 %collective-permute-done.7.refs_2_ = bf16[1,32,1152]{2,1,0:T(8,128)(2,1)S(1)} collective-permute-done((bf16[1,32,1152]{2,1,0:T(8,128)(2,1)S(1)}, bf16[1,32,1152]{2,1,0:T(8,128)(2,1)S(1)}, u32[]{:S(2)}, u32[]{:S(2)}) %collective-permute-start.7) | collective-permute-done | bytes 73760 | tf_op jit(solution)/shard_map/ppermute | solution.py:40
  54.4 0.8 collective-permute-done.10.refs_7_
  55.1 1.5 %collective-permute-done.11.refs_10_ = bf16[1,32,1152]{2,1,0:T(8,128)(2,1)S(1)} collective-permute-done((bf16[1,32,1152]{2,1,0:T(8,128)(2,1)S(1)}, bf16[1,32,1152]{2,1,0:T(8,128)(2,1)S(1)}, u32[]{:S(2)}, u32[]{:S(2)}) %collective-permute-start.11) | collective-permute-done | bytes 73760 | tf_op jit(solution)/shard_map/ppermute | solution.py:40
  56.7 0.6 copy-done.16
  57.3 6.1 %project.1 = (bf16[32,2048]{1,0:T(8,128)(2,1)}, bf16[32,2048]{1,0:T(8,128)(2,1)}, bf16[32,2048]{1,0:T(8,128)(2,1)}, bf16[32,2048]{1,0:T(8,128)(2,1)}) custom-call(bf16[1,32,1152]{2,1,0:T(8,128)(2,1)} %copy-done.2, bf16[2,32,1152]{2,1,0:T(8,128)(2,1)} %copy-done.5, bf16[1,32,1152]{2,1,0:T(8,128)(2,1)} %copy-done.14, bf16[2,32,1152]{2,1,0:T(8,128)(2,1)} %copy-done.6, ...), custom_call_target="tpu_custom_call" | custom-call | tf_op jit(solution)/shard_map/project/pallas_call | solution.py:287
  63.4 0.9 collective-permute-start.12
  64.3 0.8 collective-permute-start.13
  65.1 1.0 collective-permute-start.14
  66.2 0.6 pad.4.refs_5_
  66.8 3.0 %collective-permute-done.12.refs_1_ = bf16[32,2048]{1,0:T(8,128)(2,1)S(1)} collective-permute-done((bf16[32,2048]{1,0:T(8,128)(2,1)}, bf16[32,2048]{1,0:T(8,128)(2,1)S(1)}, u32[]{:S(2)}, u32[]{:S(2)}) %collective-permute-start.12) | collective-permute-done | bytes 131104 | tf_op jit(solution)/shard_map/ppermute | solution.py:40
  69.9 4.2 %collective-permute-done.13.refs_2_ = bf16[32,2048]{1,0:T(8,128)(2,1)S(1)} collective-permute-done((bf16[32,2048]{1,0:T(8,128)(2,1)}, bf16[32,2048]{1,0:T(8,128)(2,1)S(1)}, u32[]{:S(2)}, u32[]{:S(2)}) %collective-permute-start.13) | collective-permute-done | bytes 131104 | tf_op jit(solution)/shard_map/ppermute | solution.py:40
  74.1 0.6 copy-done.9
  74.8 2.0 %normalize.1 = (f32[32,2048]{1,0:T(8,128)}, bf16[32,2176]{1,0:T(8,128)(2,1)}) custom-call(bf16[32,2048]{1,0:T(8,128)(2,1)} %residual_ref.1, bf16[32,2048]{1,0:T(8,128)(2,1)} %get-tuple-element.67.refs_0_, bf16[32,2048]{1,0:T(8,128)(2,1)} %copy-done.8, bf16[32,2048]{1,0:T(8,128)(2,1)} %copy-done.9, bf16[32,2048]{1,0:T(8,128)(2,1)} %copy-done.10, ...), custom_call_target="tpu_custom_call" | custom-call | tf_op jit(solution)/shard_map/normalize/pallas_call | solution.py:317
  76.8 1.6 %collective-permute-start.21 = (bf16[32,2176]{1,0:T(8,128)(2,1)}, bf16[32,2176]{1,0:T(8,128)(2,1)S(1)}, u32[]{:S(2)}, u32[]{:S(2)}) collective-permute-start(bf16[32,2176]{1,0:T(8,128)(2,1)} %get-tuple-element.72.refs_3_), channel_id=1, source_target_pairs={{0,8},{4,12},{8,0},{12,4},{1,9},{5,13},{9,1},{13,5},{2,10},{6,14},... | collective-permute-start | bytes 417800 | tf_op jit(solution)/shard_map/ppermute | solution.py:44
  78.4 1.1 collective-permute-start.17
  79.5 0.9 collective-permute-start.16
  80.4 1.6 %collective-permute-start.15 = (bf16[32,2176]{1,0:T(8,128)(2,1)}, bf16[32,2176]{1,0:T(8,128)(2,1)S(1)}, u32[]{:S(2)}, u32[]{:S(2)}) collective-permute-start(bf16[32,2176]{1,0:T(8,128)(2,1)} %get-tuple-element.72.refs_3_), channel_id=1, source_target_pairs={{0,2},{1,3},{2,0},{3,1},{4,6},{5,7},{6,4},{7,5},{8,10},{9,11},{10,... | collective-permute-start | bytes 417800 | tf_op jit(solution)/shard_map/ppermute | solution.py:40
  82.1 1.6 %collective-permute-done.17.refs_2_ = bf16[32,2176]{1,0:T(8,128)(2,1)S(1)} collective-permute-done((bf16[32,2176]{1,0:T(8,128)(2,1)}, bf16[32,2176]{1,0:T(8,128)(2,1)S(1)}, u32[]{:S(2)}, u32[]{:S(2)}) %collective-permute-start.17) | collective-permute-done | bytes 139296 | tf_op jit(solution)/shard_map/ppermute | solution.py:40
  84.2 3.9 %collective-permute-done.16.refs_1_ = bf16[32,2176]{1,0:T(8,128)(2,1)S(1)} collective-permute-done((bf16[32,2176]{1,0:T(8,128)(2,1)}, bf16[32,2176]{1,0:T(8,128)(2,1)S(1)}, u32[]{:S(2)}, u32[]{:S(2)}) %collective-permute-start.16) | collective-permute-done | bytes 139296 | tf_op jit(solution)/shard_map/ppermute | solution.py:40
  88.6 4.7 %collective-permute-done.15.refs_0_ = bf16[32,2176]{1,0:T(8,128)(2,1)S(1)} collective-permute-done((bf16[32,2176]{1,0:T(8,128)(2,1)}, bf16[32,2176]{1,0:T(8,128)(2,1)S(1)}, u32[]{:S(2)}, u32[]{:S(2)}) %collective-permute-start.15) | collective-permute-done | bytes 139296 | tf_op jit(solution)/shard_map/ppermute | solution.py:40
  94.8 3.9 %collective-permute-done.18.refs_4_ = bf16[32,2176]{1,0:T(8,128)(2,1)S(1)} collective-permute-done((bf16[32,2176]{1,0:T(8,128)(2,1)S(1)}, bf16[32,2176]{1,0:T(8,128)(2,1)S(1)}, u32[]{:S(2)}, u32[]{:S(2)}) %collective-permute-start.18) | collective-permute-done | bytes 139296 | tf_op jit(solution)/shard_map/ppermute | solution.py:44
  98.7 1.3 collective-permute-done.26.refs_12_
  100.0 0.9 copy-done.1
  100.9 7.8 %run_expert.1 = (f32[256,2048]{1,0:T(8,128)S(1)}, bf16[256,2048]{1,0:T(8,128)(2,1)S(1)}) custom-call(s32[1]{0:T(128)} %bitcast.11.expert_ref, bf16[32,2176]{1,0:T(8,128)(2,1)S(1)} %collective-permute-done.15.refs_0_, bf16[32,2176]{1,0:T(8,128)(2,1)S(1)} %collective-permute-done.16.refs_1_, bf16[32,2176]{1,0:T(8,128)(2,1)S(1)} %collective-permute-done.17.refs_2_, ...), custom_call_target="tpu_custom_call" | custom-call | tf_op jit(solution)/shard_map/run_expert/pallas_call | solution.py:370
  109.0 2.5 %collective-permute-done.30 = bf16[256,2048]{1,0:T(8,128)(2,1)S(1)} collective-permute-done((bf16[256,2048]{1,0:T(8,128)(2,1)S(1)}, bf16[256,2048]{1,0:T(8,128)(2,1)S(1)}, u32[]{:S(2)}, u32[]{:S(2)}) %collective-permute-start.30) | collective-permute-done | bytes 1048608 | tf_op jit(solution)/shard_map/ppermute | solution.py:44
  112.4 1.7 %collective-permute-start.35 = (bf16[32,2048]{1,0:T(8,128)(2,1)S(1)}, bf16[32,2048]{1,0:T(8,128)(2,1)S(1)}, u32[]{:S(2)}, u32[]{:S(2)}) collective-permute-start(bf16[32,2048]{1,0:T(8,128)(2,1)S(1)} %get-tuple-element.82), channel_id=1, source_target_pairs={{0,8},{4,12},{8,0},{12,4},{1,9},{5,13},{9,1},{13,5},{2,10},{6,14},... | collective-permute-start | bytes 393224 | tf_op jit(solution)/shard_map/ppermute | solution.py:44
  114.4 1.7 %collective-permute-start.37 = (bf16[32,2048]{1,0:T(8,128)(2,1)S(1)}, bf16[32,2048]{1,0:T(8,128)(2,1)S(1)}, u32[]{:S(2)}, u32[]{:S(2)}) collective-permute-start(bf16[32,2048]{1,0:T(8,128)(2,1)S(1)} %get-tuple-element.81), channel_id=1, source_target_pairs={{0,8},{4,12},{8,0},{12,4},{1,9},{5,13},{9,1},{13,5},{2,10},{6,14},... | collective-permute-start | bytes 393224 | tf_op jit(solution)/shard_map/ppermute | solution.py:44
  116.0 2.3 %collective-permute-done.31 = bf16[32,2048]{1,0:T(8,128)(2,1)S(1)} collective-permute-done((bf16[32,2048]{1,0:T(8,128)(2,1)S(1)}, bf16[32,2048]{1,0:T(8,128)(2,1)S(1)}, u32[]{:S(2)}, u32[]{:S(2)}) %collective-permute-start.31) | collective-permute-done | bytes 131104 | tf_op jit(solution)/shard_map/ppermute | solution.py:44
  118.3 2.8 %collective-permute-done.35 = bf16[32,2048]{1,0:T(8,128)(2,1)S(1)} collective-permute-done((bf16[32,2048]{1,0:T(8,128)(2,1)S(1)}, bf16[32,2048]{1,0:T(8,128)(2,1)S(1)}, u32[]{:S(2)}, u32[]{:S(2)}) %collective-permute-start.35) | collective-permute-done | bytes 131104 | tf_op jit(solution)/shard_map/ppermute | solution.py:44
  121.1 2.8 %collective-permute-done.33 = bf16[32,2048]{1,0:T(8,128)(2,1)S(1)} collective-permute-done((bf16[32,2048]{1,0:T(8,128)(2,1)S(1)}, bf16[32,2048]{1,0:T(8,128)(2,1)S(1)}, u32[]{:S(2)}, u32[]{:S(2)}) %collective-permute-start.33) | collective-permute-done | bytes 131104 | tf_op jit(solution)/shard_map/ppermute | solution.py:44
  124.1 2.1 %collective-permute-start.36 = (bf16[32,2048]{1,0:T(8,128)(2,1)S(1)}, bf16[32,2048]{1,0:T(8,128)(2,1)S(1)}, u32[]{:S(2)}, u32[]{:S(2)}) collective-permute-start(bf16[32,2048]{1,0:T(8,128)(2,1)S(1)} %get-tuple-element.78), channel_id=1, source_target_pairs={{0,1},{1,2},{2,3},{3,0},{4,5},{5,6},{6,7},{7,4},{8,9},{9,10},{10,1... | collective-permute-start | bytes 393224 | tf_op jit(solution)/shard_map/ppermute | solution.py:40
  126.3 1.7 %collective-permute-start.34 = (bf16[32,2048]{1,0:T(8,128)(2,1)S(1)}, bf16[32,2048]{1,0:T(8,128)(2,1)S(1)}, u32[]{:S(2)}, u32[]{:S(2)}) collective-permute-start(bf16[32,2048]{1,0:T(8,128)(2,1)S(1)} %get-tuple-element.79), channel_id=1, source_target_pairs={{0,3},{1,0},{2,1},{3,2},{4,7},{5,4},{6,5},{7,6},{8,11},{9,8},{10,9... | collective-permute-start | bytes 393224 | tf_op jit(solution)/shard_map/ppermute | solution.py:40
  128.0 6.3 %collective-permute-done.32 = bf16[32,2048]{1,0:T(8,128)(2,1)S(1)} collective-permute-done((bf16[32,2048]{1,0:T(8,128)(2,1)S(1)}, bf16[32,2048]{1,0:T(8,128)(2,1)S(1)}, u32[]{:S(2)}, u32[]{:S(2)}) %collective-permute-start.32) | collective-permute-done | bytes 131104 | tf_op jit(solution)/shard_map/ppermute | solution.py:40
  134.3 0.6 collective-permute-done.34
  134.9 0.8 fusion.2
  (85 shorter events, 4.6 us)
Async XLA Ops:
  0.0 19.2 %collective-permute-start = (bf16[32,4096]{1,0:T(8,128)(2,1)}, bf16[32,4096]{1,0:T(8,128)(2,1)S(1)}, u32[]{:S(2)}, u32[]{:S(2)}) collective-permute-start(bf16[32,4096]{1,0:T(8,128)(2,1)} %refs_3_.1), channel_id=1, source_target_pairs={{0,1},{1,2},{2,3},{3,0},{4,5},{5,6},{6,7},{7,4},{8,9},{9,10},{10,1... | collective-permute-start | bytes 786440 | tf_op jit(solution)/shard_map/ppermute | solution.py:40
  3.0 16.2 %collective-permute-start.1 = (bf16[32,4096]{1,0:T(8,128)(2,1)}, bf16[32,4096]{1,0:T(8,128)(2,1)S(1)}, u32[]{:S(2)}, u32[]{:S(2)}) collective-permute-start(bf16[32,4096]{1,0:T(8,128)(2,1)} %refs_3_.1), channel_id=1, source_target_pairs={{0,3},{1,0},{2,1},{3,2},{4,7},{5,4},{6,5},{7,6},{8,11},{9,8},{10,9... | collective-permute-start | bytes 786440 | tf_op jit(solution)/shard_map/ppermute | solution.py:40
  5.8 13.4 %copy-start.19 = (bf16[32,4096]{1,0:T(8,128)(2,1)S(1)}, bf16[32,4096]{1,0:T(8,128)(2,1)}, u32[]{:S(2)}) copy-start(bf16[32,4096]{1,0:T(8,128)(2,1)} %refs_3_.1) | copy-start | bytes 786436
  15.3 18.8 %collective-permute-start.2 = (bf16[1,32,1152]{2,1,0:T(8,128)(2,1)S(1)}, bf16[1,32,1152]{2,1,0:T(8,128)(2,1)S(1)}, u32[]{:S(2)}, u32[]{:S(2)}) collective-permute-start(bf16[1,32,1152]{2,1,0:T(8,128)(2,1)S(1)} %get-tuple-element.50), channel_id=1, source_target_pairs={{0,1},{1,2},{2,3},{3,0},{4,5},{5,6},{6,7},{7,4},{8,9},{9,10},{10,1... | collective-permute-start | bytes 221192 | tf_op jit(solution)/shard_map/ppermute | solution.py:40
  15.3 18.8 %collective-permute-start.3 = (bf16[1,32,1152]{2,1,0:T(8,128)(2,1)S(1)}, bf16[1,32,1152]{2,1,0:T(8,128)(2,1)S(1)}, u32[]{:S(2)}, u32[]{:S(2)}) collective-permute-start(bf16[1,32,1152]{2,1,0:T(8,128)(2,1)S(1)} %get-tuple-element.51), channel_id=1, source_target_pairs={{0,2},{1,3},{2,0},{3,1},{4,6},{5,7},{6,4},{7,5},{8,10},{9,11},{10,... | collective-permute-start | bytes 221192 | tf_op jit(solution)/shard_map/ppermute | solution.py:40
  17.9 16.3 %collective-permute-start.4 = (bf16[1,32,1152]{2,1,0:T(8,128)(2,1)S(1)}, bf16[1,32,1152]{2,1,0:T(8,128)(2,1)S(1)}, u32[]{:S(2)}, u32[]{:S(2)}) collective-permute-start(bf16[1,32,1152]{2,1,0:T(8,128)(2,1)S(1)} %get-tuple-element.52), channel_id=1, source_target_pairs={{0,3},{1,0},{2,1},{3,2},{4,7},{5,4},{6,5},{7,6},{8,11},{9,8},{10,9... | collective-permute-start | bytes 221192 | tf_op jit(solution)/shard_map/ppermute | solution.py:40
  19.3 18.8 %collective-permute-start.6 = (bf16[32,4096]{1,0:T(8,128)(2,1)S(1)}, bf16[32,4096]{1,0:T(8,128)(2,1)S(1)}, u32[]{:S(2)}, u32[]{:S(2)}) collective-permute-start(bf16[32,4096]{1,0:T(8,128)(2,1)S(1)} %copy-done.19), channel_id=1, source_target_pairs={{0,2},{1,3},{2,0},{3,1},{4,6},{5,7},{6,4},{7,5},{8,10},{9,11},{10,... | collective-permute-start | bytes 786440 | tf_op jit(solution)/shard_map/ppermute | solution.py:40
  34.1 12.7 %copy-start = (bf16[2,32,1152]{2,1,0:T(8,128)(2,1)}, bf16[2,32,1152]{2,1,0:T(8,128)(2,1)S(1)}, u32[]{:S(2)}) copy-start(bf16[2,32,1152]{2,1,0:T(8,128)(2,1)S(1)} %get-tuple-element.59.refs_4_) | copy-start | bytes 442372
  34.2 12.7 %copy-start.11 = (bf16[1,32,1152]{2,1,0:T(8,128)(2,1)}, bf16[1,32,1152]{2,1,0:T(8,128)(2,1)S(1)}, u32[]{:S(2)}) copy-start(bf16[1,32,1152]{2,1,0:T(8,128)(2,1)S(1)} %collective-permute-done.2.refs_5_) | copy-start | bytes 221188
  34.2 12.7 %copy-start.12 = (bf16[1,32,1152]{2,1,0:T(8,128)(2,1)}, bf16[1,32,1152]{2,1,0:T(8,128)(2,1)S(1)}, u32[]{:S(2)}) copy-start(bf16[1,32,1152]{2,1,0:T(8,128)(2,1)S(1)} %collective-permute-done.3.refs_9_) | copy-start | bytes 221188
  34.2 12.7 %copy-start.13 = (bf16[1,32,1152]{2,1,0:T(8,128)(2,1)}, bf16[1,32,1152]{2,1,0:T(8,128)(2,1)S(1)}, u32[]{:S(2)}) copy-start(bf16[1,32,1152]{2,1,0:T(8,128)(2,1)S(1)} %collective-permute-done.4.refs_11_) | copy-start | bytes 221188
  34.2 16.2 %collective-permute-start.5 = (bf16[2,32,1152]{2,1,0:T(8,128)(2,1)S(1)}, bf16[2,32,1152]{2,1,0:T(8,128)(2,1)S(1)}, u32[]{:S(2)}, u32[]{:S(2)}) collective-permute-start(bf16[2,32,1152]{2,1,0:T(8,128)(2,1)S(1)} %get-tuple-element.54), channel_id=1, source_target_pairs={{0,1},{1,2},{2,3},{3,0},{4,5},{5,6},{6,7},{7,4},{8,9},{9,10},{10,1... | collective-permute-start | bytes 442376 | tf_op jit(solution)/shard_map/ppermute | solution.py:40
  34.3 18.2 %collective-permute-start.8 = (bf16[2,32,1152]{2,1,0:T(8,128)(2,1)S(1)}, bf16[2,32,1152]{2,1,0:T(8,128)(2,1)S(1)}, u32[]{:S(2)}, u32[]{:S(2)}) collective-permute-start(bf16[2,32,1152]{2,1,0:T(8,128)(2,1)S(1)} %get-tuple-element.58), channel_id=1, source_target_pairs={{0,3},{1,0},{2,1},{3,2},{4,7},{5,4},{6,5},{7,6},{8,11},{9,8},{10,9... | collective-permute-start | bytes 442376 | tf_op jit(solution)/shard_map/ppermute | solution.py:40
  38.1 14.4 %collective-permute-start.9 = (bf16[2,32,1152]{2,1,0:T(8,128)(2,1)S(1)}, bf16[2,32,1152]{2,1,0:T(8,128)(2,1)S(1)}, u32[]{:S(2)}, u32[]{:S(2)}) collective-permute-start(bf16[2,32,1152]{2,1,0:T(8,128)(2,1)S(1)} %get-tuple-element.61), channel_id=1, source_target_pairs={{0,2},{1,3},{2,0},{3,1},{4,6},{5,7},{6,4},{7,5},{8,10},{9,11},{10,... | collective-permute-start | bytes 442376 | tf_op jit(solution)/shard_map/ppermute | solution.py:40
  47.5 6.9 %collective-permute-start.7 = (bf16[1,32,1152]{2,1,0:T(8,128)(2,1)S(1)}, bf16[1,32,1152]{2,1,0:T(8,128)(2,1)S(1)}, u32[]{:S(2)}, u32[]{:S(2)}) collective-permute-start(bf16[1,32,1152]{2,1,0:T(8,128)(2,1)S(1)} %get-tuple-element.57), channel_id=1, source_target_pairs={{0,2},{1,3},{2,0},{3,1},{4,6},{5,7},{6,4},{7,5},{8,10},{9,11},{10,... | collective-permute-start | bytes 221192 | tf_op jit(solution)/shard_map/ppermute | solution.py:40
  50.4 4.7 %collective-permute-start.10 = (bf16[1,32,1152]{2,1,0:T(8,128)(2,1)S(1)}, bf16[1,32,1152]{2,1,0:T(8,128)(2,1)S(1)}, u32[]{:S(2)}, u32[]{:S(2)}) collective-permute-start(bf16[1,32,1152]{2,1,0:T(8,128)(2,1)S(1)} %get-tuple-element.62), channel_id=1, source_target_pairs={{0,3},{1,0},{2,1},{3,2},{4,7},{5,4},{6,5},{7,6},{8,11},{9,8},{10,9... | collective-permute-start | bytes 221192 | tf_op jit(solution)/shard_map/ppermute | solution.py:40
  50.4 6.2 %copy-start.5 = (bf16[2,32,1152]{2,1,0:T(8,128)(2,1)}, bf16[2,32,1152]{2,1,0:T(8,128)(2,1)S(1)}, u32[]{:S(2)}) copy-start(bf16[2,32,1152]{2,1,0:T(8,128)(2,1)S(1)} %collective-permute-done.5.refs_1_) | copy-start | bytes 442372
  50.4 6.2 %collective-permute-start.11 = (bf16[1,32,1152]{2,1,0:T(8,128)(2,1)S(1)}, bf16[1,32,1152]{2,1,0:T(8,128)(2,1)S(1)}, u32[]{:S(2)}, u32[]{:S(2)}) collective-permute-start(bf16[1,32,1152]{2,1,0:T(8,128)(2,1)S(1)} %get-tuple-element.65), channel_id=1, source_target_pairs={{0,1},{1,2},{2,3},{3,0},{4,5},{5,6},{6,7},{7,4},{8,9},{9,10},{10,1... | collective-permute-start | bytes 221192 | tf_op jit(solution)/shard_map/ppermute | solution.py:40
  57.3 8.8 %copy-start.17 = (f32[32,8]{0,1:T(8,128)S(1)}, f32[32,8]{0,1:T(8,128)}, u32[]{:S(2)}) copy-start(f32[32,8]{0,1:T(8,128)} %param.25) | copy-start | bytes 3076
  57.3 8.8 %copy-start.18 = (s32[32,8]{0,1:T(8,128)S(1)}, s32[32,8]{0,1:T(8,128)}, u32[]{:S(2)}) copy-start(s32[32,8]{0,1:T(8,128)} %param.24) | copy-start | bytes 3076
  63.4 6.5 %collective-permute-start.12 = (bf16[32,2048]{1,0:T(8,128)(2,1)}, bf16[32,2048]{1,0:T(8,128)(2,1)S(1)}, u32[]{:S(2)}, u32[]{:S(2)}) collective-permute-start(bf16[32,2048]{1,0:T(8,128)(2,1)} %get-tuple-element.68), channel_id=1, source_target_pairs={{0,3},{1,0},{2,1},{3,2},{4,7},{5,4},{6,5},{7,6},{8,11},{9,8},{10,9... | collective-permute-start | bytes 393224 | tf_op jit(solution)/shard_map/ppermute | solution.py:40
  64.3 9.7 %collective-permute-start.13 = (bf16[32,2048]{1,0:T(8,128)(2,1)}, bf16[32,2048]{1,0:T(8,128)(2,1)S(1)}, u32[]{:S(2)}, u32[]{:S(2)}) collective-permute-start(bf16[32,2048]{1,0:T(8,128)(2,1)} %get-tuple-element.69), channel_id=1, source_target_pairs={{0,2},{1,3},{2,0},{3,1},{4,6},{5,7},{6,4},{7,5},{8,10},{9,11},{10,... | collective-permute-start | bytes 393224 | tf_op jit(solution)/shard_map/ppermute | solution.py:40
  65.1 9.0 %collective-permute-start.14 = (bf16[32,2048]{1,0:T(8,128)(2,1)}, bf16[32,2048]{1,0:T(8,128)(2,1)S(1)}, u32[]{:S(2)}, u32[]{:S(2)}) collective-permute-start(bf16[32,2048]{1,0:T(8,128)(2,1)} %get-tuple-element.70), channel_id=1, source_target_pairs={{0,1},{1,2},{2,3},{3,0},{4,5},{5,6},{6,7},{7,4},{8,9},{9,10},{10,1... | collective-permute-start | bytes 393224 | tf_op jit(solution)/shard_map/ppermute | solution.py:40
  69.9 4.2 %copy-start.8 = (bf16[32,2048]{1,0:T(8,128)(2,1)}, bf16[32,2048]{1,0:T(8,128)(2,1)S(1)}, u32[]{:S(2)}) copy-start(bf16[32,2048]{1,0:T(8,128)(2,1)S(1)} %collective-permute-done.12.refs_1_) | copy-start | bytes 393220
  76.8 5.3 %collective-permute-start.21 = (bf16[32,2176]{1,0:T(8,128)(2,1)}, bf16[32,2176]{1,0:T(8,128)(2,1)S(1)}, u32[]{:S(2)}, u32[]{:S(2)}) collective-permute-start(bf16[32,2176]{1,0:T(8,128)(2,1)} %get-tuple-element.72.refs_3_), channel_id=1, source_target_pairs={{0,8},{4,12},{8,0},{12,4},{1,9},{5,13},{9,1},{13,5},{2,10},{6,14},... | collective-permute-start | bytes 417800 | tf_op jit(solution)/shard_map/ppermute | solution.py:44
  78.4 5.3 %collective-permute-start.17 = (bf16[32,2176]{1,0:T(8,128)(2,1)}, bf16[32,2176]{1,0:T(8,128)(2,1)S(1)}, u32[]{:S(2)}, u32[]{:S(2)}) collective-permute-start(bf16[32,2176]{1,0:T(8,128)(2,1)} %get-tuple-element.72.refs_3_), channel_id=1, source_target_pairs={{0,3},{1,0},{2,1},{3,2},{4,7},{5,4},{6,5},{7,6},{8,11},{9,8},{10,9... | collective-permute-start | bytes 417800 | tf_op jit(solution)/shard_map/ppermute | solution.py:40
  79.5 4.2 %collective-permute-start.25 = (bf16[32,2176]{1,0:T(8,128)(2,1)}, bf16[32,2176]{1,0:T(8,128)(2,1)S(1)}, u32[]{:S(2)}, u32[]{:S(2)}) collective-permute-start(bf16[32,2176]{1,0:T(8,128)(2,1)} %get-tuple-element.72.refs_3_), channel_id=1, source_target_pairs={{0,4},{4,0},{8,12},{12,8},{1,5},{5,1},{9,13},{13,9},{2,6},{6,2},{1... | collective-permute-start | bytes 417800 | tf_op jit(solution)/shard_map/ppermute | solution.py:44
  79.5 8.6 %collective-permute-start.16 = (bf16[32,2176]{1,0:T(8,128)(2,1)}, bf16[32,2176]{1,0:T(8,128)(2,1)S(1)}, u32[]{:S(2)}, u32[]{:S(2)}) collective-permute-start(bf16[32,2176]{1,0:T(8,128)(2,1)} %get-tuple-element.72.refs_3_), channel_id=1, source_target_pairs={{0,1},{1,2},{2,3},{3,0},{4,5},{5,6},{6,7},{7,4},{8,9},{9,10},{10,1... | collective-permute-start | bytes 417800 | tf_op jit(solution)/shard_map/ppermute | solution.py:40
  80.4 12.9 %collective-permute-start.15 = (bf16[32,2176]{1,0:T(8,128)(2,1)}, bf16[32,2176]{1,0:T(8,128)(2,1)S(1)}, u32[]{:S(2)}, u32[]{:S(2)}) collective-permute-start(bf16[32,2176]{1,0:T(8,128)(2,1)} %get-tuple-element.72.refs_3_), channel_id=1, source_target_pairs={{0,2},{1,3},{2,0},{3,1},{4,6},{5,7},{6,4},{7,5},{8,10},{9,11},{10,... | collective-permute-start | bytes 417800 | tf_op jit(solution)/shard_map/ppermute | solution.py:40
  82.1 11.7 %collective-permute-start.29 = (bf16[32,2176]{1,0:T(8,128)(2,1)S(1)}, bf16[32,2176]{1,0:T(8,128)(2,1)S(1)}, u32[]{:S(2)}, u32[]{:S(2)}) collective-permute-start(bf16[32,2176]{1,0:T(8,128)(2,1)S(1)} %collective-permute-done.21.refs_7_), channel_id=1, source_target_pairs={{0,4},{4,0},{8,12},{12,8},{1,5},{5,1},{9,13},{13,9},{2,6},{6,2},{1... | collective-permute-start | bytes 417800 | tf_op jit(solution)/shard_map/ppermute | solution.py:44
  83.7 10.1 %collective-permute-start.24 = (bf16[32,2176]{1,0:T(8,128)(2,1)S(1)}, bf16[32,2176]{1,0:T(8,128)(2,1)S(1)}, u32[]{:S(2)}, u32[]{:S(2)}) collective-permute-start(bf16[32,2176]{1,0:T(8,128)(2,1)S(1)} %collective-permute-done.17.refs_2_), channel_id=1, source_target_pairs={{0,4},{4,0},{8,12},{12,8},{1,5},{5,1},{9,13},{13,9},{2,6},{6,2},{1... | collective-permute-start | bytes 417800 | tf_op jit(solution)/shard_map/ppermute | solution.py:44
  83.7 10.6 %collective-permute-start.20 = (bf16[32,2176]{1,0:T(8,128)(2,1)S(1)}, bf16[32,2176]{1,0:T(8,128)(2,1)S(1)}, u32[]{:S(2)}, u32[]{:S(2)}) collective-permute-start(bf16[32,2176]{1,0:T(8,128)(2,1)S(1)} %collective-permute-done.17.refs_2_), channel_id=1, source_target_pairs={{0,8},{4,12},{8,0},{12,4},{1,9},{5,13},{9,1},{13,5},{2,10},{6,14},... | collective-permute-start | bytes 417800 | tf_op jit(solution)/shard_map/ppermute | solution.py:44
  88.1 6.3 %collective-permute-start.19 = (bf16[32,2176]{1,0:T(8,128)(2,1)S(1)}, bf16[32,2176]{1,0:T(8,128)(2,1)S(1)}, u32[]{:S(2)}, u32[]{:S(2)}) collective-permute-start(bf16[32,2176]{1,0:T(8,128)(2,1)S(1)} %collective-permute-done.16.refs_1_), channel_id=1, source_target_pairs={{0,8},{4,12},{8,0},{12,4},{1,9},{5,13},{9,1},{13,5},{2,10},{6,14},... | collective-permute-start | bytes 417800 | tf_op jit(solution)/shard_map/ppermute | solution.py:44
  93.3 5.3 %collective-permute-start.18 = (bf16[32,2176]{1,0:T(8,128)(2,1)S(1)}, bf16[32,2176]{1,0:T(8,128)(2,1)S(1)}, u32[]{:S(2)}, u32[]{:S(2)}) collective-permute-start(bf16[32,2176]{1,0:T(8,128)(2,1)S(1)} %collective-permute-done.15.refs_0_), channel_id=1, source_target_pairs={{0,8},{4,12},{8,0},{12,4},{1,9},{5,13},{9,1},{13,5},{2,10},{6,14},... | collective-permute-start | bytes 417800 | tf_op jit(solution)/shard_map/ppermute | solution.py:44
  93.8 4.9 %collective-permute-start.23 = (bf16[32,2176]{1,0:T(8,128)(2,1)S(1)}, bf16[32,2176]{1,0:T(8,128)(2,1)S(1)}, u32[]{:S(2)}, u32[]{:S(2)}) collective-permute-start(bf16[32,2176]{1,0:T(8,128)(2,1)S(1)} %collective-permute-done.16.refs_1_), channel_id=1, source_target_pairs={{0,4},{4,0},{8,12},{12,8},{1,5},{5,1},{9,13},{13,9},{2,6},{6,2},{1... | collective-permute-start | bytes 417800 | tf_op jit(solution)/shard_map/ppermute | solution.py:44
  93.8 4.9 %collective-permute-start.22 = (bf16[32,2176]{1,0:T(8,128)(2,1)S(1)}, bf16[32,2176]{1,0:T(8,128)(2,1)S(1)}, u32[]{:S(2)}, u32[]{:S(2)}) collective-permute-start(bf16[32,2176]{1,0:T(8,128)(2,1)S(1)} %collective-permute-done.15.refs_0_), channel_id=1, source_target_pairs={{0,4},{4,0},{8,12},{12,8},{1,5},{5,1},{9,13},{13,9},{2,6},{6,2},{1... | collective-permute-start | bytes 417800 | tf_op jit(solution)/shard_map/ppermute | solution.py:44
  94.3 4.4 %collective-permute-start.28 = (bf16[32,2176]{1,0:T(8,128)(2,1)S(1)}, bf16[32,2176]{1,0:T(8,128)(2,1)S(1)}, u32[]{:S(2)}, u32[]{:S(2)}) collective-permute-start(bf16[32,2176]{1,0:T(8,128)(2,1)S(1)} %collective-permute-done.20.refs_6_), channel_id=1, source_target_pairs={{0,4},{4,0},{8,12},{12,8},{1,5},{5,1},{9,13},{13,9},{2,6},{6,2},{1... | collective-permute-start | bytes 417800 | tf_op jit(solution)/shard_map/ppermute | solution.py:44
  94.3 4.3 %collective-permute-start.27 = (bf16[32,2176]{1,0:T(8,128)(2,1)S(1)}, bf16[32,2176]{1,0:T(8,128)(2,1)S(1)}, u32[]{:S(2)}, u32[]{:S(2)}) collective-permute-start(bf16[32,2176]{1,0:T(8,128)(2,1)S(1)} %collective-permute-done.19.refs_5_), channel_id=1, source_target_pairs={{0,4},{4,0},{8,12},{12,8},{1,5},{5,1},{9,13},{13,9},{2,6},{6,2},{1... | collective-permute-start | bytes 417800 | tf_op jit(solution)/shard_map/ppermute | solution.py:44
  98.7 1.4 %collective-permute-start.26 = (bf16[32,2176]{1,0:T(8,128)(2,1)S(1)}, bf16[32,2176]{1,0:T(8,128)(2,1)S(1)}, u32[]{:S(2)}, u32[]{:S(2)}) collective-permute-start(bf16[32,2176]{1,0:T(8,128)(2,1)S(1)} %collective-permute-done.18.refs_4_), channel_id=1, source_target_pairs={{0,4},{4,0},{8,12},{12,8},{1,5},{5,1},{9,13},{13,9},{2,6},{6,2},{1... | collective-permute-start | bytes 417800 | tf_op jit(solution)/shard_map/ppermute | solution.py:44
  108.7 2.7 %collective-permute-start.30 = (bf16[256,2048]{1,0:T(8,128)(2,1)S(1)}, bf16[256,2048]{1,0:T(8,128)(2,1)S(1)}, u32[]{:S(2)}, u32[]{:S(2)}) collective-permute-start(bf16[256,2048]{1,0:T(8,128)(2,1)S(1)} %get-tuple-element.74), channel_id=1, source_target_pairs={{0,4},{4,0},{8,12},{12,8},{1,5},{5,1},{9,13},{13,9},{2,6},{6,2},{1... | collective-permute-start | bytes 3145736 | tf_op jit(solution)/shard_map/ppermute | solution.py:44
  111.9 23.0 %copy-start.4 = (f32[32,2048]{1,0:T(8,128)S(1)}, f32[32,2048]{1,0:T(8,128)}, u32[]{:S(2)}) copy-start(f32[32,2048]{1,0:T(8,128)} %get-tuple-element.71) | copy-start | bytes 786436
  111.9 6.4 %collective-permute-start.31 = (bf16[32,2048]{1,0:T(8,128)(2,1)S(1)}, bf16[32,2048]{1,0:T(8,128)(2,1)S(1)}, u32[]{:S(2)}, u32[]{:S(2)}) collective-permute-start(bf16[32,2048]{1,0:T(8,128)(2,1)S(1)} %get-tuple-element.80), channel_id=1, source_target_pairs={{0,8},{4,12},{8,0},{12,4},{1,9},{5,13},{9,1},{13,5},{2,10},{6,14},... | collective-permute-start | bytes 393224 | tf_op jit(solution)/shard_map/ppermute | solution.py:44
  112.4 8.8 %collective-permute-start.35 = (bf16[32,2048]{1,0:T(8,128)(2,1)S(1)}, bf16[32,2048]{1,0:T(8,128)(2,1)S(1)}, u32[]{:S(2)}, u32[]{:S(2)}) collective-permute-start(bf16[32,2048]{1,0:T(8,128)(2,1)S(1)} %get-tuple-element.82), channel_id=1, source_target_pairs={{0,8},{4,12},{8,0},{12,4},{1,9},{5,13},{9,1},{13,5},{2,10},{6,14},... | collective-permute-start | bytes 393224 | tf_op jit(solution)/shard_map/ppermute | solution.py:44
  114.0 9.9 %collective-permute-start.33 = (bf16[32,2048]{1,0:T(8,128)(2,1)S(1)}, bf16[32,2048]{1,0:T(8,128)(2,1)S(1)}, u32[]{:S(2)}, u32[]{:S(2)}) collective-permute-start(bf16[32,2048]{1,0:T(8,128)(2,1)S(1)} %get-tuple-element.83), channel_id=1, source_target_pairs={{0,8},{4,12},{8,0},{12,4},{1,9},{5,13},{9,1},{13,5},{2,10},{6,14},... | collective-permute-start | bytes 393224 | tf_op jit(solution)/shard_map/ppermute | solution.py:44
  114.4 13.6 %collective-permute-start.37 = (bf16[32,2048]{1,0:T(8,128)(2,1)S(1)}, bf16[32,2048]{1,0:T(8,128)(2,1)S(1)}, u32[]{:S(2)}, u32[]{:S(2)}) collective-permute-start(bf16[32,2048]{1,0:T(8,128)(2,1)S(1)} %get-tuple-element.81), channel_id=1, source_target_pairs={{0,8},{4,12},{8,0},{12,4},{1,9},{5,13},{9,1},{13,5},{2,10},{6,14},... | collective-permute-start | bytes 393224 | tf_op jit(solution)/shard_map/ppermute | solution.py:44
  124.1 10.2 %collective-permute-start.32 = (bf16[32,2048]{1,0:T(8,128)(2,1)S(1)}, bf16[32,2048]{1,0:T(8,128)(2,1)S(1)}, u32[]{:S(2)}, u32[]{:S(2)}) collective-permute-start(bf16[32,2048]{1,0:T(8,128)(2,1)S(1)} %get-tuple-element.77), channel_id=1, source_target_pairs={{0,2},{1,3},{2,0},{3,1},{4,6},{5,7},{6,4},{7,5},{8,10},{9,11},{10,... | collective-permute-start | bytes 393224 | tf_op jit(solution)/shard_map/ppermute | solution.py:40
  124.1 10.2 %collective-permute-start.36 = (bf16[32,2048]{1,0:T(8,128)(2,1)S(1)}, bf16[32,2048]{1,0:T(8,128)(2,1)S(1)}, u32[]{:S(2)}, u32[]{:S(2)}) collective-permute-start(bf16[32,2048]{1,0:T(8,128)(2,1)S(1)} %get-tuple-element.78), channel_id=1, source_target_pairs={{0,1},{1,2},{2,3},{3,0},{4,5},{5,6},{6,7},{7,4},{8,9},{9,10},{10,1... | collective-permute-start | bytes 393224 | tf_op jit(solution)/shard_map/ppermute | solution.py:40
  126.3 8.6 %collective-permute-start.34 = (bf16[32,2048]{1,0:T(8,128)(2,1)S(1)}, bf16[32,2048]{1,0:T(8,128)(2,1)S(1)}, u32[]{:S(2)}, u32[]{:S(2)}) collective-permute-start(bf16[32,2048]{1,0:T(8,128)(2,1)S(1)} %get-tuple-element.79), channel_id=1, source_target_pairs={{0,3},{1,0},{2,1},{3,2},{4,7},{5,4},{6,5},{7,6},{8,11},{9,8},{10,9... | collective-permute-start | bytes 393224 | tf_op jit(solution)/shard_map/ppermute | solution.py:40
  (10 other events, 16.3 us)

commit v4 on v3

--- a/solution.py
+++ b/solution.py
@@ -251,7 +251,7 @@
     sources = len(pieces[0])
     rows = arrays[0].shape[1]
     width = heads * HD
-    step = 512
+    step = 1024
 
     def body(*refs):
         held = refs[: len(arrays)]
@@ -291,6 +291,7 @@
         out_specs=[pl.BlockSpec((rows, step), lambda n: (0, n))] * chunks,
         out_shape=[jax.ShapeDtypeStruct((rows, D), bf16)] * chunks,
         scratch_shapes=[pltpu.VMEM((chunks * rows, width), bf16)],
+        compiler_params=pltpu.CompilerParams(vmem_limit_bytes=20 << 20),
         name="project",
     )(*arrays, in_hbm(weight))
 
@@ -322,6 +323,7 @@
             jax.ShapeDtypeStruct((rows, D), f32),
             jax.ShapeDtypeStruct((rows, D + (HD if experts else 0)), bf16),
         ],
+        compiler_params=pltpu.CompilerParams(vmem_limit_bytes=12 << 20),
         name="normalize",
     )(residual, *shares, gain, gates)
 

time: 136 us -> 130 us (0.956)
  local copies, waits for them, and re-layouts: 4.22 us -> 0.14 us
  Pallas kernels: 46.4 us -> 42.5 us
    unnamed x40 -> x10, local copies, waits for them, and re-layouts: 3.49 us -> 0.02 us
    pallas_call x1, Pallas kernels: 6.12 us -> 4.06 us  [project(): pl.pallas_call(body, grid=(D // step,), in_specs=[VM] * len(arrays) + [pl...]
    pallas_call x1, Pallas kernels: 2.04 us -> 0.19 us  [normalize(): pl.pallas_call(body, in_specs=[VM] * (len(shares) + 3), out_specs=[VM] *...]
    ppermute x21, starting transfers between devices: 30 us -> 31.6 us  [shifted(): lax.ppermute(array, axis, [(i, (i + by) % size) for i in range(size)])]
  transfers between devices with their start and end apart: 38 -> 38, of which waited for: 17 -> 16; matrix products, arithmetic and copies ran while one was open for 1% -> 0% of each run, Pallas kernels for 22% -> 23%
where the time goes in v4:
time: 130 us; the launch traced here: 129 us
  waiting for transfers between devices  45 us (35%)
  Pallas kernels  42.5 us (33%)
  starting transfers between devices  39.5 us (30%)
  other arithmetic  1.43 us (1%)
    ppermute x21, starting transfers between devices, shifted(): lax.ppermute(array, axis, [(i, (i + by) % size) for i in range(size)])  31.6 us
    pallas_call x3, Pallas kernels, attend(): pl.pallas_call(body, in_specs=[SM] * 3 + [HBM if own_first and n == 0 els...  30.4 us
    ppermute x21, waiting for transfers between devices, shifted(): lax.ppermute(array, axis, [(i, (i + by) % size) for i in range(size)])  29.1 us
    ppermute x17, waiting for transfers between devices, swapped(): lax.ppermute(array, axis, [(i, i ^ bit) for i in range(lax.axis_size(axis...  15.9 us
    ppermute x17, starting transfers between devices, swapped(): lax.ppermute(array, axis, [(i, i ^ bit) for i in range(lax.axis_size(axis...  7.83 us
    pallas_call x1, Pallas kernels, run_expert(): pl.pallas_call(body, grid=(steps,), in_specs=[SM] + [VM] * count + [pl.Bl...  7.8 us
    pallas_call x1, Pallas kernels, project(): pl.pallas_call(body, grid=(D // step,), in_specs=[VM] * len(arrays) + [pl...  4.06 us
  transfers between devices with their start and end apart: 38, of which 16 were waited for; matrix products, arithmetic and copies ran while one was open for 0% of the time, Pallas kernels for 23%

profile of v4, /device:TPU:0, one launch (start us, length us, event | category | flops | bytes accessed | tf_op | source)
XLA Modules:
  0.0 129.4 jit_solution(12602697160443743978)
XLA Ops:
  0.0 3.0 %collective-permute-start = (bf16[32,4096]{1,0:T(8,128)(2,1)}, bf16[32,4096]{1,0:T(8,128)(2,1)S(1)}, u32[]{:S(2)}, u32[]{:S(2)}) collective-permute-start(bf16[32,4096]{1,0:T(8,128)(2,1)} %refs_3_.1), channel_id=1, source_target_pairs={{0,1},{1,2},{2,3},{3,0},{4,5},{5,6},{6,7},{7,4},{8,9},{9,10},{10,1... | collective-permute-start | bytes 786440 | tf_op jit(solution)/shard_map/ppermute | solution.py:40
  3.0 2.0 %collective-permute-start.1 = (bf16[32,4096]{1,0:T(8,128)(2,1)}, bf16[32,4096]{1,0:T(8,128)(2,1)S(1)}, u32[]{:S(2)}, u32[]{:S(2)}) collective-permute-start(bf16[32,4096]{1,0:T(8,128)(2,1)} %refs_3_.1), channel_id=1, source_target_pairs={{0,3},{1,0},{2,1},{3,2},{4,7},{5,4},{6,5},{7,6},{8,11},{9,8},{10,9... | collective-permute-start | bytes 786440 | tf_op jit(solution)/shard_map/ppermute | solution.py:40
  5.8 8.8 %shard_map.127 = (bf16[1,32,1152]{2,1,0:T(8,128)(2,1)S(1)}, bf16[1,32,1152]{2,1,0:T(8,128)(2,1)S(1)}, bf16[1,32,1152]{2,1,0:T(8,128)(2,1)S(1)}, bf16[1,32,1152]{2,1,0:T(8,128)(2,1)S(1)}) custom-call(s32[2]{0:T(128)S(1)} %pad_add_fusion.refs_0_, s32[4]{0:T(128)S(1)} %and_select_fusion.refs_1_, s32[1]{0:T(128)} %bitcast.6.refs_2_, bf16[32,4096]{1,0:T(8,128)(2,1)} %refs_3_.1, ...), custom_call_target="tpu_custom_call" | custom-call | flops 17716740096 | bytes 8388608 | tf_op jit(solution)/shard_map/pallas_call | solution.py:207
  14.7 2.6 %collective-permute-start.3 = (bf16[1,32,1152]{2,1,0:T(8,128)(2,1)S(1)}, bf16[1,32,1152]{2,1,0:T(8,128)(2,1)S(1)}, u32[]{:S(2)}, u32[]{:S(2)}) collective-permute-start(bf16[1,32,1152]{2,1,0:T(8,128)(2,1)S(1)} %get-tuple-element.51), channel_id=1, source_target_pairs={{0,2},{1,3},{2,0},{3,1},{4,6},{5,7},{6,4},{7,5},{8,10},{9,11},{10,... | collective-permute-start | bytes 221192 | tf_op jit(solution)/shard_map/ppermute | solution.py:40
  17.3 1.3 %collective-permute-start.4 = (bf16[1,32,1152]{2,1,0:T(8,128)(2,1)S(1)}, bf16[1,32,1152]{2,1,0:T(8,128)(2,1)S(1)}, u32[]{:S(2)}, u32[]{:S(2)}) collective-permute-start(bf16[1,32,1152]{2,1,0:T(8,128)(2,1)S(1)} %get-tuple-element.52), channel_id=1, source_target_pairs={{0,3},{1,0},{2,1},{3,2},{4,7},{5,4},{6,5},{7,6},{8,11},{9,8},{10,9... | collective-permute-start | bytes 221192 | tf_op jit(solution)/shard_map/ppermute | solution.py:40
  18.7 2.0 %collective-permute-start.6 = (bf16[32,4096]{1,0:T(8,128)(2,1)S(1)}, bf16[32,4096]{1,0:T(8,128)(2,1)S(1)}, u32[]{:S(2)}, u32[]{:S(2)}) collective-permute-start(bf16[32,4096]{1,0:T(8,128)(2,1)S(1)} %copy-done.4), channel_id=1, source_target_pairs={{0,2},{1,3},{2,0},{3,1},{4,6},{5,7},{6,4},{7,5},{8,10},{9,11},{10,... | collective-permute-start | bytes 786440 | tf_op jit(solution)/shard_map/ppermute | solution.py:40
  20.7 12.9 %shard_map.128 = (bf16[2,32,1152]{2,1,0:T(8,128)(2,1)S(1)}, bf16[2,32,1152]{2,1,0:T(8,128)(2,1)S(1)}, bf16[2,32,1152]{2,1,0:T(8,128)(2,1)S(1)}, bf16[2,32,1152]{2,1,0:T(8,128)(2,1)S(1)}) custom-call(s32[2]{0:T(128)S(1)} %pad_add_fusion.refs_0_, s32[4]{0:T(128)S(1)} %and_select_fusion.refs_1_, s32[2]{0:T(128)S(1)} %pad_add_fusion.1.refs_2_, ...), custom_call_target="tpu_custom_call" | custom-call | flops 35433480192 | bytes 8388608 | tf_op jit(solution)/shard_map/pallas_call | solution.py:207
  33.6 3.8 %collective-permute-start.8 = (bf16[2,32,1152]{2,1,0:T(8,128)(2,1)S(1)}, bf16[2,32,1152]{2,1,0:T(8,128)(2,1)S(1)}, u32[]{:S(2)}, u32[]{:S(2)}) collective-permute-start(bf16[2,32,1152]{2,1,0:T(8,128)(2,1)S(1)} %get-tuple-element.58), channel_id=1, source_target_pairs={{0,3},{1,0},{2,1},{3,2},{4,7},{5,4},{6,5},{7,6},{8,11},{9,8},{10,9... | collective-permute-start | bytes 442376 | tf_op jit(solution)/shard_map/ppermute | solution.py:40
  37.5 8.7 %shard_map.129 = (bf16[1,32,1152]{2,1,0:T(8,128)(2,1)S(1)}, bf16[1,32,1152]{2,1,0:T(8,128)(2,1)S(1)}, bf16[1,32,1152]{2,1,0:T(8,128)(2,1)S(1)}, bf16[1,32,1152]{2,1,0:T(8,128)(2,1)S(1)}) custom-call(s32[2]{0:T(128)S(1)} %pad_add_fusion.refs_0_, s32[4]{0:T(128)S(1)} %and_select_fusion.refs_1_, s32[1]{0:T(128)} %bitcast.refs_2_, ...), custom_call_target="tpu_custom_call" | custom-call | flops 17716740096 | bytes 8388608 | tf_op jit(solution)/shard_map/pallas_call | solution.py:207
  46.2 3.0 %collective-permute-start.7 = (bf16[1,32,1152]{2,1,0:T(8,128)(2,1)S(1)}, bf16[1,32,1152]{2,1,0:T(8,128)(2,1)S(1)}, u32[]{:S(2)}, u32[]{:S(2)}) collective-permute-start(bf16[1,32,1152]{2,1,0:T(8,128)(2,1)S(1)} %get-tuple-element.57), channel_id=1, source_target_pairs={{0,2},{1,3},{2,0},{3,1},{4,6},{5,7},{6,4},{7,5},{8,10},{9,11},{10,... | collective-permute-start | bytes 221192 | tf_op jit(solution)/shard_map/ppermute | solution.py:40
  49.2 2.0 %collective-permute-start.11 = (bf16[1,32,1152]{2,1,0:T(8,128)(2,1)S(1)}, bf16[1,32,1152]{2,1,0:T(8,128)(2,1)S(1)}, u32[]{:S(2)}, u32[]{:S(2)}) collective-permute-start(bf16[1,32,1152]{2,1,0:T(8,128)(2,1)S(1)} %get-tuple-element.65), channel_id=1, source_target_pairs={{0,1},{1,2},{2,3},{3,0},{4,5},{5,6},{6,7},{7,4},{8,9},{9,10},{10,1... | collective-permute-start | bytes 221192 | tf_op jit(solution)/shard_map/ppermute | solution.py:40
  51.2 1.9 %collective-permute-done.7.refs_2_ = bf16[1,32,1152]{2,1,0:T(8,128)(2,1)S(1)} collective-permute-done((bf16[1,32,1152]{2,1,0:T(8,128)(2,1)S(1)}, bf16[1,32,1152]{2,1,0:T(8,128)(2,1)S(1)}, u32[]{:S(2)}, u32[]{:S(2)}) %collective-permute-start.7) | collective-permute-done | bytes 73760 | tf_op jit(solution)/shard_map/ppermute | solution.py:40
  53.1 0.8 collective-permute-done.10.refs_7_
  53.9 1.5 %collective-permute-done.11.refs_10_ = bf16[1,32,1152]{2,1,0:T(8,128)(2,1)S(1)} collective-permute-done((bf16[1,32,1152]{2,1,0:T(8,128)(2,1)S(1)}, bf16[1,32,1152]{2,1,0:T(8,128)(2,1)S(1)}, u32[]{:S(2)}, u32[]{:S(2)}) %collective-permute-start.11) | collective-permute-done | bytes 73760 | tf_op jit(solution)/shard_map/ppermute | solution.py:40
  55.4 4.1 %project.1 = (bf16[32,2048]{1,0:T(8,128)(2,1)S(1)}, bf16[32,2048]{1,0:T(8,128)(2,1)S(1)}, bf16[32,2048]{1,0:T(8,128)(2,1)S(1)}, bf16[32,2048]{1,0:T(8,128)(2,1)S(1)}) custom-call(bf16[1,32,1152]{2,1,0:T(8,128)(2,1)S(1)} %get-tuple-element.53.refs_0_, bf16[2,32,1152]{2,1,0:T(8,128)(2,1)S(1)} %collective-permute-done.5.refs_1_, ...), custom_call_target="tpu_custom_call" | custom-call | tf_op jit(solution)/shard_map/project/pallas_call | solution.py:287
  59.4 1.0 collective-permute-start.12
  60.4 0.8 collective-permute-start.13
  61.2 1.0 collective-permute-start.14
  62.3 3.4 %collective-permute-done.12.refs_1_ = bf16[32,2048]{1,0:T(8,128)(2,1)S(1)} collective-permute-done((bf16[32,2048]{1,0:T(8,128)(2,1)S(1)}, bf16[32,2048]{1,0:T(8,128)(2,1)S(1)}, u32[]{:S(2)}, u32[]{:S(2)}) %collective-permute-start.12) | collective-permute-done | bytes 131104 | tf_op jit(solution)/shard_map/ppermute | solution.py:40
  65.7 4.2 %collective-permute-done.13.refs_2_ = bf16[32,2048]{1,0:T(8,128)(2,1)S(1)} collective-permute-done((bf16[32,2048]{1,0:T(8,128)(2,1)S(1)}, bf16[32,2048]{1,0:T(8,128)(2,1)S(1)}, u32[]{:S(2)}, u32[]{:S(2)}) %collective-permute-start.13) | collective-permute-done | bytes 131104 | tf_op jit(solution)/shard_map/ppermute | solution.py:40
  69.9 0.2 normalize.1
  70.1 1.7 %collective-permute-start.21 = (bf16[32,2176]{1,0:T(8,128)(2,1)S(1)}, bf16[32,2176]{1,0:T(8,128)(2,1)S(1)}, u32[]{:S(2)}, u32[]{:S(2)}) collective-permute-start(bf16[32,2176]{1,0:T(8,128)(2,1)S(1)} %get-tuple-element.72.refs_3_), channel_id=1, source_target_pairs={{0,8},{4,12},{8,0},{12,4},{1,9},{5,13},{9,1},{13,5},{2,10},{6,14},... | collective-permute-start | bytes 417800 | tf_op jit(solution)/shard_map/ppermute | solution.py:44
  71.8 2.6 %collective-permute-start.17 = (bf16[32,2176]{1,0:T(8,128)(2,1)S(1)}, bf16[32,2176]{1,0:T(8,128)(2,1)S(1)}, u32[]{:S(2)}, u32[]{:S(2)}) collective-permute-start(bf16[32,2176]{1,0:T(8,128)(2,1)S(1)} %get-tuple-element.72.refs_3_), channel_id=1, source_target_pairs={{0,3},{1,0},{2,1},{3,2},{4,7},{5,4},{6,5},{7,6},{8,11},{9,8},{10,9... | collective-permute-start | bytes 417800 | tf_op jit(solution)/shard_map/ppermute | solution.py:40
  74.4 2.5 %collective-permute-start.15 = (bf16[32,2176]{1,0:T(8,128)(2,1)S(1)}, bf16[32,2176]{1,0:T(8,128)(2,1)S(1)}, u32[]{:S(2)}, u32[]{:S(2)}) collective-permute-start(bf16[32,2176]{1,0:T(8,128)(2,1)S(1)} %get-tuple-element.72.refs_3_), channel_id=1, source_target_pairs={{0,2},{1,3},{2,0},{3,1},{4,6},{5,7},{6,4},{7,5},{8,10},{9,11},{10,... | collective-permute-start | bytes 417800 | tf_op jit(solution)/shard_map/ppermute | solution.py:40
  76.9 1.5 %collective-permute-done.17.refs_2_ = bf16[32,2176]{1,0:T(8,128)(2,1)S(1)} collective-permute-done((bf16[32,2176]{1,0:T(8,128)(2,1)S(1)}, bf16[32,2176]{1,0:T(8,128)(2,1)S(1)}, u32[]{:S(2)}, u32[]{:S(2)}) %collective-permute-start.17) | collective-permute-done | bytes 139296 | tf_op jit(solution)/shard_map/ppermute | solution.py:40
  78.5 4.2 %collective-permute-done.16.refs_1_ = bf16[32,2176]{1,0:T(8,128)(2,1)S(1)} collective-permute-done((bf16[32,2176]{1,0:T(8,128)(2,1)S(1)}, bf16[32,2176]{1,0:T(8,128)(2,1)S(1)}, u32[]{:S(2)}, u32[]{:S(2)}) %collective-permute-start.16) | collective-permute-done | bytes 139296 | tf_op jit(solution)/shard_map/ppermute | solution.py:40
  82.8 0.6 collective-permute-start.19
  83.4 4.0 %collective-permute-done.15.refs_0_ = bf16[32,2176]{1,0:T(8,128)(2,1)S(1)} collective-permute-done((bf16[32,2176]{1,0:T(8,128)(2,1)S(1)}, bf16[32,2176]{1,0:T(8,128)(2,1)S(1)}, u32[]{:S(2)}, u32[]{:S(2)}) %collective-permute-start.15) | collective-permute-done | bytes 139296 | tf_op jit(solution)/shard_map/ppermute | solution.py:40
  87.5 0.5 collective-permute-start.22
  88.0 0.4 collective-permute-start.27
  88.5 4.2 %collective-permute-done.18.refs_4_ = bf16[32,2176]{1,0:T(8,128)(2,1)S(1)} collective-permute-done((bf16[32,2176]{1,0:T(8,128)(2,1)S(1)}, bf16[32,2176]{1,0:T(8,128)(2,1)S(1)}, u32[]{:S(2)}, u32[]{:S(2)}) %collective-permute-start.18) | collective-permute-done | bytes 139296 | tf_op jit(solution)/shard_map/ppermute | solution.py:44
  92.7 1.3 %collective-permute-done.26.refs_12_ = bf16[32,2176]{1,0:T(8,128)(2,1)S(1)} collective-permute-done((bf16[32,2176]{1,0:T(8,128)(2,1)S(1)}, bf16[32,2176]{1,0:T(8,128)(2,1)S(1)}, u32[]{:S(2)}, u32[]{:S(2)}) %collective-permute-start.26) | collective-permute-done | bytes 139296 | tf_op jit(solution)/shard_map/ppermute | solution.py:44
  94.0 7.8 %run_expert.1 = (f32[256,2048]{1,0:T(8,128)S(1)}, bf16[256,2048]{1,0:T(8,128)(2,1)S(1)}) custom-call(s32[1]{0:T(128)} %bitcast.11.expert_ref, bf16[32,2176]{1,0:T(8,128)(2,1)S(1)} %collective-permute-done.15.refs_0_, bf16[32,2176]{1,0:T(8,128)(2,1)S(1)} %collective-permute-done.16.refs_1_, bf16[32,2176]{1,0:T(8,128)(2,1)S(1)} %collective-permute-done.17.refs_2_, ...), custom_call_target="tpu_custom_call" | custom-call | tf_op jit(solution)/shard_map/run_expert/pallas_call | solution.py:372
  101.8 0.2 collective-permute-start.30
  102.0 2.5 %collective-permute-done.30 = bf16[256,2048]{1,0:T(8,128)(2,1)S(1)} collective-permute-done((bf16[256,2048]{1,0:T(8,128)(2,1)S(1)}, bf16[256,2048]{1,0:T(8,128)(2,1)S(1)}, u32[]{:S(2)}, u32[]{:S(2)}) %collective-permute-start.30) | collective-permute-done | bytes 1048608 | tf_op jit(solution)/shard_map/ppermute | solution.py:44
  104.5 0.4 fusion.7
  105.0 0.3 collective-permute-start.31
  105.4 1.7 %collective-permute-start.35 = (bf16[32,2048]{1,0:T(8,128)(2,1)S(1)}, bf16[32,2048]{1,0:T(8,128)(2,1)S(1)}, u32[]{:S(2)}, u32[]{:S(2)}) collective-permute-start(bf16[32,2048]{1,0:T(8,128)(2,1)S(1)} %get-tuple-element.82), channel_id=1, source_target_pairs={{0,8},{4,12},{8,0},{12,4},{1,9},{5,13},{9,1},{13,5},{2,10},{6,14},... | collective-permute-start | bytes 393224 | tf_op jit(solution)/shard_map/ppermute | solution.py:44
  107.1 0.3 collective-permute-start.33
  107.4 1.7 %collective-permute-start.37 = (bf16[32,2048]{1,0:T(8,128)(2,1)S(1)}, bf16[32,2048]{1,0:T(8,128)(2,1)S(1)}, u32[]{:S(2)}, u32[]{:S(2)}) collective-permute-start(bf16[32,2048]{1,0:T(8,128)(2,1)S(1)} %get-tuple-element.81), channel_id=1, source_target_pairs={{0,8},{4,12},{8,0},{12,4},{1,9},{5,13},{9,1},{13,5},{2,10},{6,14},... | collective-permute-start | bytes 393224 | tf_op jit(solution)/shard_map/ppermute | solution.py:44
  109.1 2.3 %collective-permute-done.31 = bf16[32,2048]{1,0:T(8,128)(2,1)S(1)} collective-permute-done((bf16[32,2048]{1,0:T(8,128)(2,1)S(1)}, bf16[32,2048]{1,0:T(8,128)(2,1)S(1)}, u32[]{:S(2)}, u32[]{:S(2)}) %collective-permute-start.31) | collective-permute-done | bytes 131104 | tf_op jit(solution)/shard_map/ppermute | solution.py:44
  111.4 2.8 %collective-permute-done.35 = bf16[32,2048]{1,0:T(8,128)(2,1)S(1)} collective-permute-done((bf16[32,2048]{1,0:T(8,128)(2,1)S(1)}, bf16[32,2048]{1,0:T(8,128)(2,1)S(1)}, u32[]{:S(2)}, u32[]{:S(2)}) %collective-permute-start.35) | collective-permute-done | bytes 131104 | tf_op jit(solution)/shard_map/ppermute | solution.py:44
  114.2 2.8 %collective-permute-done.33 = bf16[32,2048]{1,0:T(8,128)(2,1)S(1)} collective-permute-done((bf16[32,2048]{1,0:T(8,128)(2,1)S(1)}, bf16[32,2048]{1,0:T(8,128)(2,1)S(1)}, u32[]{:S(2)}, u32[]{:S(2)}) %collective-permute-start.33) | collective-permute-done | bytes 131104 | tf_op jit(solution)/shard_map/ppermute | solution.py:44
  117.2 2.8 %collective-permute-start.36 = (bf16[32,2048]{1,0:T(8,128)(2,1)S(1)}, bf16[32,2048]{1,0:T(8,128)(2,1)S(1)}, u32[]{:S(2)}, u32[]{:S(2)}) collective-permute-start(bf16[32,2048]{1,0:T(8,128)(2,1)S(1)} %get-tuple-element.78), channel_id=1, source_target_pairs={{0,1},{1,2},{2,3},{3,0},{4,5},{5,6},{6,7},{7,4},{8,9},{9,10},{10,1... | collective-permute-start | bytes 393224 | tf_op jit(solution)/shard_map/ppermute | solution.py:40
  120.0 1.1 collective-permute-start.34
  121.1 6.2 %collective-permute-done.32 = bf16[32,2048]{1,0:T(8,128)(2,1)S(1)} collective-permute-done((bf16[32,2048]{1,0:T(8,128)(2,1)S(1)}, bf16[32,2048]{1,0:T(8,128)(2,1)S(1)}, u32[]{:S(2)}, u32[]{:S(2)}) %collective-permute-start.32) | collective-permute-done | bytes 131104 | tf_op jit(solution)/shard_map/ppermute | solution.py:40
  127.3 1.3 %collective-permute-done.34 = bf16[32,2048]{1,0:T(8,128)(2,1)S(1)} collective-permute-done((bf16[32,2048]{1,0:T(8,128)(2,1)S(1)}, bf16[32,2048]{1,0:T(8,128)(2,1)S(1)}, u32[]{:S(2)}, u32[]{:S(2)}) %collective-permute-start.34) | collective-permute-done | bytes 131104 | tf_op jit(solution)/shard_map/ppermute | solution.py:40
  128.7 0.8 fusion.2
  (55 shorter events, 0.9 us)
Async XLA Ops:
  0.0 18.7 %collective-permute-start = (bf16[32,4096]{1,0:T(8,128)(2,1)}, bf16[32,4096]{1,0:T(8,128)(2,1)S(1)}, u32[]{:S(2)}, u32[]{:S(2)}) collective-permute-start(bf16[32,4096]{1,0:T(8,128)(2,1)} %refs_3_.1), channel_id=1, source_target_pairs={{0,1},{1,2},{2,3},{3,0},{4,5},{5,6},{6,7},{7,4},{8,9},{9,10},{10,1... | collective-permute-start | bytes 786440 | tf_op jit(solution)/shard_map/ppermute | solution.py:40
  3.0 15.6 %collective-permute-start.1 = (bf16[32,4096]{1,0:T(8,128)(2,1)}, bf16[32,4096]{1,0:T(8,128)(2,1)S(1)}, u32[]{:S(2)}, u32[]{:S(2)}) collective-permute-start(bf16[32,4096]{1,0:T(8,128)(2,1)} %refs_3_.1), channel_id=1, source_target_pairs={{0,3},{1,0},{2,1},{3,2},{4,7},{5,4},{6,5},{7,6},{8,11},{9,8},{10,9... | collective-permute-start | bytes 786440 | tf_op jit(solution)/shard_map/ppermute | solution.py:40
  5.8 12.9 %copy-start.4 = (bf16[32,4096]{1,0:T(8,128)(2,1)S(1)}, bf16[32,4096]{1,0:T(8,128)(2,1)}, u32[]{:S(2)}) copy-start(bf16[32,4096]{1,0:T(8,128)(2,1)} %refs_3_.1) | copy-start | bytes 786436
  14.7 18.8 %collective-permute-start.2 = (bf16[1,32,1152]{2,1,0:T(8,128)(2,1)S(1)}, bf16[1,32,1152]{2,1,0:T(8,128)(2,1)S(1)}, u32[]{:S(2)}, u32[]{:S(2)}) collective-permute-start(bf16[1,32,1152]{2,1,0:T(8,128)(2,1)S(1)} %get-tuple-element.50), channel_id=1, source_target_pairs={{0,1},{1,2},{2,3},{3,0},{4,5},{5,6},{6,7},{7,4},{8,9},{9,10},{10,1... | collective-permute-start | bytes 221192 | tf_op jit(solution)/shard_map/ppermute | solution.py:40
  14.7 18.8 %collective-permute-start.3 = (bf16[1,32,1152]{2,1,0:T(8,128)(2,1)S(1)}, bf16[1,32,1152]{2,1,0:T(8,128)(2,1)S(1)}, u32[]{:S(2)}, u32[]{:S(2)}) collective-permute-start(bf16[1,32,1152]{2,1,0:T(8,128)(2,1)S(1)} %get-tuple-element.51), channel_id=1, source_target_pairs={{0,2},{1,3},{2,0},{3,1},{4,6},{5,7},{6,4},{7,5},{8,10},{9,11},{10,... | collective-permute-start | bytes 221192 | tf_op jit(solution)/shard_map/ppermute | solution.py:40
  17.3 16.3 %collective-permute-start.4 = (bf16[1,32,1152]{2,1,0:T(8,128)(2,1)S(1)}, bf16[1,32,1152]{2,1,0:T(8,128)(2,1)S(1)}, u32[]{:S(2)}, u32[]{:S(2)}) collective-permute-start(bf16[1,32,1152]{2,1,0:T(8,128)(2,1)S(1)} %get-tuple-element.52), channel_id=1, source_target_pairs={{0,3},{1,0},{2,1},{3,2},{4,7},{5,4},{6,5},{7,6},{8,11},{9,8},{10,9... | collective-permute-start | bytes 221192 | tf_op jit(solution)/shard_map/ppermute | solution.py:40
  18.7 18.8 %collective-permute-start.6 = (bf16[32,4096]{1,0:T(8,128)(2,1)S(1)}, bf16[32,4096]{1,0:T(8,128)(2,1)S(1)}, u32[]{:S(2)}, u32[]{:S(2)}) collective-permute-start(bf16[32,4096]{1,0:T(8,128)(2,1)S(1)} %copy-done.4), channel_id=1, source_target_pairs={{0,2},{1,3},{2,0},{3,1},{4,6},{5,7},{6,4},{7,5},{8,10},{9,11},{10,... | collective-permute-start | bytes 786440 | tf_op jit(solution)/shard_map/ppermute | solution.py:40
  33.6 15.6 %collective-permute-start.5 = (bf16[2,32,1152]{2,1,0:T(8,128)(2,1)S(1)}, bf16[2,32,1152]{2,1,0:T(8,128)(2,1)S(1)}, u32[]{:S(2)}, u32[]{:S(2)}) collective-permute-start(bf16[2,32,1152]{2,1,0:T(8,128)(2,1)S(1)} %get-tuple-element.54), channel_id=1, source_target_pairs={{0,1},{1,2},{2,3},{3,0},{4,5},{5,6},{6,7},{7,4},{8,9},{9,10},{10,1... | collective-permute-start | bytes 442376 | tf_op jit(solution)/shard_map/ppermute | solution.py:40
  33.6 17.6 %collective-permute-start.8 = (bf16[2,32,1152]{2,1,0:T(8,128)(2,1)S(1)}, bf16[2,32,1152]{2,1,0:T(8,128)(2,1)S(1)}, u32[]{:S(2)}, u32[]{:S(2)}) collective-permute-start(bf16[2,32,1152]{2,1,0:T(8,128)(2,1)S(1)} %get-tuple-element.58), channel_id=1, source_target_pairs={{0,3},{1,0},{2,1},{3,2},{4,7},{5,4},{6,5},{7,6},{8,11},{9,8},{10,9... | collective-permute-start | bytes 442376 | tf_op jit(solution)/shard_map/ppermute | solution.py:40
  37.5 13.8 %collective-permute-start.9 = (bf16[2,32,1152]{2,1,0:T(8,128)(2,1)S(1)}, bf16[2,32,1152]{2,1,0:T(8,128)(2,1)S(1)}, u32[]{:S(2)}, u32[]{:S(2)}) collective-permute-start(bf16[2,32,1152]{2,1,0:T(8,128)(2,1)S(1)} %get-tuple-element.61), channel_id=1, source_target_pairs={{0,2},{1,3},{2,0},{3,1},{4,6},{5,7},{6,4},{7,5},{8,10},{9,11},{10,... | collective-permute-start | bytes 442376 | tf_op jit(solution)/shard_map/ppermute | solution.py:40
  46.2 6.9 %collective-permute-start.7 = (bf16[1,32,1152]{2,1,0:T(8,128)(2,1)S(1)}, bf16[1,32,1152]{2,1,0:T(8,128)(2,1)S(1)}, u32[]{:S(2)}, u32[]{:S(2)}) collective-permute-start(bf16[1,32,1152]{2,1,0:T(8,128)(2,1)S(1)} %get-tuple-element.57), channel_id=1, source_target_pairs={{0,2},{1,3},{2,0},{3,1},{4,6},{5,7},{6,4},{7,5},{8,10},{9,11},{10,... | collective-permute-start | bytes 221192 | tf_op jit(solution)/shard_map/ppermute | solution.py:40
  49.2 4.7 %collective-permute-start.10 = (bf16[1,32,1152]{2,1,0:T(8,128)(2,1)S(1)}, bf16[1,32,1152]{2,1,0:T(8,128)(2,1)S(1)}, u32[]{:S(2)}, u32[]{:S(2)}) collective-permute-start(bf16[1,32,1152]{2,1,0:T(8,128)(2,1)S(1)} %get-tuple-element.62), channel_id=1, source_target_pairs={{0,3},{1,0},{2,1},{3,2},{4,7},{5,4},{6,5},{7,6},{8,11},{9,8},{10,9... | collective-permute-start | bytes 221192 | tf_op jit(solution)/shard_map/ppermute | solution.py:40
  49.2 6.2 %collective-permute-start.11 = (bf16[1,32,1152]{2,1,0:T(8,128)(2,1)S(1)}, bf16[1,32,1152]{2,1,0:T(8,128)(2,1)S(1)}, u32[]{:S(2)}, u32[]{:S(2)}) collective-permute-start(bf16[1,32,1152]{2,1,0:T(8,128)(2,1)S(1)} %get-tuple-element.65), channel_id=1, source_target_pairs={{0,1},{1,2},{2,3},{3,0},{4,5},{5,6},{6,7},{7,4},{8,9},{9,10},{10,1... | collective-permute-start | bytes 221192 | tf_op jit(solution)/shard_map/ppermute | solution.py:40
  55.3 6.8 %copy-start.2 = (f32[32,8]{0,1:T(8,128)S(1)}, f32[32,8]{0,1:T(8,128)}, u32[]{:S(2)}) copy-start(f32[32,8]{0,1:T(8,128)} %param.25) | copy-start | bytes 3076
  55.4 6.8 %copy-start.3 = (s32[32,8]{0,1:T(8,128)S(1)}, s32[32,8]{0,1:T(8,128)}, u32[]{:S(2)}) copy-start(s32[32,8]{0,1:T(8,128)} %param.24) | copy-start | bytes 3076
  55.4 14.6 %copy-start = (bf16[32,2048]{1,0:T(8,128)(2,1)S(1)}, bf16[32,2048]{1,0:T(8,128)(2,1)}, u32[]{:S(2)}) copy-start(bf16[32,2048]{1,0:T(8,128)(2,1)} %residual_ref.1) | copy-start | bytes 393220
  55.4 14.6 %copy-start.1 = (f32[2048]{0:T(1024)S(1)}, f32[2048]{0:T(1024)}, u32[]{:S(2)}) copy-start(f32[2048]{0:T(1024)} %param.21) | copy-start | bytes 24580
  59.4 6.3 %collective-permute-start.12 = (bf16[32,2048]{1,0:T(8,128)(2,1)S(1)}, bf16[32,2048]{1,0:T(8,128)(2,1)S(1)}, u32[]{:S(2)}, u32[]{:S(2)}) collective-permute-start(bf16[32,2048]{1,0:T(8,128)(2,1)S(1)} %get-tuple-element.68), channel_id=1, source_target_pairs={{0,3},{1,0},{2,1},{3,2},{4,7},{5,4},{6,5},{7,6},{8,11},{9,8},{10,9... | collective-permute-start | bytes 393224 | tf_op jit(solution)/shard_map/ppermute | solution.py:40
  60.4 9.5 %collective-permute-start.13 = (bf16[32,2048]{1,0:T(8,128)(2,1)S(1)}, bf16[32,2048]{1,0:T(8,128)(2,1)S(1)}, u32[]{:S(2)}, u32[]{:S(2)}) collective-permute-start(bf16[32,2048]{1,0:T(8,128)(2,1)S(1)} %get-tuple-element.69), channel_id=1, source_target_pairs={{0,2},{1,3},{2,0},{3,1},{4,6},{5,7},{6,4},{7,5},{8,10},{9,11},{10,... | collective-permute-start | bytes 393224 | tf_op jit(solution)/shard_map/ppermute | solution.py:40
  61.2 8.8 %collective-permute-start.14 = (bf16[32,2048]{1,0:T(8,128)(2,1)S(1)}, bf16[32,2048]{1,0:T(8,128)(2,1)S(1)}, u32[]{:S(2)}, u32[]{:S(2)}) collective-permute-start(bf16[32,2048]{1,0:T(8,128)(2,1)S(1)} %get-tuple-element.70), channel_id=1, source_target_pairs={{0,1},{1,2},{2,3},{3,0},{4,5},{5,6},{6,7},{7,4},{8,9},{9,10},{10,1... | collective-permute-start | bytes 393224 | tf_op jit(solution)/shard_map/ppermute | solution.py:40
  70.1 6.8 %collective-permute-start.21 = (bf16[32,2176]{1,0:T(8,128)(2,1)S(1)}, bf16[32,2176]{1,0:T(8,128)(2,1)S(1)}, u32[]{:S(2)}, u32[]{:S(2)}) collective-permute-start(bf16[32,2176]{1,0:T(8,128)(2,1)S(1)} %get-tuple-element.72.refs_3_), channel_id=1, source_target_pairs={{0,8},{4,12},{8,0},{12,4},{1,9},{5,13},{9,1},{13,5},{2,10},{6,14},... | collective-permute-start | bytes 417800 | tf_op jit(solution)/shard_map/ppermute | solution.py:44
  71.8 6.7 %collective-permute-start.17 = (bf16[32,2176]{1,0:T(8,128)(2,1)S(1)}, bf16[32,2176]{1,0:T(8,128)(2,1)S(1)}, u32[]{:S(2)}, u32[]{:S(2)}) collective-permute-start(bf16[32,2176]{1,0:T(8,128)(2,1)S(1)} %get-tuple-element.72.refs_3_), channel_id=1, source_target_pairs={{0,3},{1,0},{2,1},{3,2},{4,7},{5,4},{6,5},{7,6},{8,11},{9,8},{10,9... | collective-permute-start | bytes 417800 | tf_op jit(solution)/shard_map/ppermute | solution.py:40
  74.4 4.1 %collective-permute-start.25 = (bf16[32,2176]{1,0:T(8,128)(2,1)S(1)}, bf16[32,2176]{1,0:T(8,128)(2,1)S(1)}, u32[]{:S(2)}, u32[]{:S(2)}) collective-permute-start(bf16[32,2176]{1,0:T(8,128)(2,1)S(1)} %get-tuple-element.72.refs_3_), channel_id=1, source_target_pairs={{0,4},{4,0},{8,12},{12,8},{1,5},{5,1},{9,13},{13,9},{2,6},{6,2},{1... | collective-permute-start | bytes 417800 | tf_op jit(solution)/shard_map/ppermute | solution.py:44
  74.4 8.4 %collective-permute-start.16 = (bf16[32,2176]{1,0:T(8,128)(2,1)S(1)}, bf16[32,2176]{1,0:T(8,128)(2,1)S(1)}, u32[]{:S(2)}, u32[]{:S(2)}) collective-permute-start(bf16[32,2176]{1,0:T(8,128)(2,1)S(1)} %get-tuple-element.72.refs_3_), channel_id=1, source_target_pairs={{0,1},{1,2},{2,3},{3,0},{4,5},{5,6},{6,7},{7,4},{8,9},{9,10},{10,1... | collective-permute-start | bytes 417800 | tf_op jit(solution)/shard_map/ppermute | solution.py:40
  74.4 13.0 %collective-permute-start.15 = (bf16[32,2176]{1,0:T(8,128)(2,1)S(1)}, bf16[32,2176]{1,0:T(8,128)(2,1)S(1)}, u32[]{:S(2)}, u32[]{:S(2)}) collective-permute-start(bf16[32,2176]{1,0:T(8,128)(2,1)S(1)} %get-tuple-element.72.refs_3_), channel_id=1, source_target_pairs={{0,2},{1,3},{2,0},{3,1},{4,6},{5,7},{6,4},{7,5},{8,10},{9,11},{10,... | collective-permute-start | bytes 417800 | tf_op jit(solution)/shard_map/ppermute | solution.py:40
  76.9 10.5 %collective-permute-start.29 = (bf16[32,2176]{1,0:T(8,128)(2,1)S(1)}, bf16[32,2176]{1,0:T(8,128)(2,1)S(1)}, u32[]{:S(2)}, u32[]{:S(2)}) collective-permute-start(bf16[32,2176]{1,0:T(8,128)(2,1)S(1)} %collective-permute-done.21.refs_7_), channel_id=1, source_target_pairs={{0,4},{4,0},{8,12},{12,8},{1,5},{5,1},{9,13},{13,9},{2,6},{6,2},{1... | collective-permute-start | bytes 417800 | tf_op jit(solution)/shard_map/ppermute | solution.py:44
  78.5 9.0 %collective-permute-start.24 = (bf16[32,2176]{1,0:T(8,128)(2,1)S(1)}, bf16[32,2176]{1,0:T(8,128)(2,1)S(1)}, u32[]{:S(2)}, u32[]{:S(2)}) collective-permute-start(bf16[32,2176]{1,0:T(8,128)(2,1)S(1)} %collective-permute-done.17.refs_2_), channel_id=1, source_target_pairs={{0,4},{4,0},{8,12},{12,8},{1,5},{5,1},{9,13},{13,9},{2,6},{6,2},{1... | collective-permute-start | bytes 417800 | tf_op jit(solution)/shard_map/ppermute | solution.py:44
  78.5 9.5 %collective-permute-start.20 = (bf16[32,2176]{1,0:T(8,128)(2,1)S(1)}, bf16[32,2176]{1,0:T(8,128)(2,1)S(1)}, u32[]{:S(2)}, u32[]{:S(2)}) collective-permute-start(bf16[32,2176]{1,0:T(8,128)(2,1)S(1)} %collective-permute-done.17.refs_2_), channel_id=1, source_target_pairs={{0,8},{4,12},{8,0},{12,4},{1,9},{5,13},{9,1},{13,5},{2,10},{6,14},... | collective-permute-start | bytes 417800 | tf_op jit(solution)/shard_map/ppermute | solution.py:44
  82.8 5.3 %collective-permute-start.19 = (bf16[32,2176]{1,0:T(8,128)(2,1)S(1)}, bf16[32,2176]{1,0:T(8,128)(2,1)S(1)}, u32[]{:S(2)}, u32[]{:S(2)}) collective-permute-start(bf16[32,2176]{1,0:T(8,128)(2,1)S(1)} %collective-permute-done.16.refs_1_), channel_id=1, source_target_pairs={{0,8},{4,12},{8,0},{12,4},{1,9},{5,13},{9,1},{13,5},{2,10},{6,14},... | collective-permute-start | bytes 417800 | tf_op jit(solution)/shard_map/ppermute | solution.py:44
  87.3 5.3 %collective-permute-start.18 = (bf16[32,2176]{1,0:T(8,128)(2,1)S(1)}, bf16[32,2176]{1,0:T(8,128)(2,1)S(1)}, u32[]{:S(2)}, u32[]{:S(2)}) collective-permute-start(bf16[32,2176]{1,0:T(8,128)(2,1)S(1)} %collective-permute-done.15.refs_0_), channel_id=1, source_target_pairs={{0,8},{4,12},{8,0},{12,4},{1,9},{5,13},{9,1},{13,5},{2,10},{6,14},... | collective-permute-start | bytes 417800 | tf_op jit(solution)/shard_map/ppermute | solution.py:44
  87.5 5.2 %collective-permute-start.23 = (bf16[32,2176]{1,0:T(8,128)(2,1)S(1)}, bf16[32,2176]{1,0:T(8,128)(2,1)S(1)}, u32[]{:S(2)}, u32[]{:S(2)}) collective-permute-start(bf16[32,2176]{1,0:T(8,128)(2,1)S(1)} %collective-permute-done.16.refs_1_), channel_id=1, source_target_pairs={{0,4},{4,0},{8,12},{12,8},{1,5},{5,1},{9,13},{13,9},{2,6},{6,2},{1... | collective-permute-start | bytes 417800 | tf_op jit(solution)/shard_map/ppermute | solution.py:44
  87.5 5.2 %collective-permute-start.22 = (bf16[32,2176]{1,0:T(8,128)(2,1)S(1)}, bf16[32,2176]{1,0:T(8,128)(2,1)S(1)}, u32[]{:S(2)}, u32[]{:S(2)}) collective-permute-start(bf16[32,2176]{1,0:T(8,128)(2,1)S(1)} %collective-permute-done.15.refs_0_), channel_id=1, source_target_pairs={{0,4},{4,0},{8,12},{12,8},{1,5},{5,1},{9,13},{13,9},{2,6},{6,2},{1... | collective-permute-start | bytes 417800 | tf_op jit(solution)/shard_map/ppermute | solution.py:44
  88.0 4.7 %collective-permute-start.28 = (bf16[32,2176]{1,0:T(8,128)(2,1)S(1)}, bf16[32,2176]{1,0:T(8,128)(2,1)S(1)}, u32[]{:S(2)}, u32[]{:S(2)}) collective-permute-start(bf16[32,2176]{1,0:T(8,128)(2,1)S(1)} %collective-permute-done.20.refs_6_), channel_id=1, source_target_pairs={{0,4},{4,0},{8,12},{12,8},{1,5},{5,1},{9,13},{13,9},{2,6},{6,2},{1... | collective-permute-start | bytes 417800 | tf_op jit(solution)/shard_map/ppermute | solution.py:44
  88.0 4.6 %collective-permute-start.27 = (bf16[32,2176]{1,0:T(8,128)(2,1)S(1)}, bf16[32,2176]{1,0:T(8,128)(2,1)S(1)}, u32[]{:S(2)}, u32[]{:S(2)}) collective-permute-start(bf16[32,2176]{1,0:T(8,128)(2,1)S(1)} %collective-permute-done.19.refs_5_), channel_id=1, source_target_pairs={{0,4},{4,0},{8,12},{12,8},{1,5},{5,1},{9,13},{13,9},{2,6},{6,2},{1... | collective-permute-start | bytes 417800 | tf_op jit(solution)/shard_map/ppermute | solution.py:44
  92.7 1.4 %collective-permute-start.26 = (bf16[32,2176]{1,0:T(8,128)(2,1)S(1)}, bf16[32,2176]{1,0:T(8,128)(2,1)S(1)}, u32[]{:S(2)}, u32[]{:S(2)}) collective-permute-start(bf16[32,2176]{1,0:T(8,128)(2,1)S(1)} %collective-permute-done.18.refs_4_), channel_id=1, source_target_pairs={{0,4},{4,0},{8,12},{12,8},{1,5},{5,1},{9,13},{13,9},{2,6},{6,2},{1... | collective-permute-start | bytes 417800 | tf_op jit(solution)/shard_map/ppermute | solution.py:44
  101.8 2.7 %collective-permute-start.30 = (bf16[256,2048]{1,0:T(8,128)(2,1)S(1)}, bf16[256,2048]{1,0:T(8,128)(2,1)S(1)}, u32[]{:S(2)}, u32[]{:S(2)}) collective-permute-start(bf16[256,2048]{1,0:T(8,128)(2,1)S(1)} %get-tuple-element.74), channel_id=1, source_target_pairs={{0,4},{4,0},{8,12},{12,8},{1,5},{5,1},{9,13},{13,9},{2,6},{6,2},{1... | collective-permute-start | bytes 3145736 | tf_op jit(solution)/shard_map/ppermute | solution.py:44
  105.0 6.4 %collective-permute-start.31 = (bf16[32,2048]{1,0:T(8,128)(2,1)S(1)}, bf16[32,2048]{1,0:T(8,128)(2,1)S(1)}, u32[]{:S(2)}, u32[]{:S(2)}) collective-permute-start(bf16[32,2048]{1,0:T(8,128)(2,1)S(1)} %get-tuple-element.80), channel_id=1, source_target_pairs={{0,8},{4,12},{8,0},{12,4},{1,9},{5,13},{9,1},{13,5},{2,10},{6,14},... | collective-permute-start | bytes 393224 | tf_op jit(solution)/shard_map/ppermute | solution.py:44
  105.4 8.9 %collective-permute-start.35 = (bf16[32,2048]{1,0:T(8,128)(2,1)S(1)}, bf16[32,2048]{1,0:T(8,128)(2,1)S(1)}, u32[]{:S(2)}, u32[]{:S(2)}) collective-permute-start(bf16[32,2048]{1,0:T(8,128)(2,1)S(1)} %get-tuple-element.82), channel_id=1, source_target_pairs={{0,8},{4,12},{8,0},{12,4},{1,9},{5,13},{9,1},{13,5},{2,10},{6,14},... | collective-permute-start | bytes 393224 | tf_op jit(solution)/shard_map/ppermute | solution.py:44
  107.1 9.9 %collective-permute-start.33 = (bf16[32,2048]{1,0:T(8,128)(2,1)S(1)}, bf16[32,2048]{1,0:T(8,128)(2,1)S(1)}, u32[]{:S(2)}, u32[]{:S(2)}) collective-permute-start(bf16[32,2048]{1,0:T(8,128)(2,1)S(1)} %get-tuple-element.83), channel_id=1, source_target_pairs={{0,8},{4,12},{8,0},{12,4},{1,9},{5,13},{9,1},{13,5},{2,10},{6,14},... | collective-permute-start | bytes 393224 | tf_op jit(solution)/shard_map/ppermute | solution.py:44
  107.4 13.7 %collective-permute-start.37 = (bf16[32,2048]{1,0:T(8,128)(2,1)S(1)}, bf16[32,2048]{1,0:T(8,128)(2,1)S(1)}, u32[]{:S(2)}, u32[]{:S(2)}) collective-permute-start(bf16[32,2048]{1,0:T(8,128)(2,1)S(1)} %get-tuple-element.81), channel_id=1, source_target_pairs={{0,8},{4,12},{8,0},{12,4},{1,9},{5,13},{9,1},{13,5},{2,10},{6,14},... | collective-permute-start | bytes 393224 | tf_op jit(solution)/shard_map/ppermute | solution.py:44
  117.1 10.2 %collective-permute-start.32 = (bf16[32,2048]{1,0:T(8,128)(2,1)S(1)}, bf16[32,2048]{1,0:T(8,128)(2,1)S(1)}, u32[]{:S(2)}, u32[]{:S(2)}) collective-permute-start(bf16[32,2048]{1,0:T(8,128)(2,1)S(1)} %get-tuple-element.77), channel_id=1, source_target_pairs={{0,2},{1,3},{2,0},{3,1},{4,6},{5,7},{6,4},{7,5},{8,10},{9,11},{10,... | collective-permute-start | bytes 393224 | tf_op jit(solution)/shard_map/ppermute | solution.py:40
  117.2 10.1 %collective-permute-start.36 = (bf16[32,2048]{1,0:T(8,128)(2,1)S(1)}, bf16[32,2048]{1,0:T(8,128)(2,1)S(1)}, u32[]{:S(2)}, u32[]{:S(2)}) collective-permute-start(bf16[32,2048]{1,0:T(8,128)(2,1)S(1)} %get-tuple-element.78), channel_id=1, source_target_pairs={{0,1},{1,2},{2,3},{3,0},{4,5},{5,6},{6,7},{7,4},{8,9},{9,10},{10,1... | collective-permute-start | bytes 393224 | tf_op jit(solution)/shard_map/ppermute | solution.py:40
  120.0 8.6 %collective-permute-start.34 = (bf16[32,2048]{1,0:T(8,128)(2,1)S(1)}, bf16[32,2048]{1,0:T(8,128)(2,1)S(1)}, u32[]{:S(2)}, u32[]{:S(2)}) collective-permute-start(bf16[32,2048]{1,0:T(8,128)(2,1)S(1)} %get-tuple-element.79), channel_id=1, source_target_pairs={{0,3},{1,0},{2,1},{3,2},{4,7},{5,4},{6,5},{7,6},{8,11},{9,8},{10,9... | collective-permute-start | bytes 393224 | tf_op jit(solution)/shard_map/ppermute | solution.py:40

commit v5 on v4

--- a/solution.py
+++ b/solution.py
@@ -222,7 +222,7 @@
             pltpu.SemaphoreType.DMA((2, block_count)),
             pltpu.SemaphoreType.DMA((3,)),
         ],
-        compiler_params=pltpu.CompilerParams(vmem_limit_bytes=12 * size * padded + (16 << 20)),
+        compiler_params=pltpu.CompilerParams(vmem_limit_bytes=10 * size * padded + (13 << 20)),
         cost_estimate=pl.CostEstimate(
             flops=block_count * size * padded * HD * 2 * 16,
             transcendentals=block_count * size * padded,
@@ -387,7 +387,7 @@
             pltpu.VMEM((FF, D), bf16),
             pltpu.SemaphoreType.DMA,
         ],
-        compiler_params=pltpu.CompilerParams(vmem_limit_bytes=36 << 20),
+        compiler_params=pltpu.CompilerParams(vmem_limit_bytes=28 << 20),
         name="run_expert",
     )(expert, *messages, in_hbm(gate_up), in_hbm(gate_up), in_hbm(down))
 

time: 130 us -> 130 us (level)
  no operation moved by 1% of the time
where the time goes in v5:
time: 130 us; the launch traced here: 129 us
  waiting for transfers between devices  45 us (35%)
  Pallas kernels  42.5 us (33%)
  starting transfers between devices  39.5 us (30%)
  other arithmetic  1.43 us (1%)
    ppermute x21, starting transfers between devices, shifted(): lax.ppermute(array, axis, [(i, (i + by) % size) for i in range(size)])  31.6 us
    pallas_call x3, Pallas kernels, attend(): pl.pallas_call(body, in_specs=[SM] * 3 + [HBM if own_first and n == 0 els...  30.4 us
    ppermute x21, waiting for transfers between devices, shifted(): lax.ppermute(array, axis, [(i, (i + by) % size) for i in range(size)])  29.1 us
    ppermute x17, waiting for transfers between devices, swapped(): lax.ppermute(array, axis, [(i, i ^ bit) for i in range(lax.axis_size(axis...  15.9 us
    ppermute x17, starting transfers between devices, swapped(): lax.ppermute(array, axis, [(i, i ^ bit) for i in range(lax.axis_size(axis...  7.83 us
    pallas_call x1, Pallas kernels, run_expert(): pl.pallas_call(body, grid=(steps,), in_specs=[SM] + [VM] * count + [pl.Bl...  7.8 us
    pallas_call x1, Pallas kernels, project(): pl.pallas_call(body, grid=(D // step,), in_specs=[VM] * len(arrays) + [pl...  4.06 us
  transfers between devices with their start and end apart: 38, of which 16 were waited for; matrix products, arithmetic and copies ran while one was open for 0% of the time, Pallas kernels for 23%

profile of v5, /device:TPU:0, one launch (start us, length us, event | category | flops | bytes accessed | tf_op | source)
XLA Modules:
  0.0 129.4 jit_solution(6503530135573974261)
XLA Ops:
  0.0 3.0 %collective-permute-start = (bf16[32,4096]{1,0:T(8,128)(2,1)}, bf16[32,4096]{1,0:T(8,128)(2,1)S(1)}, u32[]{:S(2)}, u32[]{:S(2)}) collective-permute-start(bf16[32,4096]{1,0:T(8,128)(2,1)} %refs_3_.1), channel_id=1, source_target_pairs={{0,1},{1,2},{2,3},{3,0},{4,5},{5,6},{6,7},{7,4},{8,9},{9,10},{10,1... | collective-permute-start | bytes 786440 | tf_op jit(solution)/shard_map/ppermute | solution.py:40
  3.0 2.0 %collective-permute-start.1 = (bf16[32,4096]{1,0:T(8,128)(2,1)}, bf16[32,4096]{1,0:T(8,128)(2,1)S(1)}, u32[]{:S(2)}, u32[]{:S(2)}) collective-permute-start(bf16[32,4096]{1,0:T(8,128)(2,1)} %refs_3_.1), channel_id=1, source_target_pairs={{0,3},{1,0},{2,1},{3,2},{4,7},{5,4},{6,5},{7,6},{8,11},{9,8},{10,9... | collective-permute-start | bytes 786440 | tf_op jit(solution)/shard_map/ppermute | solution.py:40
  5.8 8.8 %shard_map.127 = (bf16[1,32,1152]{2,1,0:T(8,128)(2,1)S(1)}, bf16[1,32,1152]{2,1,0:T(8,128)(2,1)S(1)}, bf16[1,32,1152]{2,1,0:T(8,128)(2,1)S(1)}, bf16[1,32,1152]{2,1,0:T(8,128)(2,1)S(1)}) custom-call(s32[2]{0:T(128)S(1)} %pad_add_fusion.refs_0_, s32[4]{0:T(128)S(1)} %and_select_fusion.refs_1_, s32[1]{0:T(128)} %bitcast.6.refs_2_, bf16[32,4096]{1,0:T(8,128)(2,1)} %refs_3_.1, ...), custom_call_target="tpu_custom_call" | custom-call | flops 17716740096 | bytes 8388608 | tf_op jit(solution)/shard_map/pallas_call | solution.py:207
  14.7 2.6 %collective-permute-start.3 = (bf16[1,32,1152]{2,1,0:T(8,128)(2,1)S(1)}, bf16[1,32,1152]{2,1,0:T(8,128)(2,1)S(1)}, u32[]{:S(2)}, u32[]{:S(2)}) collective-permute-start(bf16[1,32,1152]{2,1,0:T(8,128)(2,1)S(1)} %get-tuple-element.51), channel_id=1, source_target_pairs={{0,2},{1,3},{2,0},{3,1},{4,6},{5,7},{6,4},{7,5},{8,10},{9,11},{10,... | collective-permute-start | bytes 221192 | tf_op jit(solution)/shard_map/ppermute | solution.py:40
  17.3 1.3 %collective-permute-start.4 = (bf16[1,32,1152]{2,1,0:T(8,128)(2,1)S(1)}, bf16[1,32,1152]{2,1,0:T(8,128)(2,1)S(1)}, u32[]{:S(2)}, u32[]{:S(2)}) collective-permute-start(bf16[1,32,1152]{2,1,0:T(8,128)(2,1)S(1)} %get-tuple-element.52), channel_id=1, source_target_pairs={{0,3},{1,0},{2,1},{3,2},{4,7},{5,4},{6,5},{7,6},{8,11},{9,8},{10,9... | collective-permute-start | bytes 221192 | tf_op jit(solution)/shard_map/ppermute | solution.py:40
  18.7 2.0 %collective-permute-start.6 = (bf16[32,4096]{1,0:T(8,128)(2,1)S(1)}, bf16[32,4096]{1,0:T(8,128)(2,1)S(1)}, u32[]{:S(2)}, u32[]{:S(2)}) collective-permute-start(bf16[32,4096]{1,0:T(8,128)(2,1)S(1)} %copy-done.4), channel_id=1, source_target_pairs={{0,2},{1,3},{2,0},{3,1},{4,6},{5,7},{6,4},{7,5},{8,10},{9,11},{10,... | collective-permute-start | bytes 786440 | tf_op jit(solution)/shard_map/ppermute | solution.py:40
  20.7 12.9 %shard_map.128 = (bf16[2,32,1152]{2,1,0:T(8,128)(2,1)S(1)}, bf16[2,32,1152]{2,1,0:T(8,128)(2,1)S(1)}, bf16[2,32,1152]{2,1,0:T(8,128)(2,1)S(1)}, bf16[2,32,1152]{2,1,0:T(8,128)(2,1)S(1)}) custom-call(s32[2]{0:T(128)S(1)} %pad_add_fusion.refs_0_, s32[4]{0:T(128)S(1)} %and_select_fusion.refs_1_, s32[2]{0:T(128)S(1)} %pad_add_fusion.1.refs_2_, ...), custom_call_target="tpu_custom_call" | custom-call | flops 35433480192 | bytes 8388608 | tf_op jit(solution)/shard_map/pallas_call | solution.py:207
  33.6 3.8 %collective-permute-start.8 = (bf16[2,32,1152]{2,1,0:T(8,128)(2,1)S(1)}, bf16[2,32,1152]{2,1,0:T(8,128)(2,1)S(1)}, u32[]{:S(2)}, u32[]{:S(2)}) collective-permute-start(bf16[2,32,1152]{2,1,0:T(8,128)(2,1)S(1)} %get-tuple-element.58), channel_id=1, source_target_pairs={{0,3},{1,0},{2,1},{3,2},{4,7},{5,4},{6,5},{7,6},{8,11},{9,8},{10,9... | collective-permute-start | bytes 442376 | tf_op jit(solution)/shard_map/ppermute | solution.py:40
  37.5 8.7 %shard_map.129 = (bf16[1,32,1152]{2,1,0:T(8,128)(2,1)S(1)}, bf16[1,32,1152]{2,1,0:T(8,128)(2,1)S(1)}, bf16[1,32,1152]{2,1,0:T(8,128)(2,1)S(1)}, bf16[1,32,1152]{2,1,0:T(8,128)(2,1)S(1)}) custom-call(s32[2]{0:T(128)S(1)} %pad_add_fusion.refs_0_, s32[4]{0:T(128)S(1)} %and_select_fusion.refs_1_, s32[1]{0:T(128)} %bitcast.refs_2_, ...), custom_call_target="tpu_custom_call" | custom-call | flops 17716740096 | bytes 8388608 | tf_op jit(solution)/shard_map/pallas_call | solution.py:207
  46.2 3.0 %collective-permute-start.7 = (bf16[1,32,1152]{2,1,0:T(8,128)(2,1)S(1)}, bf16[1,32,1152]{2,1,0:T(8,128)(2,1)S(1)}, u32[]{:S(2)}, u32[]{:S(2)}) collective-permute-start(bf16[1,32,1152]{2,1,0:T(8,128)(2,1)S(1)} %get-tuple-element.57), channel_id=1, source_target_pairs={{0,2},{1,3},{2,0},{3,1},{4,6},{5,7},{6,4},{7,5},{8,10},{9,11},{10,... | collective-permute-start | bytes 221192 | tf_op jit(solution)/shard_map/ppermute | solution.py:40
  49.2 2.0 %collective-permute-start.11 = (bf16[1,32,1152]{2,1,0:T(8,128)(2,1)S(1)}, bf16[1,32,1152]{2,1,0:T(8,128)(2,1)S(1)}, u32[]{:S(2)}, u32[]{:S(2)}) collective-permute-start(bf16[1,32,1152]{2,1,0:T(8,128)(2,1)S(1)} %get-tuple-element.65), channel_id=1, source_target_pairs={{0,1},{1,2},{2,3},{3,0},{4,5},{5,6},{6,7},{7,4},{8,9},{9,10},{10,1... | collective-permute-start | bytes 221192 | tf_op jit(solution)/shard_map/ppermute | solution.py:40
  51.2 1.9 %collective-permute-done.7.refs_2_ = bf16[1,32,1152]{2,1,0:T(8,128)(2,1)S(1)} collective-permute-done((bf16[1,32,1152]{2,1,0:T(8,128)(2,1)S(1)}, bf16[1,32,1152]{2,1,0:T(8,128)(2,1)S(1)}, u32[]{:S(2)}, u32[]{:S(2)}) %collective-permute-start.7) | collective-permute-done | bytes 73760 | tf_op jit(solution)/shard_map/ppermute | solution.py:40
  53.1 0.8 collective-permute-done.10.refs_7_
  53.9 1.5 %collective-permute-done.11.refs_10_ = bf16[1,32,1152]{2,1,0:T(8,128)(2,1)S(1)} collective-permute-done((bf16[1,32,1152]{2,1,0:T(8,128)(2,1)S(1)}, bf16[1,32,1152]{2,1,0:T(8,128)(2,1)S(1)}, u32[]{:S(2)}, u32[]{:S(2)}) %collective-permute-start.11) | collective-permute-done | bytes 73760 | tf_op jit(solution)/shard_map/ppermute | solution.py:40
  55.4 4.1 %project.1 = (bf16[32,2048]{1,0:T(8,128)(2,1)S(1)}, bf16[32,2048]{1,0:T(8,128)(2,1)S(1)}, bf16[32,2048]{1,0:T(8,128)(2,1)S(1)}, bf16[32,2048]{1,0:T(8,128)(2,1)S(1)}) custom-call(bf16[1,32,1152]{2,1,0:T(8,128)(2,1)S(1)} %get-tuple-element.53.refs_0_, bf16[2,32,1152]{2,1,0:T(8,128)(2,1)S(1)} %collective-permute-done.5.refs_1_, ...), custom_call_target="tpu_custom_call" | custom-call | tf_op jit(solution)/shard_map/project/pallas_call | solution.py:287
  59.4 1.0 collective-permute-start.12
  60.4 0.8 collective-permute-start.13
  61.2 1.0 collective-permute-start.14
  62.3 3.4 %collective-permute-done.12.refs_1_ = bf16[32,2048]{1,0:T(8,128)(2,1)S(1)} collective-permute-done((bf16[32,2048]{1,0:T(8,128)(2,1)S(1)}, bf16[32,2048]{1,0:T(8,128)(2,1)S(1)}, u32[]{:S(2)}, u32[]{:S(2)}) %collective-permute-start.12) | collective-permute-done | bytes 131104 | tf_op jit(solution)/shard_map/ppermute | solution.py:40
  65.7 4.2 %collective-permute-done.13.refs_2_ = bf16[32,2048]{1,0:T(8,128)(2,1)S(1)} collective-permute-done((bf16[32,2048]{1,0:T(8,128)(2,1)S(1)}, bf16[32,2048]{1,0:T(8,128)(2,1)S(1)}, u32[]{:S(2)}, u32[]{:S(2)}) %collective-permute-start.13) | collective-permute-done | bytes 131104 | tf_op jit(solution)/shard_map/ppermute | solution.py:40
  69.9 0.2 normalize.1
  70.1 1.7 %collective-permute-start.21 = (bf16[32,2176]{1,0:T(8,128)(2,1)S(1)}, bf16[32,2176]{1,0:T(8,128)(2,1)S(1)}, u32[]{:S(2)}, u32[]{:S(2)}) collective-permute-start(bf16[32,2176]{1,0:T(8,128)(2,1)S(1)} %get-tuple-element.72.refs_3_), channel_id=1, source_target_pairs={{0,8},{4,12},{8,0},{12,4},{1,9},{5,13},{9,1},{13,5},{2,10},{6,14},... | collective-permute-start | bytes 417800 | tf_op jit(solution)/shard_map/ppermute | solution.py:44
  71.8 2.6 %collective-permute-start.17 = (bf16[32,2176]{1,0:T(8,128)(2,1)S(1)}, bf16[32,2176]{1,0:T(8,128)(2,1)S(1)}, u32[]{:S(2)}, u32[]{:S(2)}) collective-permute-start(bf16[32,2176]{1,0:T(8,128)(2,1)S(1)} %get-tuple-element.72.refs_3_), channel_id=1, source_target_pairs={{0,3},{1,0},{2,1},{3,2},{4,7},{5,4},{6,5},{7,6},{8,11},{9,8},{10,9... | collective-permute-start | bytes 417800 | tf_op jit(solution)/shard_map/ppermute | solution.py:40
  74.4 2.5 %collective-permute-start.15 = (bf16[32,2176]{1,0:T(8,128)(2,1)S(1)}, bf16[32,2176]{1,0:T(8,128)(2,1)S(1)}, u32[]{:S(2)}, u32[]{:S(2)}) collective-permute-start(bf16[32,2176]{1,0:T(8,128)(2,1)S(1)} %get-tuple-element.72.refs_3_), channel_id=1, source_target_pairs={{0,2},{1,3},{2,0},{3,1},{4,6},{5,7},{6,4},{7,5},{8,10},{9,11},{10,... | collective-permute-start | bytes 417800 | tf_op jit(solution)/shard_map/ppermute | solution.py:40
  76.9 1.5 %collective-permute-done.17.refs_2_ = bf16[32,2176]{1,0:T(8,128)(2,1)S(1)} collective-permute-done((bf16[32,2176]{1,0:T(8,128)(2,1)S(1)}, bf16[32,2176]{1,0:T(8,128)(2,1)S(1)}, u32[]{:S(2)}, u32[]{:S(2)}) %collective-permute-start.17) | collective-permute-done | bytes 139296 | tf_op jit(solution)/shard_map/ppermute | solution.py:40
  78.5 4.2 %collective-permute-done.16.refs_1_ = bf16[32,2176]{1,0:T(8,128)(2,1)S(1)} collective-permute-done((bf16[32,2176]{1,0:T(8,128)(2,1)S(1)}, bf16[32,2176]{1,0:T(8,128)(2,1)S(1)}, u32[]{:S(2)}, u32[]{:S(2)}) %collective-permute-start.16) | collective-permute-done | bytes 139296 | tf_op jit(solution)/shard_map/ppermute | solution.py:40
  82.8 0.6 collective-permute-start.19
  83.4 4.0 %collective-permute-done.15.refs_0_ = bf16[32,2176]{1,0:T(8,128)(2,1)S(1)} collective-permute-done((bf16[32,2176]{1,0:T(8,128)(2,1)S(1)}, bf16[32,2176]{1,0:T(8,128)(2,1)S(1)}, u32[]{:S(2)}, u32[]{:S(2)}) %collective-permute-start.15) | collective-permute-done | bytes 139296 | tf_op jit(solution)/shard_map/ppermute | solution.py:40
  87.5 0.5 collective-permute-start.22
  88.0 0.4 collective-permute-start.27
  88.5 4.2 %collective-permute-done.18.refs_4_ = bf16[32,2176]{1,0:T(8,128)(2,1)S(1)} collective-permute-done((bf16[32,2176]{1,0:T(8,128)(2,1)S(1)}, bf16[32,2176]{1,0:T(8,128)(2,1)S(1)}, u32[]{:S(2)}, u32[]{:S(2)}) %collective-permute-start.18) | collective-permute-done | bytes 139296 | tf_op jit(solution)/shard_map/ppermute | solution.py:44
  92.7 1.3 %collective-permute-done.26.refs_12_ = bf16[32,2176]{1,0:T(8,128)(2,1)S(1)} collective-permute-done((bf16[32,2176]{1,0:T(8,128)(2,1)S(1)}, bf16[32,2176]{1,0:T(8,128)(2,1)S(1)}, u32[]{:S(2)}, u32[]{:S(2)}) %collective-permute-start.26) | collective-permute-done | bytes 139296 | tf_op jit(solution)/shard_map/ppermute | solution.py:44
  94.0 7.8 %run_expert.1 = (f32[256,2048]{1,0:T(8,128)S(1)}, bf16[256,2048]{1,0:T(8,128)(2,1)S(1)}) custom-call(s32[1]{0:T(128)} %bitcast.11.expert_ref, bf16[32,2176]{1,0:T(8,128)(2,1)S(1)} %collective-permute-done.15.refs_0_, bf16[32,2176]{1,0:T(8,128)(2,1)S(1)} %collective-permute-done.16.refs_1_, bf16[32,2176]{1,0:T(8,128)(2,1)S(1)} %collective-permute-done.17.refs_2_, ...), custom_call_target="tpu_custom_call" | custom-call | tf_op jit(solution)/shard_map/run_expert/pallas_call | solution.py:372
  101.8 0.2 collective-permute-start.30
  102.0 2.5 %collective-permute-done.30 = bf16[256,2048]{1,0:T(8,128)(2,1)S(1)} collective-permute-done((bf16[256,2048]{1,0:T(8,128)(2,1)S(1)}, bf16[256,2048]{1,0:T(8,128)(2,1)S(1)}, u32[]{:S(2)}, u32[]{:S(2)}) %collective-permute-start.30) | collective-permute-done | bytes 1048608 | tf_op jit(solution)/shard_map/ppermute | solution.py:44
  104.5 0.4 fusion.7
  105.0 0.3 collective-permute-start.31
  105.4 1.7 %collective-permute-start.35 = (bf16[32,2048]{1,0:T(8,128)(2,1)S(1)}, bf16[32,2048]{1,0:T(8,128)(2,1)S(1)}, u32[]{:S(2)}, u32[]{:S(2)}) collective-permute-start(bf16[32,2048]{1,0:T(8,128)(2,1)S(1)} %get-tuple-element.82), channel_id=1, source_target_pairs={{0,8},{4,12},{8,0},{12,4},{1,9},{5,13},{9,1},{13,5},{2,10},{6,14},... | collective-permute-start | bytes 393224 | tf_op jit(solution)/shard_map/ppermute | solution.py:44
  107.1 0.3 collective-permute-start.33
  107.4 1.7 %collective-permute-start.37 = (bf16[32,2048]{1,0:T(8,128)(2,1)S(1)}, bf16[32,2048]{1,0:T(8,128)(2,1)S(1)}, u32[]{:S(2)}, u32[]{:S(2)}) collective-permute-start(bf16[32,2048]{1,0:T(8,128)(2,1)S(1)} %get-tuple-element.81), channel_id=1, source_target_pairs={{0,8},{4,12},{8,0},{12,4},{1,9},{5,13},{9,1},{13,5},{2,10},{6,14},... | collective-permute-start | bytes 393224 | tf_op jit(solution)/shard_map/ppermute | solution.py:44
  109.1 2.3 %collective-permute-done.31 = bf16[32,2048]{1,0:T(8,128)(2,1)S(1)} collective-permute-done((bf16[32,2048]{1,0:T(8,128)(2,1)S(1)}, bf16[32,2048]{1,0:T(8,128)(2,1)S(1)}, u32[]{:S(2)}, u32[]{:S(2)}) %collective-permute-start.31) | collective-permute-done | bytes 131104 | tf_op jit(solution)/shard_map/ppermute | solution.py:44
  111.4 2.8 %collective-permute-done.35 = bf16[32,2048]{1,0:T(8,128)(2,1)S(1)} collective-permute-done((bf16[32,2048]{1,0:T(8,128)(2,1)S(1)}, bf16[32,2048]{1,0:T(8,128)(2,1)S(1)}, u32[]{:S(2)}, u32[]{:S(2)}) %collective-permute-start.35) | collective-permute-done | bytes 131104 | tf_op jit(solution)/shard_map/ppermute | solution.py:44
  114.2 2.8 %collective-permute-done.33 = bf16[32,2048]{1,0:T(8,128)(2,1)S(1)} collective-permute-done((bf16[32,2048]{1,0:T(8,128)(2,1)S(1)}, bf16[32,2048]{1,0:T(8,128)(2,1)S(1)}, u32[]{:S(2)}, u32[]{:S(2)}) %collective-permute-start.33) | collective-permute-done | bytes 131104 | tf_op jit(solution)/shard_map/ppermute | solution.py:44
  117.2 2.8 %collective-permute-start.36 = (bf16[32,2048]{1,0:T(8,128)(2,1)S(1)}, bf16[32,2048]{1,0:T(8,128)(2,1)S(1)}, u32[]{:S(2)}, u32[]{:S(2)}) collective-permute-start(bf16[32,2048]{1,0:T(8,128)(2,1)S(1)} %get-tuple-element.78), channel_id=1, source_target_pairs={{0,1},{1,2},{2,3},{3,0},{4,5},{5,6},{6,7},{7,4},{8,9},{9,10},{10,1... | collective-permute-start | bytes 393224 | tf_op jit(solution)/shard_map/ppermute | solution.py:40
  120.0 1.1 collective-permute-start.34
  121.1 6.2 %collective-permute-done.32 = bf16[32,2048]{1,0:T(8,128)(2,1)S(1)} collective-permute-done((bf16[32,2048]{1,0:T(8,128)(2,1)S(1)}, bf16[32,2048]{1,0:T(8,128)(2,1)S(1)}, u32[]{:S(2)}, u32[]{:S(2)}) %collective-permute-start.32) | collective-permute-done | bytes 131104 | tf_op jit(solution)/shard_map/ppermute | solution.py:40
  127.3 1.3 %collective-permute-done.34 = bf16[32,2048]{1,0:T(8,128)(2,1)S(1)} collective-permute-done((bf16[32,2048]{1,0:T(8,128)(2,1)S(1)}, bf16[32,2048]{1,0:T(8,128)(2,1)S(1)}, u32[]{:S(2)}, u32[]{:S(2)}) %collective-permute-start.34) | collective-permute-done | bytes 131104 | tf_op jit(solution)/shard_map/ppermute | solution.py:40
  128.7 0.8 fusion.2
  (55 shorter events, 0.9 us)
Async XLA Ops:
  0.0 18.7 %collective-permute-start = (bf16[32,4096]{1,0:T(8,128)(2,1)}, bf16[32,4096]{1,0:T(8,128)(2,1)S(1)}, u32[]{:S(2)}, u32[]{:S(2)}) collective-permute-start(bf16[32,4096]{1,0:T(8,128)(2,1)} %refs_3_.1), channel_id=1, source_target_pairs={{0,1},{1,2},{2,3},{3,0},{4,5},{5,6},{6,7},{7,4},{8,9},{9,10},{10,1... | collective-permute-start | bytes 786440 | tf_op jit(solution)/shard_map/ppermute | solution.py:40
  3.0 15.6 %collective-permute-start.1 = (bf16[32,4096]{1,0:T(8,128)(2,1)}, bf16[32,4096]{1,0:T(8,128)(2,1)S(1)}, u32[]{:S(2)}, u32[]{:S(2)}) collective-permute-start(bf16[32,4096]{1,0:T(8,128)(2,1)} %refs_3_.1), channel_id=1, source_target_pairs={{0,3},{1,0},{2,1},{3,2},{4,7},{5,4},{6,5},{7,6},{8,11},{9,8},{10,9... | collective-permute-start | bytes 786440 | tf_op jit(solution)/shard_map/ppermute | solution.py:40
  5.8 12.9 %copy-start.4 = (bf16[32,4096]{1,0:T(8,128)(2,1)S(1)}, bf16[32,4096]{1,0:T(8,128)(2,1)}, u32[]{:S(2)}) copy-start(bf16[32,4096]{1,0:T(8,128)(2,1)} %refs_3_.1) | copy-start | bytes 786436
  14.7 18.8 %collective-permute-start.2 = (bf16[1,32,1152]{2,1,0:T(8,128)(2,1)S(1)}, bf16[1,32,1152]{2,1,0:T(8,128)(2,1)S(1)}, u32[]{:S(2)}, u32[]{:S(2)}) collective-permute-start(bf16[1,32,1152]{2,1,0:T(8,128)(2,1)S(1)} %get-tuple-element.50), channel_id=1, source_target_pairs={{0,1},{1,2},{2,3},{3,0},{4,5},{5,6},{6,7},{7,4},{8,9},{9,10},{10,1... | collective-permute-start | bytes 221192 | tf_op jit(solution)/shard_map/ppermute | solution.py:40
  14.7 18.8 %collective-permute-start.3 = (bf16[1,32,1152]{2,1,0:T(8,128)(2,1)S(1)}, bf16[1,32,1152]{2,1,0:T(8,128)(2,1)S(1)}, u32[]{:S(2)}, u32[]{:S(2)}) collective-permute-start(bf16[1,32,1152]{2,1,0:T(8,128)(2,1)S(1)} %get-tuple-element.51), channel_id=1, source_target_pairs={{0,2},{1,3},{2,0},{3,1},{4,6},{5,7},{6,4},{7,5},{8,10},{9,11},{10,... | collective-permute-start | bytes 221192 | tf_op jit(solution)/shard_map/ppermute | solution.py:40
  17.3 16.3 %collective-permute-start.4 = (bf16[1,32,1152]{2,1,0:T(8,128)(2,1)S(1)}, bf16[1,32,1152]{2,1,0:T(8,128)(2,1)S(1)}, u32[]{:S(2)}, u32[]{:S(2)}) collective-permute-start(bf16[1,32,1152]{2,1,0:T(8,128)(2,1)S(1)} %get-tuple-element.52), channel_id=1, source_target_pairs={{0,3},{1,0},{2,1},{3,2},{4,7},{5,4},{6,5},{7,6},{8,11},{9,8},{10,9... | collective-permute-start | bytes 221192 | tf_op jit(solution)/shard_map/ppermute | solution.py:40
  18.7 18.8 %collective-permute-start.6 = (bf16[32,4096]{1,0:T(8,128)(2,1)S(1)}, bf16[32,4096]{1,0:T(8,128)(2,1)S(1)}, u32[]{:S(2)}, u32[]{:S(2)}) collective-permute-start(bf16[32,4096]{1,0:T(8,128)(2,1)S(1)} %copy-done.4), channel_id=1, source_target_pairs={{0,2},{1,3},{2,0},{3,1},{4,6},{5,7},{6,4},{7,5},{8,10},{9,11},{10,... | collective-permute-start | bytes 786440 | tf_op jit(solution)/shard_map/ppermute | solution.py:40
  33.6 15.6 %collective-permute-start.5 = (bf16[2,32,1152]{2,1,0:T(8,128)(2,1)S(1)}, bf16[2,32,1152]{2,1,0:T(8,128)(2,1)S(1)}, u32[]{:S(2)}, u32[]{:S(2)}) collective-permute-start(bf16[2,32,1152]{2,1,0:T(8,128)(2,1)S(1)} %get-tuple-element.54), channel_id=1, source_target_pairs={{0,1},{1,2},{2,3},{3,0},{4,5},{5,6},{6,7},{7,4},{8,9},{9,10},{10,1... | collective-permute-start | bytes 442376 | tf_op jit(solution)/shard_map/ppermute | solution.py:40
  33.6 17.6 %collective-permute-start.8 = (bf16[2,32,1152]{2,1,0:T(8,128)(2,1)S(1)}, bf16[2,32,1152]{2,1,0:T(8,128)(2,1)S(1)}, u32[]{:S(2)}, u32[]{:S(2)}) collective-permute-start(bf16[2,32,1152]{2,1,0:T(8,128)(2,1)S(1)} %get-tuple-element.58), channel_id=1, source_target_pairs={{0,3},{1,0},{2,1},{3,2},{4,7},{5,4},{6,5},{7,6},{8,11},{9,8},{10,9... | collective-permute-start | bytes 442376 | tf_op jit(solution)/shard_map/ppermute | solution.py:40
  37.5 13.8 %collective-permute-start.9 = (bf16[2,32,1152]{2,1,0:T(8,128)(2,1)S(1)}, bf16[2,32,1152]{2,1,0:T(8,128)(2,1)S(1)}, u32[]{:S(2)}, u32[]{:S(2)}) collective-permute-start(bf16[2,32,1152]{2,1,0:T(8,128)(2,1)S(1)} %get-tuple-element.61), channel_id=1, source_target_pairs={{0,2},{1,3},{2,0},{3,1},{4,6},{5,7},{6,4},{7,5},{8,10},{9,11},{10,... | collective-permute-start | bytes 442376 | tf_op jit(solution)/shard_map/ppermute | solution.py:40
  46.2 6.9 %collective-permute-start.7 = (bf16[1,32,1152]{2,1,0:T(8,128)(2,1)S(1)}, bf16[1,32,1152]{2,1,0:T(8,128)(2,1)S(1)}, u32[]{:S(2)}, u32[]{:S(2)}) collective-permute-start(bf16[1,32,1152]{2,1,0:T(8,128)(2,1)S(1)} %get-tuple-element.57), channel_id=1, source_target_pairs={{0,2},{1,3},{2,0},{3,1},{4,6},{5,7},{6,4},{7,5},{8,10},{9,11},{10,... | collective-permute-start | bytes 221192 | tf_op jit(solution)/shard_map/ppermute | solution.py:40
  49.2 4.7 %collective-permute-start.10 = (bf16[1,32,1152]{2,1,0:T(8,128)(2,1)S(1)}, bf16[1,32,1152]{2,1,0:T(8,128)(2,1)S(1)}, u32[]{:S(2)}, u32[]{:S(2)}) collective-permute-start(bf16[1,32,1152]{2,1,0:T(8,128)(2,1)S(1)} %get-tuple-element.62), channel_id=1, source_target_pairs={{0,3},{1,0},{2,1},{3,2},{4,7},{5,4},{6,5},{7,6},{8,11},{9,8},{10,9... | collective-permute-start | bytes 221192 | tf_op jit(solution)/shard_map/ppermute | solution.py:40
  49.2 6.2 %collective-permute-start.11 = (bf16[1,32,1152]{2,1,0:T(8,128)(2,1)S(1)}, bf16[1,32,1152]{2,1,0:T(8,128)(2,1)S(1)}, u32[]{:S(2)}, u32[]{:S(2)}) collective-permute-start(bf16[1,32,1152]{2,1,0:T(8,128)(2,1)S(1)} %get-tuple-element.65), channel_id=1, source_target_pairs={{0,1},{1,2},{2,3},{3,0},{4,5},{5,6},{6,7},{7,4},{8,9},{9,10},{10,1... | collective-permute-start | bytes 221192 | tf_op jit(solution)/shard_map/ppermute | solution.py:40
  55.3 6.8 %copy-start.2 = (f32[32,8]{0,1:T(8,128)S(1)}, f32[32,8]{0,1:T(8,128)}, u32[]{:S(2)}) copy-start(f32[32,8]{0,1:T(8,128)} %param.25) | copy-start | bytes 3076
  55.4 6.8 %copy-start.3 = (s32[32,8]{0,1:T(8,128)S(1)}, s32[32,8]{0,1:T(8,128)}, u32[]{:S(2)}) copy-start(s32[32,8]{0,1:T(8,128)} %param.24) | copy-start | bytes 3076
  55.4 14.6 %copy-start = (bf16[32,2048]{1,0:T(8,128)(2,1)S(1)}, bf16[32,2048]{1,0:T(8,128)(2,1)}, u32[]{:S(2)}) copy-start(bf16[32,2048]{1,0:T(8,128)(2,1)} %residual_ref.1) | copy-start | bytes 393220
  55.4 14.6 %copy-start.1 = (f32[2048]{0:T(1024)S(1)}, f32[2048]{0:T(1024)}, u32[]{:S(2)}) copy-start(f32[2048]{0:T(1024)} %param.21) | copy-start | bytes 24580
  59.4 6.3 %collective-permute-start.12 = (bf16[32,2048]{1,0:T(8,128)(2,1)S(1)}, bf16[32,2048]{1,0:T(8,128)(2,1)S(1)}, u32[]{:S(2)}, u32[]{:S(2)}) collective-permute-start(bf16[32,2048]{1,0:T(8,128)(2,1)S(1)} %get-tuple-element.68), channel_id=1, source_target_pairs={{0,3},{1,0},{2,1},{3,2},{4,7},{5,4},{6,5},{7,6},{8,11},{9,8},{10,9... | collective-permute-start | bytes 393224 | tf_op jit(solution)/shard_map/ppermute | solution.py:40
  60.4 9.5 %collective-permute-start.13 = (bf16[32,2048]{1,0:T(8,128)(2,1)S(1)}, bf16[32,2048]{1,0:T(8,128)(2,1)S(1)}, u32[]{:S(2)}, u32[]{:S(2)}) collective-permute-start(bf16[32,2048]{1,0:T(8,128)(2,1)S(1)} %get-tuple-element.69), channel_id=1, source_target_pairs={{0,2},{1,3},{2,0},{3,1},{4,6},{5,7},{6,4},{7,5},{8,10},{9,11},{10,... | collective-permute-start | bytes 393224 | tf_op jit(solution)/shard_map/ppermute | solution.py:40
  61.2 8.8 %collective-permute-start.14 = (bf16[32,2048]{1,0:T(8,128)(2,1)S(1)}, bf16[32,2048]{1,0:T(8,128)(2,1)S(1)}, u32[]{:S(2)}, u32[]{:S(2)}) collective-permute-start(bf16[32,2048]{1,0:T(8,128)(2,1)S(1)} %get-tuple-element.70), channel_id=1, source_target_pairs={{0,1},{1,2},{2,3},{3,0},{4,5},{5,6},{6,7},{7,4},{8,9},{9,10},{10,1... | collective-permute-start | bytes 393224 | tf_op jit(solution)/shard_map/ppermute | solution.py:40
  70.1 6.8 %collective-permute-start.21 = (bf16[32,2176]{1,0:T(8,128)(2,1)S(1)}, bf16[32,2176]{1,0:T(8,128)(2,1)S(1)}, u32[]{:S(2)}, u32[]{:S(2)}) collective-permute-start(bf16[32,2176]{1,0:T(8,128)(2,1)S(1)} %get-tuple-element.72.refs_3_), channel_id=1, source_target_pairs={{0,8},{4,12},{8,0},{12,4},{1,9},{5,13},{9,1},{13,5},{2,10},{6,14},... | collective-permute-start | bytes 417800 | tf_op jit(solution)/shard_map/ppermute | solution.py:44
  71.8 6.7 %collective-permute-start.17 = (bf16[32,2176]{1,0:T(8,128)(2,1)S(1)}, bf16[32,2176]{1,0:T(8,128)(2,1)S(1)}, u32[]{:S(2)}, u32[]{:S(2)}) collective-permute-start(bf16[32,2176]{1,0:T(8,128)(2,1)S(1)} %get-tuple-element.72.refs_3_), channel_id=1, source_target_pairs={{0,3},{1,0},{2,1},{3,2},{4,7},{5,4},{6,5},{7,6},{8,11},{9,8},{10,9... | collective-permute-start | bytes 417800 | tf_op jit(solution)/shard_map/ppermute | solution.py:40
  74.4 4.1 %collective-permute-start.25 = (bf16[32,2176]{1,0:T(8,128)(2,1)S(1)}, bf16[32,2176]{1,0:T(8,128)(2,1)S(1)}, u32[]{:S(2)}, u32[]{:S(2)}) collective-permute-start(bf16[32,2176]{1,0:T(8,128)(2,1)S(1)} %get-tuple-element.72.refs_3_), channel_id=1, source_target_pairs={{0,4},{4,0},{8,12},{12,8},{1,5},{5,1},{9,13},{13,9},{2,6},{6,2},{1... | collective-permute-start | bytes 417800 | tf_op jit(solution)/shard_map/ppermute | solution.py:44
  74.4 8.4 %collective-permute-start.16 = (bf16[32,2176]{1,0:T(8,128)(2,1)S(1)}, bf16[32,2176]{1,0:T(8,128)(2,1)S(1)}, u32[]{:S(2)}, u32[]{:S(2)}) collective-permute-start(bf16[32,2176]{1,0:T(8,128)(2,1)S(1)} %get-tuple-element.72.refs_3_), channel_id=1, source_target_pairs={{0,1},{1,2},{2,3},{3,0},{4,5},{5,6},{6,7},{7,4},{8,9},{9,10},{10,1... | collective-permute-start | bytes 417800 | tf_op jit(solution)/shard_map/ppermute | solution.py:40
  74.4 13.0 %collective-permute-start.15 = (bf16[32,2176]{1,0:T(8,128)(2,1)S(1)}, bf16[32,2176]{1,0:T(8,128)(2,1)S(1)}, u32[]{:S(2)}, u32[]{:S(2)}) collective-permute-start(bf16[32,2176]{1,0:T(8,128)(2,1)S(1)} %get-tuple-element.72.refs_3_), channel_id=1, source_target_pairs={{0,2},{1,3},{2,0},{3,1},{4,6},{5,7},{6,4},{7,5},{8,10},{9,11},{10,... | collective-permute-start | bytes 417800 | tf_op jit(solution)/shard_map/ppermute | solution.py:40
  76.9 10.5 %collective-permute-start.29 = (bf16[32,2176]{1,0:T(8,128)(2,1)S(1)}, bf16[32,2176]{1,0:T(8,128)(2,1)S(1)}, u32[]{:S(2)}, u32[]{:S(2)}) collective-permute-start(bf16[32,2176]{1,0:T(8,128)(2,1)S(1)} %collective-permute-done.21.refs_7_), channel_id=1, source_target_pairs={{0,4},{4,0},{8,12},{12,8},{1,5},{5,1},{9,13},{13,9},{2,6},{6,2},{1... | collective-permute-start | bytes 417800 | tf_op jit(solution)/shard_map/ppermute | solution.py:44
  78.5 9.0 %collective-permute-start.24 = (bf16[32,2176]{1,0:T(8,128)(2,1)S(1)}, bf16[32,2176]{1,0:T(8,128)(2,1)S(1)}, u32[]{:S(2)}, u32[]{:S(2)}) collective-permute-start(bf16[32,2176]{1,0:T(8,128)(2,1)S(1)} %collective-permute-done.17.refs_2_), channel_id=1, source_target_pairs={{0,4},{4,0},{8,12},{12,8},{1,5},{5,1},{9,13},{13,9},{2,6},{6,2},{1... | collective-permute-start | bytes 417800 | tf_op jit(solution)/shard_map/ppermute | solution.py:44
  78.5 9.5 %collective-permute-start.20 = (bf16[32,2176]{1,0:T(8,128)(2,1)S(1)}, bf16[32,2176]{1,0:T(8,128)(2,1)S(1)}, u32[]{:S(2)}, u32[]{:S(2)}) collective-permute-start(bf16[32,2176]{1,0:T(8,128)(2,1)S(1)} %collective-permute-done.17.refs_2_), channel_id=1, source_target_pairs={{0,8},{4,12},{8,0},{12,4},{1,9},{5,13},{9,1},{13,5},{2,10},{6,14},... | collective-permute-start | bytes 417800 | tf_op jit(solution)/shard_map/ppermute | solution.py:44
  82.8 5.3 %collective-permute-start.19 = (bf16[32,2176]{1,0:T(8,128)(2,1)S(1)}, bf16[32,2176]{1,0:T(8,128)(2,1)S(1)}, u32[]{:S(2)}, u32[]{:S(2)}) collective-permute-start(bf16[32,2176]{1,0:T(8,128)(2,1)S(1)} %collective-permute-done.16.refs_1_), channel_id=1, source_target_pairs={{0,8},{4,12},{8,0},{12,4},{1,9},{5,13},{9,1},{13,5},{2,10},{6,14},... | collective-permute-start | bytes 417800 | tf_op jit(solution)/shard_map/ppermute | solution.py:44
  87.3 5.3 %collective-permute-start.18 = (bf16[32,2176]{1,0:T(8,128)(2,1)S(1)}, bf16[32,2176]{1,0:T(8,128)(2,1)S(1)}, u32[]{:S(2)}, u32[]{:S(2)}) collective-permute-start(bf16[32,2176]{1,0:T(8,128)(2,1)S(1)} %collective-permute-done.15.refs_0_), channel_id=1, source_target_pairs={{0,8},{4,12},{8,0},{12,4},{1,9},{5,13},{9,1},{13,5},{2,10},{6,14},... | collective-permute-start | bytes 417800 | tf_op jit(solution)/shard_map/ppermute | solution.py:44
  87.5 5.2 %collective-permute-start.23 = (bf16[32,2176]{1,0:T(8,128)(2,1)S(1)}, bf16[32,2176]{1,0:T(8,128)(2,1)S(1)}, u32[]{:S(2)}, u32[]{:S(2)}) collective-permute-start(bf16[32,2176]{1,0:T(8,128)(2,1)S(1)} %collective-permute-done.16.refs_1_), channel_id=1, source_target_pairs={{0,4},{4,0},{8,12},{12,8},{1,5},{5,1},{9,13},{13,9},{2,6},{6,2},{1... | collective-permute-start | bytes 417800 | tf_op jit(solution)/shard_map/ppermute | solution.py:44
  87.5 5.2 %collective-permute-start.22 = (bf16[32,2176]{1,0:T(8,128)(2,1)S(1)}, bf16[32,2176]{1,0:T(8,128)(2,1)S(1)}, u32[]{:S(2)}, u32[]{:S(2)}) collective-permute-start(bf16[32,2176]{1,0:T(8,128)(2,1)S(1)} %collective-permute-done.15.refs_0_), channel_id=1, source_target_pairs={{0,4},{4,0},{8,12},{12,8},{1,5},{5,1},{9,13},{13,9},{2,6},{6,2},{1... | collective-permute-start | bytes 417800 | tf_op jit(solution)/shard_map/ppermute | solution.py:44
  88.0 4.7 %collective-permute-start.28 = (bf16[32,2176]{1,0:T(8,128)(2,1)S(1)}, bf16[32,2176]{1,0:T(8,128)(2,1)S(1)}, u32[]{:S(2)}, u32[]{:S(2)}) collective-permute-start(bf16[32,2176]{1,0:T(8,128)(2,1)S(1)} %collective-permute-done.20.refs_6_), channel_id=1, source_target_pairs={{0,4},{4,0},{8,12},{12,8},{1,5},{5,1},{9,13},{13,9},{2,6},{6,2},{1... | collective-permute-start | bytes 417800 | tf_op jit(solution)/shard_map/ppermute | solution.py:44
  88.0 4.6 %collective-permute-start.27 = (bf16[32,2176]{1,0:T(8,128)(2,1)S(1)}, bf16[32,2176]{1,0:T(8,128)(2,1)S(1)}, u32[]{:S(2)}, u32[]{:S(2)}) collective-permute-start(bf16[32,2176]{1,0:T(8,128)(2,1)S(1)} %collective-permute-done.19.refs_5_), channel_id=1, source_target_pairs={{0,4},{4,0},{8,12},{12,8},{1,5},{5,1},{9,13},{13,9},{2,6},{6,2},{1... | collective-permute-start | bytes 417800 | tf_op jit(solution)/shard_map/ppermute | solution.py:44
  92.7 1.4 %collective-permute-start.26 = (bf16[32,2176]{1,0:T(8,128)(2,1)S(1)}, bf16[32,2176]{1,0:T(8,128)(2,1)S(1)}, u32[]{:S(2)}, u32[]{:S(2)}) collective-permute-start(bf16[32,2176]{1,0:T(8,128)(2,1)S(1)} %collective-permute-done.18.refs_4_), channel_id=1, source_target_pairs={{0,4},{4,0},{8,12},{12,8},{1,5},{5,1},{9,13},{13,9},{2,6},{6,2},{1... | collective-permute-start | bytes 417800 | tf_op jit(solution)/shard_map/ppermute | solution.py:44
  101.8 2.7 %collective-permute-start.30 = (bf16[256,2048]{1,0:T(8,128)(2,1)S(1)}, bf16[256,2048]{1,0:T(8,128)(2,1)S(1)}, u32[]{:S(2)}, u32[]{:S(2)}) collective-permute-start(bf16[256,2048]{1,0:T(8,128)(2,1)S(1)} %get-tuple-element.74), channel_id=1, source_target_pairs={{0,4},{4,0},{8,12},{12,8},{1,5},{5,1},{9,13},{13,9},{2,6},{6,2},{1... | collective-permute-start | bytes 3145736 | tf_op jit(solution)/shard_map/ppermute | solution.py:44
  105.0 6.4 %collective-permute-start.31 = (bf16[32,2048]{1,0:T(8,128)(2,1)S(1)}, bf16[32,2048]{1,0:T(8,128)(2,1)S(1)}, u32[]{:S(2)}, u32[]{:S(2)}) collective-permute-start(bf16[32,2048]{1,0:T(8,128)(2,1)S(1)} %get-tuple-element.80), channel_id=1, source_target_pairs={{0,8},{4,12},{8,0},{12,4},{1,9},{5,13},{9,1},{13,5},{2,10},{6,14},... | collective-permute-start | bytes 393224 | tf_op jit(solution)/shard_map/ppermute | solution.py:44
  105.4 8.9 %collective-permute-start.35 = (bf16[32,2048]{1,0:T(8,128)(2,1)S(1)}, bf16[32,2048]{1,0:T(8,128)(2,1)S(1)}, u32[]{:S(2)}, u32[]{:S(2)}) collective-permute-start(bf16[32,2048]{1,0:T(8,128)(2,1)S(1)} %get-tuple-element.82), channel_id=1, source_target_pairs={{0,8},{4,12},{8,0},{12,4},{1,9},{5,13},{9,1},{13,5},{2,10},{6,14},... | collective-permute-start | bytes 393224 | tf_op jit(solution)/shard_map/ppermute | solution.py:44
  107.1 9.9 %collective-permute-start.33 = (bf16[32,2048]{1,0:T(8,128)(2,1)S(1)}, bf16[32,2048]{1,0:T(8,128)(2,1)S(1)}, u32[]{:S(2)}, u32[]{:S(2)}) collective-permute-start(bf16[32,2048]{1,0:T(8,128)(2,1)S(1)} %get-tuple-element.83), channel_id=1, source_target_pairs={{0,8},{4,12},{8,0},{12,4},{1,9},{5,13},{9,1},{13,5},{2,10},{6,14},... | collective-permute-start | bytes 393224 | tf_op jit(solution)/shard_map/ppermute | solution.py:44
  107.4 13.7 %collective-permute-start.37 = (bf16[32,2048]{1,0:T(8,128)(2,1)S(1)}, bf16[32,2048]{1,0:T(8,128)(2,1)S(1)}, u32[]{:S(2)}, u32[]{:S(2)}) collective-permute-start(bf16[32,2048]{1,0:T(8,128)(2,1)S(1)} %get-tuple-element.81), channel_id=1, source_target_pairs={{0,8},{4,12},{8,0},{12,4},{1,9},{5,13},{9,1},{13,5},{2,10},{6,14},... | collective-permute-start | bytes 393224 | tf_op jit(solution)/shard_map/ppermute | solution.py:44
  117.1 10.2 %collective-permute-start.32 = (bf16[32,2048]{1,0:T(8,128)(2,1)S(1)}, bf16[32,2048]{1,0:T(8,128)(2,1)S(1)}, u32[]{:S(2)}, u32[]{:S(2)}) collective-permute-start(bf16[32,2048]{1,0:T(8,128)(2,1)S(1)} %get-tuple-element.77), channel_id=1, source_target_pairs={{0,2},{1,3},{2,0},{3,1},{4,6},{5,7},{6,4},{7,5},{8,10},{9,11},{10,... | collective-permute-start | bytes 393224 | tf_op jit(solution)/shard_map/ppermute | solution.py:40
  117.2 10.1 %collective-permute-start.36 = (bf16[32,2048]{1,0:T(8,128)(2,1)S(1)}, bf16[32,2048]{1,0:T(8,128)(2,1)S(1)}, u32[]{:S(2)}, u32[]{:S(2)}) collective-permute-start(bf16[32,2048]{1,0:T(8,128)(2,1)S(1)} %get-tuple-element.78), channel_id=1, source_target_pairs={{0,1},{1,2},{2,3},{3,0},{4,5},{5,6},{6,7},{7,4},{8,9},{9,10},{10,1... | collective-permute-start | bytes 393224 | tf_op jit(solution)/shard_map/ppermute | solution.py:40
  120.0 8.6 %collective-permute-start.34 = (bf16[32,2048]{1,0:T(8,128)(2,1)S(1)}, bf16[32,2048]{1,0:T(8,128)(2,1)S(1)}, u32[]{:S(2)}, u32[]{:S(2)}) collective-permute-start(bf16[32,2048]{1,0:T(8,128)(2,1)S(1)} %get-tuple-element.79), channel_id=1, source_target_pairs={{0,3},{1,0},{2,1},{3,2},{4,7},{5,4},{6,5},{7,6},{8,11},{9,8},{10,9... | collective-permute-start | bytes 393224 | tf_op jit(solution)/shard_map/ppermute | solution.py:40
